TPU v7x, 32 devices: a whole 2x2x4 slice. The times are simulated.
32 devices in a mesh: face: 8 (over z, x), band: 4 (over y, core).
Axes of the slice: x: 2, y: 2, z: 4, core: 2. Of those that a mesh axis runs over, the one named last changes fastest.
Arguments:
- node_latents: bfloat16 [8192, 512], P(('face', 'band')), may hold values from -6 to 6
- coarse_latents: bfloat16 [1024, 512], replicated, may hold values from -6 to 6
- edge_latents: bfloat16 [32768, 512], P(('face', 'band')), may hold values from -6 to 6
- up_latents: bfloat16 [8192, 512], P(('face', 'band')), may hold values from -6 to 6
- edge_weight_in: bfloat16 [1536, 512], replicated, may hold values from -0.15625 to 0.15625
- edge_weight_out: bfloat16 [512, 512], replicated, may hold values from -0.25 to 0.25
- edge_gain: float32 [512], replicated, may hold values from 0.5 to 1.5
- node_weight_in: bfloat16 [1024, 512], replicated, may hold values from -0.1875 to 0.1875
- node_weight_out: bfloat16 [512, 512], replicated, may hold values from -0.25 to 0.25
- node_gain: float32 [512], replicated, may hold values from 0.5 to 1.5
- nodes_cotangent: bfloat16 [8192, 512], P(('face', 'band')), may hold values from -6 to 6
- coarse_cotangent: bfloat16 [1024, 512], replicated, may hold values from -6 to 6
- edges_cotangent: bfloat16 [32768, 512], P(('face', 'band')), may hold values from -6 to 6
- ups_cotangent: bfloat16 [8192, 512], P(('face', 'band')), may hold values from -6 to 6
- send_rows: int32 [32, 32, 4], P(('face', 'band')), may hold values from 0 to 255, as said below
- edge_sender: int32 [32768], P(('face', 'band')), may hold values from 0 to 1407, as said below
- edge_receiver: int32 [32768], P(('face', 'band')), may hold values from 0 to 255
- up_sender: int32 [8192], P(('face', 'band')), may hold values from 0 to 255
- up_receiver: int32 [8192], P(('face', 'band')), may hold values from 0 to 1023
Outputs:
- grad_nodes: float32 [8192, 512], P(('face', 'band'))
- grad_coarse: float32 [1024, 512], replicated
- grad_edges: float32 [32768, 512], P(('face', 'band'))
- grad_ups: float32 [8192, 512], P(('face', 'band'))
- grad_edge_in: float32 [1536, 512], replicated
- grad_edge_out: float32 [512, 512], replicated
- grad_edge_gain: float32 [512], replicated
- grad_node_in: float32 [1024, 512], replicated
- grad_node_out: float32 [512, 512], replicated
- grad_node_gain: float32 [512], replicated
Inputs may be any that keep to these rules, and one draw needn't show every extreme that they name: `send_rows`: entry [s, p, k] is a row of device s's nodes sent to device p in slot k. Each pair uses its first few slots, at most 4; every device fills all 4 slots to at least one device, and in every draw some device receives 4 rows from every device. Unused slots hold 0 and no edge reads them. `edge_sender`: an edge of device p reads row t of p's sender table: its own node t below 256; slot k of the rows that device s sends to p for t = 256 + s * 4 + k, always a used slot; coarse node t - 384 from 384 on.
All inputs are finite; a program needn't handle non-finite values.
Results may differ from a plain program's by a relative error of at most 0.0068.
Values may be sent and summed in bfloat16 or wider, within the bound.
No kernel may reach another device: no remote copies, remote signals or barrier semaphores. Data moves between devices by JAX's collectives and lax.ppermute only.
A program may use at most 192 MiB of HBM per device.

v0:
```python
import math

import jax
import jax.numpy as jnp
from jax import lax
from jax.experimental import pallas as pl
from jax.experimental.pallas import tpu as pltpu
from jax.sharding import Mesh, PartitionSpec as P

EPSILON = 1e-05
BF = jnp.bfloat16
F32 = jnp.float32
TAIL = 16
EVERYONE = ("z", "x", "y", "core")
VMEM_LIMIT = 56 * 1024 * 1024


def dot(a, b):
    return lax.dot_general(a, b, (((1,), (0,)), ((), ())), preferred_element_type=F32)


def dot_lt(a, b):
    return lax.dot_general(a, b, (((0,), (0,)), ((), ())), preferred_element_type=F32)


def dot_rt(a, b):
    return lax.dot_general(a, b, (((1,), (1,)), ((), ())), preferred_element_type=F32)


def onehot_t(index_row, rows, offset=0):
    ids = lax.broadcasted_iota(jnp.int32, (rows, index_row.shape[1]), 0) + offset
    return jnp.where(ids == index_row, 1.0, 0.0).astype(BF)


def hidden_of(pre):
    return (pre * jax.nn.sigmoid(pre)).astype(BF)


def normalise(projected):
    center = projected - jnp.mean(projected, axis=1, keepdims=True)
    inv_std = lax.rsqrt(jnp.mean(center * center, axis=1, keepdims=True) + EPSILON)
    return center * inv_std, inv_std


def grad_to_pre(pre, normed, inv_std, cot, gain, w2):
    gain_part = jnp.sum(cot * normed, axis=0, keepdims=True)
    scaled = cot * gain
    d_proj = (
        inv_std
        * (
            scaled
            - jnp.mean(scaled, axis=1, keepdims=True)
            - normed * jnp.mean(scaled * normed, axis=1, keepdims=True)
        )
    ).astype(BF)
    d_hidden = dot_rt(d_proj, w2)
    logistic = jax.nn.sigmoid(pre)
    d_pre = (d_hidden * logistic * (1.0 + pre * (1.0 - logistic))).astype(BF)
    return gain_part, d_proj, d_pre


def gather_f32(onehot, table):
    high = table.astype(BF)
    low = (table - high.astype(F32)).astype(BF)
    return dot_lt(onehot, high) + dot_lt(onehot, low)


def split_rows(ref, bit, keep_ref, send_ref):
    half = keep_ref.shape[0]
    keep_ref[...] = ref[pl.ds(pl.multiple_of(bit * half, 16), half), :].astype(BF)
    send_ref[...] = ref[pl.ds(pl.multiple_of((1 - bit) * half, 16), half), :].astype(BF)


def fold_split_kernel(bit, keep, recv, keep_ref, send_ref):
    half = keep_ref.shape[0]
    for side, out_ref in ((bit[0], keep_ref), (1 - bit[0], send_ref)):
        rows = pl.ds(pl.multiple_of(side * half, 16), half)
        out_ref[...] = (keep[rows, :].astype(F32) + recv[rows, :].astype(F32)).astype(BF)


def fold_pair_kernel(keep, recv, out_ref):
    count, rows, _ = out_ref.shape
    rows -= TAIL
    tail = (keep[count * rows :].astype(F32) + recv[count * rows :].astype(F32)).astype(BF)
    for k in range(count):
        piece = slice(k * rows, (k + 1) * rows)
        out_ref[k, 0:rows] = (keep[piece].astype(F32) + recv[piece].astype(F32)).astype(BF)
        out_ref[k, rows:] = tail


def fold_group_kernel(got, out_ref):
    group = got.shape[0]
    count, rows, _ = out_ref.shape
    rows -= TAIL

    def total(at, size):
        piece = slice(at, at + size)
        acc = got[0, piece].astype(F32)
        for k in range(1, group):
            acc += got[k, piece].astype(F32)
        return acc.astype(BF)

    tail = total(count * rows, TAIL)
    for k in range(count):
        out_ref[k, 0:rows] = total(k * rows, rows)
        out_ref[k, rows:] = tail


def up_forward_kernel(
    us, ur, core, up, node, coarse, w1, w2, gain, p_ref, xs_ref, xr_ref, keep_ref, send_ref, part
):
    lat = up.shape[1]
    xs = dot_lt(onehot_t(us[...], node.shape[0]), node[...]).astype(BF)
    hot_r = onehot_t(ur[...], coarse.shape[0])
    xr = dot_lt(hot_r, coarse[...]).astype(BF)
    pre = dot(up[...], w1[0:lat]) + dot(xs, w1[lat : 2 * lat]) + dot(xr, w1[2 * lat :])
    normed, _ = normalise(dot(hidden_of(pre), w2[...]))
    new = (up[...].astype(F32) + normed * gain[...]).astype(BF)
    p_ref[...] = pre
    xs_ref[...] = xs
    xr_ref[...] = xr
    part[...] = dot(hot_r, new)
    split_rows(part, core[0], keep_ref, send_ref)


def edge_forward_kernel(
    es, er, edge, node, halo, coarse, w1, w2, gain, p_ref, xs_ref, total_ref, acc
):
    step = pl.program_id(0)
    lat = edge.shape[1]
    n = node.shape[0]
    imports = halo.shape[0]

    @pl.when(step == 0)
    def _():
        acc[...] = jnp.zeros_like(acc)

    sender = es[...]
    xs = (
        dot_lt(onehot_t(sender, n), node[...])
        + dot_lt(onehot_t(sender, imports, n), halo[...])
        + dot_lt(onehot_t(sender, coarse.shape[0], n + imports), coarse[...])
    ).astype(BF)
    hot_r = onehot_t(er[...], n)
    xr = dot_lt(hot_r, node[...]).astype(BF)
    pre = dot(edge[...], w1[0:lat]) + dot(xs, w1[lat : 2 * lat]) + dot(xr, w1[2 * lat :])
    normed, _ = normalise(dot(hidden_of(pre), w2[...]))
    new = (edge[...].astype(F32) + normed * gain[...]).astype(BF)
    p_ref[...] = pre
    xs_ref[...] = xs
    acc[...] += dot(hot_r, new)

    @pl.when(step == pl.num_programs(0) - 1)
    def _():
        total_ref[...] = acc[...].astype(BF)


def node_kernel(
    node, total_in, nw1, nw2, ngain, ncot, fg_ref, gn_ref, ngw1_ref, ngw2_ref, ngg_ref
):
    lat = node.shape[1]
    total = total_in[...]
    node_pre = dot(node[...], nw1[0:lat]) + dot(total, nw1[lat:])
    hidden = hidden_of(node_pre)
    node_normed, inv_std = normalise(dot(hidden, nw2[...]))
    cot = ncot[...].astype(F32)
    gain_part, d_proj, d_pre = grad_to_pre(
        node_pre, node_normed, inv_std, cot, ngain[...], nw2[...]
    )
    ngg_ref[...] = gain_part
    ngw2_ref[...] = dot_lt(hidden, d_proj).astype(BF)
    ngw1_ref[0:lat] = dot_lt(node[...], d_pre).astype(BF)
    ngw1_ref[lat:] = dot_lt(total, d_pre).astype(BF)
    gn_ref[...] = cot + dot_rt(d_pre, nw1[0:lat])
    fg_ref[...] = dot_rt(d_pre, nw1[lat:])


def edge_cotangent_kernel(
    er, edge, pre_ref, ecot, fg, w1, w2, gain, ge_ref, dp_ref, gw2_out, gg_ref, gw2
):
    step = pl.program_id(0)
    lat = edge.shape[1]

    @pl.when(step == 0)
    def _():
        gw2[...] = jnp.zeros_like(gw2)
        gg_ref[...] = jnp.zeros_like(gg_ref)

    cot = ecot[...].astype(F32) + gather_f32(onehot_t(er[...], fg.shape[0]), fg[...])
    pre = pre_ref[...]
    hidden = hidden_of(pre)
    normed, inv_std = normalise(dot(hidden, w2[...]))
    gain_part, d_proj, d_pre = grad_to_pre(pre, normed, inv_std, cot, gain[...], w2[...])
    gg_ref[...] += gain_part
    gw2[...] += dot_lt(hidden, d_proj)
    ge_ref[...] = cot + dot_rt(d_pre, w1[0:lat])
    dp_ref[...] = d_pre

    @pl.when(step == pl.num_programs(0) - 1)
    def _():
        gw2_out[...] = gw2[...].astype(BF)


def edge_product_kernel(
    es, er, edge, xs, dp, node, w1, gw1_out, np_ref, ret_ref, cp_ref, sum_s, sum_r, gw1
):
    step = pl.program_id(0)
    lat = edge.shape[1]
    n = node.shape[0]
    imports = ret_ref.shape[0]

    @pl.when(step == 0)
    def _():
        sum_s[...] = jnp.zeros_like(sum_s)
        sum_r[...] = jnp.zeros_like(sum_r)
        gw1[...] = jnp.zeros_like(gw1)

    d_pre = dp[...]
    gw1[0:lat] += dot_lt(edge[...], d_pre)
    gw1[lat:] += dot_lt(xs[...], d_pre)
    sum_r[...] += dot(onehot_t(er[...], n), d_pre)
    sum_s[...] += dot(onehot_t(es[...], sum_s.shape[0]), d_pre)

    @pl.when(step == pl.num_programs(0) - 1)
    def _():
        w_s = w1[lat : 2 * lat]
        recv = sum_r[...].astype(BF)
        gw1_out[0 : 2 * lat] = gw1[...].astype(BF)
        gw1_out[2 * lat :] = dot_lt(node[...], recv).astype(BF)
        np_ref[...] = dot_rt(sum_s[0:n].astype(BF), w_s) + dot_rt(recv, w1[2 * lat :])
        ret_ref[...] = dot_rt(sum_s[n : n + imports].astype(BF), w_s).astype(BF)
        cp_ref[...] = dot_rt(sum_s[n + imports :].astype(BF), w_s).astype(BF)


def coarse_kernel(
    core, rows, total_in, ccot, nw1, nw2, ngain, ngw1, ngw2, ngg,
    cg_ref, after_ref, keep_ref, send_ref, gg_ref, pay,
):
    lat = rows.shape[1]
    used = ngw1.shape[0] + ngw2.shape[0]
    total = total_in[...].astype(BF)
    pre = dot(rows[...], nw1[0:lat]) + dot(total, nw1[lat:])
    hidden = hidden_of(pre)
    normed, inv_std = normalise(dot(hidden, nw2[...]))
    cot = ccot[...].astype(F32)
    gain_part, d_proj, d_pre = grad_to_pre(pre, normed, inv_std, cot, ngain[...], nw2[...])
    cg_ref[...] = dot_rt(d_pre, nw1[lat:]).astype(BF)
    after_ref[...] = cot + dot_rt(d_pre, nw1[0:lat])
    pay[0:lat] = ngw1[0:lat].astype(F32) + dot_lt(rows[...], d_pre)
    pay[lat : 2 * lat] = ngw1[lat:].astype(F32) + dot_lt(total, d_pre)
    pay[2 * lat : used] = ngw2[...].astype(F32) + dot_lt(hidden, d_proj)
    if used < pay.shape[0]:
        pay[used:] = jnp.zeros((pay.shape[0] - used, lat), F32)
    split_rows(pay, core[0], keep_ref, send_ref)
    gg_ref[...] = ngg[...] + gain_part


def up_backward_kernel(
    us, ur, place, up, xs, xr, pre_ref, ucot, cg_own, cg_other, w1, w2, gain, gw1, gw2, gg, ngg,
    cp, after, gu_ref, np_ref, keep_ref, send_ref, csum, pay,
):
    lat = up.shape[1]
    half = cg_own.shape[0]
    coarse = csum.shape[0]
    core = place[1]
    hot_r = onehot_t(ur[...], coarse)
    turned = ur[...] - core * half
    turned = jnp.where(turned < 0, turned + coarse, turned)
    cot = (
        ucot[...].astype(F32)
        + dot_lt(onehot_t(turned, half), cg_own[...])
        + dot_lt(onehot_t(turned, half, half), cg_other[...])
    )
    pre = pre_ref[...]
    hidden = hidden_of(pre)
    normed, inv_std = normalise(dot(hidden, w2[...]))
    gain_part, d_proj, d_pre = grad_to_pre(pre, normed, inv_std, cot, gain[...], w2[...])
    gu_ref[...] = cot + dot_rt(d_pre, w1[0:lat])
    send = dot(onehot_t(us[...], np_ref.shape[0]), d_pre).astype(BF)
    np_ref[...] = dot_rt(send, w1[lat : 2 * lat])
    csum[...] = cp[...].astype(F32) + dot_rt(dot(hot_r, d_pre).astype(BF), w1[2 * lat :])
    count = after.shape[0]
    mine = pl.ds(pl.multiple_of(place[0] * count, 8), count)
    csum[mine, :] = csum[mine, :] + after[...]
    pay[0:coarse] = csum[...].astype(BF)
    start = coarse
    for x in (up, xs, xr):
        piece = slice(start - coarse, start - coarse + lat)
        pay[start : start + lat] = (gw1[piece].astype(F32) + dot_lt(x[...], d_pre)).astype(BF)
        start += lat
    end = start + gw2.shape[0]
    pay[start:end] = (gw2[...].astype(F32) + dot_lt(hidden, d_proj)).astype(BF)
    if end < pay.shape[0]:
        pay[end:] = jnp.zeros((pay.shape[0] - end, lat), BF)
    rows = pay.shape[0] // 2
    split_rows(pay, core, keep_ref.at[0:rows], send_ref.at[0:rows])
    ids = lax.broadcasted_iota(jnp.int32, (TAIL, lat), 0)
    edge_row = jnp.broadcast_to(gg[...] + gain_part, (TAIL, lat))
    node_row = jnp.broadcast_to(ngg[...], (TAIL, lat))
    tail = jnp.where(ids == 0, edge_row, jnp.where(ids == 1, node_row, 0.0)).astype(BF)
    keep_ref[rows:] = tail
    send_ref[rows:] = tail


def params(*semantics):
    return pltpu.CompilerParams(
        dimension_semantics=semantics or None, vmem_limit_bytes=VMEM_LIMIT
    )


def cost(micros):
    return pl.CostEstimate(
        flops=int(micros * 1.1e9), transcendentals=0, bytes_accessed=int(micros * 3.0e6)
    )


def shape(rows, cols, dtype):
    return jax.ShapeDtypeStruct((rows, cols), dtype)


def whole(arr):
    return pl.BlockSpec(arr.shape, lambda i: (0,) * len(arr.shape))


def swap(x, axes, count):
    if count == 1:
        return x
    return lax.all_to_all(x, axes, 0, 0, tiled=True)


GROUPS = ("core", ("x", "y"), "z")


def owner_index():
    index = jnp.int32(0)
    for axes in GROUPS:
        index = index * lax.axis_size(axes) + lax.axis_index(axes)
    return index


def exchange(x, mask):
    devices = lax.axis_size(EVERYONE)
    if devices == 1:
        return x
    return lax.ppermute(x, EVERYONE, [(i, i ^ mask) for i in range(devices)])


def sum_group(got, count):
    return jnp.sum(got.reshape(count, -1, got.shape[1]).astype(F32), axis=0)


def copies(x, count):
    return jnp.broadcast_to(x[None], (count,) + x.shape).reshape(-1, x.shape[1])


def reduce_rows(keep, send):
    x = keep.astype(F32) + exchange(send, 1).astype(F32)
    for axes in GROUPS[1:]:
        count = lax.axis_size(axes)
        x = sum_group(swap(x.astype(BF), axes, count), count)
    return x


def gather_halves(x):
    for axes in reversed(GROUPS[1:]):
        count = lax.axis_size(axes)
        x = swap(copies(x, count), axes, count)
    return x, exchange(x, 1)


def reduce_with_tail(keep, send, wait_for):
    cols = keep.shape[1]
    rows = keep.shape[0] - TAIL
    got = exchange(send, 1)
    got, wait_for = lax.optimization_barrier((got, wait_for))
    x = (keep, got)
    for axes, kernel in zip(GROUPS[1:], (fold_pair_kernel, fold_group_kernel)):
        count = lax.axis_size(axes)
        part = rows // count
        x = pl.pallas_call(
            kernel,
            out_shape=jax.ShapeDtypeStruct((count, part + TAIL, cols), BF),
            compiler_params=params(),
            cost_estimate=cost(3.0),
        )(*x)
        x = (swap(x.reshape(-1, cols), axes, count).reshape(x.shape),)
        rows = part
    x = jnp.sum(x[0].astype(F32), axis=0)
    return x[:rows].astype(BF), x[rows:], wait_for


def bit_masks(devices):
    slow = devices // lax.axis_size("z")
    order = [m for m in (1 << b for b in range(1, devices.bit_length())) if m < devices]
    return [m for m in order if m >= slow] + [m for m in order if m < slow]


def halving_sum(keep, send):
    devices = lax.axis_size(EVERYONE)
    masks = [1] + bit_masks(devices)
    place = lax.axis_index(EVERYONE)
    for mask, after in zip(masks, masks[1:]):
        rows, cols = keep.shape
        bit = ((place & after) > 0).astype(jnp.int32).reshape(1)
        got = exchange(send, mask)
        keep, send = pl.pallas_call(
            fold_split_kernel,
            in_specs=[pl.BlockSpec(memory_space=pltpu.SMEM)]
            + [pl.BlockSpec(memory_space=pltpu.VMEM)] * 2,
            out_shape=(shape(rows // 2, cols, BF),) * 2,
            compiler_params=params(),
            cost_estimate=cost(1.0),
            name="fold_split",
        )(bit, keep, got)
    got = exchange(send, masks[-1])
    x = (keep.astype(F32) + got.astype(F32)).astype(BF)
    for mask in reversed(masks):
        other = exchange(x, mask)
        x = jnp.where(
            (place & mask) > 0, jnp.concatenate([other, x], 0), jnp.concatenate([x, other], 0)
        )
    return x


def padded_rows(rows, devices):
    return -(-rows // (16 * devices)) * 16 * devices


def per_device(
    node, coarse, edge, up, w1, w2, gain, nw1, nw2, ngain, ncot, ccot, ecot, ucot,
    send_rows, edge_sender, edge_receiver, up_sender, up_receiver,
):
    n, lat = node.shape
    width = w2.shape[0]
    ccount = coarse.shape[0]
    ecount = edge.shape[0]
    ucount = up.shape[0]
    devices, slots = send_rows.shape[1], send_rows.shape[2]
    imports = devices * slots
    es, er = edge_sender.reshape(1, ecount), edge_receiver.reshape(1, ecount)
    us, ur = up_sender.reshape(1, ucount), up_receiver.reshape(1, ucount)
    gain_row, ngain_row = gain.reshape(1, lat), ngain.reshape(1, lat)
    own = owner_index()
    core = lax.axis_index("core").reshape(1)
    in_vmem = pl.BlockSpec(memory_space=pltpu.VMEM)
    in_smem = pl.BlockSpec(memory_space=pltpu.SMEM)

    table = send_rows.reshape(imports)
    hot_send = (table[:, None] == jnp.arange(n, dtype=jnp.int32)[None, :]).astype(BF)
    outgoing = dot(hot_send, node).astype(BF)
    halo = lax.all_to_all(
        outgoing.reshape(devices, slots, lat), EVERYONE, 0, 0, tiled=True
    ).reshape(imports, lat)

    up_pre, up_xs, up_xr, keep, send = pl.pallas_call(
        up_forward_kernel,
        in_specs=[in_vmem] * 2 + [in_smem] + [in_vmem] * 6,
        out_shape=(
            shape(ucount, width, F32), shape(ucount, lat, BF), shape(ucount, lat, BF),
            shape(ccount // 2, lat, BF), shape(ccount // 2, lat, BF),
        ),
        scratch_shapes=[pltpu.VMEM((ccount, lat), F32)],
        compiler_params=params(),
        cost_estimate=cost(5.0),
        name="up_forward",
    )(us, ur, core, up, node, coarse, w1, w2, gain_row)

    coarse_total = reduce_rows(keep, send)

    tile = math.gcd(ecount, 256)
    steps = ecount // tile
    rows_spec = pl.BlockSpec((tile, lat), lambda i: (i, 0))
    index_spec = pl.BlockSpec((1, tile), lambda i: (0, i))
    fixed = lambda r, c: pl.BlockSpec((r, c), lambda i: (0, 0))
    pre, xs, fine_total = pl.pallas_call(
        edge_forward_kernel,
        grid=(steps,),
        in_specs=[index_spec, index_spec, rows_spec]
        + [whole(a) for a in (node, halo, coarse, w1, w2, gain_row)],
        out_specs=[pl.BlockSpec((tile, width), lambda i: (i, 0)), rows_spec, fixed(n, lat)],
        out_shape=(shape(ecount, width, F32), shape(ecount, lat, BF), shape(n, lat, BF)),
        scratch_shapes=[pltpu.VMEM((n, lat), F32)],
        compiler_params=params("arbitrary"),
        cost_estimate=cost(9.0),
        name="edge_forward",
    )(es, er, edge, node, halo, coarse, w1, w2, gain_row)

    fine_grad, grad_n, ngw1, ngw2, ngg = pl.pallas_call(
        node_kernel,
        out_shape=(
            shape(n, lat, F32), shape(n, lat, F32), shape(2 * lat, width, BF),
            shape(width, lat, BF), shape(1, lat, F32),
        ),
        compiler_params=params(),
        cost_estimate=cost(5.0),
        name="node_mlp",
    )(node, fine_total, nw1, nw2, ngain_row, ncot)

    grad_e, d_pre, gw2, gg = pl.pallas_call(
        edge_cotangent_kernel,
        grid=(steps,),
        in_specs=[
            index_spec, rows_spec, pl.BlockSpec((tile, width), lambda i: (i, 0)), rows_spec,
        ]
        + [whole(a) for a in (fine_grad, w1, w2, gain_row)],
        out_specs=[
            rows_spec, pl.BlockSpec((tile, width), lambda i: (i, 0)), fixed(width, lat),
            fixed(1, lat),
        ],
        out_shape=(
            shape(ecount, lat, F32), shape(ecount, width, BF), shape(width, lat, BF),
            shape(1, lat, F32),
        ),
        scratch_shapes=[pltpu.VMEM((width, lat), F32)],
        compiler_params=params("arbitrary"),
        cost_estimate=cost(8.0),
        name="edge_cotangent",
    )(er, edge, pre, ecot, fine_grad, w1, w2, gain_row)

    gw1, node_part, returning, coarse_local = pl.pallas_call(
        edge_product_kernel,
        grid=(steps,),
        in_specs=[
            index_spec, index_spec, rows_spec, rows_spec,
            pl.BlockSpec((tile, width), lambda i: (i, 0)),
        ]
        + [whole(a) for a in (node, w1)],
        out_specs=[
            fixed(3 * lat, width), fixed(n, lat), fixed(imports, lat), fixed(ccount, lat),
        ],
        out_shape=(
            shape(3 * lat, width, BF), shape(n, lat, F32), shape(imports, lat, BF),
            shape(ccount, lat, BF),
        ),
        scratch_shapes=[
            pltpu.VMEM((n + imports + ccount, width), F32), pltpu.VMEM((n, width), F32),
            pltpu.VMEM((2 * lat, width), F32),
        ],
        compiler_params=params("arbitrary"),
        cost_estimate=cost(9.0),
        name="edge_product",
    )(es, er, edge, xs, d_pre, node, w1)

    returned = lax.all_to_all(
        returning.reshape(devices, slots, lat), EVERYONE, 0, 0, tiled=True
    ).reshape(imports, lat)

    mine = ccount // devices
    padded = -(-mine // 16) * 16
    pad = lambda a: jnp.pad(a, ((0, padded - mine), (0, 0))) if padded > mine else a
    own_coarse = pad(lax.dynamic_slice_in_dim(coarse, own * mine, mine, 0))
    own_cot = pad(lax.dynamic_slice_in_dim(ccot, own * mine, mine, 0))
    node_rows = padded_rows(2 * lat + width, devices)
    coarse_grad, coarse_after, node_keep, node_send, ngg_sum = pl.pallas_call(
        coarse_kernel,
        in_specs=[in_smem] + [in_vmem] * 9,
        out_shape=(
            shape(padded, lat, BF), shape(padded, lat, F32), shape(node_rows // 2, lat, BF),
            shape(node_rows // 2, lat, BF), shape(1, lat, F32),
        ),
        scratch_shapes=[pltpu.VMEM((node_rows, lat), F32)],
        compiler_params=params(),
        cost_estimate=cost(5.0),
        name="coarse_mlp",
    )(core, own_coarse, pad(coarse_total), own_cot, nw1, nw2, ngain_row, ngw1, ngw2, ngg)
    cg_own, cg_other = gather_halves(coarse_grad[:mine])

    node_total = halving_sum(node_keep, node_send)

    edge_rows = padded_rows(ccount + 3 * lat + width, devices)
    grad_u, up_node_part, keep, send = pl.pallas_call(
        up_backward_kernel,
        in_specs=[in_vmem] * 2 + [in_smem] + [in_vmem] * 16,
        out_shape=(
            shape(ucount, lat, F32), shape(n, lat, F32), shape(edge_rows // 2 + TAIL, lat, BF),
            shape(edge_rows // 2 + TAIL, lat, BF),
        ),
        scratch_shapes=[pltpu.VMEM((ccount, lat), F32), pltpu.VMEM((edge_rows, lat), BF)],
        compiler_params=params(),
        cost_estimate=cost(8.0),
        name="up_backward",
    )(
        us, ur, jnp.stack([own, core[0]]), up, up_xs, up_xr, up_pre, ucot, cg_own, cg_other,
        w1, w2, gain_row, gw1, gw2, gg, ngg_sum, coarse_local, coarse_after[:mine],
    )
    block, gains, returned = reduce_with_tail(keep, send, returned)
    own_half, other_half = gather_halves(block)
    first = core[0] == 0
    edge_total = jnp.concatenate(
        [jnp.where(first, own_half, other_half), jnp.where(first, other_half, own_half)], 0
    )

    grad_nodes = (
        grad_n
        + node_part
        + up_node_part
        + lax.dot_general(hot_send, returned, (((0,), (0,)), ((), ())), preferred_element_type=F32)
    )
    edge_scale = 1.0 / math.sqrt((ecount + ucount) * devices)
    node_scale = 1.0 / math.sqrt(n * devices + ccount)
    in_end = ccount + 3 * lat
    return (
        grad_nodes,
        edge_total[:ccount].astype(F32),
        grad_e,
        grad_u,
        edge_total[ccount:in_end].astype(F32) * edge_scale,
        edge_total[in_end : in_end + width].astype(F32) * edge_scale,
        gains[0] * edge_scale,
        node_total[: 2 * lat].astype(F32) * node_scale,
        node_total[2 * lat : 2 * lat + width].astype(F32) * node_scale,
        gains[1] * node_scale,
    )


def split_mesh(mesh):
    face, band = mesh.shape["face"], mesh.shape["band"]
    z = 1
    while z * z < face or face % z:
        z += 1
    core = 2 if band % 2 == 0 else 1
    return Mesh(
        mesh.devices.reshape(z, face // z, band // core, core), ("z", "x", "y", "core")
    )


def solution(mesh):
    rows, split = P(EVERYONE, None), P(EVERYONE)
    return jax.shard_map(
        per_device,
        mesh=split_mesh(mesh),
        in_specs=(
            rows, P(), rows, rows, P(), P(), P(), P(), P(), P(), rows, P(), rows, rows,
            P(EVERYONE, None, None), split, split, split, split,
        ),
        out_specs=(rows, P(), rows, rows, P(), P(), P(), P(), P(), P()),
        check_vma=False,
    )
```

profile of v0, /device:TPU:0, one launch (start us, length us, event | category | flops | bytes accessed | tf_op | source)
XLA Modules:
  0.0 225.7 jit_solution(5551416640139451256)
XLA Ops:
  0.7 4.9 %up_forward.1 = (f32[256,512]{1,0:T(8,128)}, bf16[256,512]{1,0:T(8,128)(2,1)}, bf16[256,512]{1,0:T(8,128)(2,1)}, bf16[512,512]{1,0:T(8,128)(2,1)}, bf16[512,512]{1,0:T(8,128)(2,1)}) custom-call(s32[1,256]{1,0:T(1,128)} %bitcast.42, s32[1,256]{1,0:T(1,128)} %bitcast.44, s32[1]{0:T(128)} %bitcast.7.core, bf16[256,512]{1,0:T(8,128)(2,1)} %up.3, ...), custom_call_target="tpu_custom_call" | custom-call | flops 5500000256 | bytes 15000000 | tf_op jit(solution)/shard_map/up_forward/pallas_call | solution.py:455
  7.2 6.9 %all-to-all-start = ((bf16[32,4,512]{2,1,0:T(4,128)(2,1)}), bf16[32,4,512]{2,1,0:T(4,128)(2,1)S(1)}, u32[]{:S(2)}, u32[]{:S(2)}) async-start(bf16[32,4,512]{2,1,0:T(4,128)(2,1)} %reshape.120), calls=%async_computation | async-start | bytes 262144 | tf_op jit(solution)/shard_map/all_to_all | solution.py:451
  16.2 6.2 %all-to-all-done = bf16[32,4,512]{2,1,0:T(4,128)(2,1)S(1)} async-done(((bf16[32,4,512]{2,1,0:T(4,128)(2,1)}), bf16[32,4,512]{2,1,0:T(4,128)(2,1)S(1)}, u32[]{:S(2)}, u32[]{:S(2)}) %all-to-all-start) | async-done | bytes 131104 | tf_op jit(solution)/shard_map/all_to_all | solution.py:451
  24.0 3.5 %all-to-all-start.1 = ((bf16[4,128,512]{2,1,0:T(8,128)(2,1)}), bf16[4,128,512]{2,1,0:T(8,128)(2,1)S(1)}, u32[]{:S(2)}, u32[]{:S(2)}) async-start(bf16[4,128,512]{2,1,0:T(8,128)(2,1)} %bitcast.8), calls=%async_computation.1 | async-start | bytes 1048576 | tf_op jit(solution)/shard_map/all_to_all | solution.py:328
  27.5 10.2 %edge_forward.1 = (f32[1024,512]{1,0:T(8,128)}, bf16[1024,512]{1,0:T(8,128)(2,1)}, bf16[256,512]{1,0:T(8,128)(2,1)}) custom-call(s32[1,1024]{1,0:T(1,128)} %bitcast.31, s32[1,1024]{1,0:T(1,128)} %bitcast.33, bf16[1024,512]{1,0:T(8,128)(2,1)} %edge.5, bf16[256,512]{1,0:T(8,128)(2,1)} %node.7, bf16[128,512]{1,0:T(8,128)(2,1)} %reshape.121.halo, ...), custom_call_target="tpu_custom_call" | custom-call | flops 9900000256 | bytes 27000000 | tf_op jit(solution)/shard_map/edge_forward/pallas_call | solution.py:475
  38.4 3.3 %all-to-all-start.2 = ((bf16[4,32,512]{2,1,0:T(8,128)(2,1)}), bf16[4,32,512]{2,1,0:T(8,128)(2,1)S(1)}, u32[]{:S(2)}, u32[]{:S(2)}) async-start(bf16[4,32,512]{2,1,0:T(8,128)(2,1)} %bitcast.9), calls=%async_computation.2 | async-start | bytes 262144 | tf_op jit(solution)/shard_map/all_to_all | solution.py:328
  41.7 4.7 %node_mlp.1 = (f32[256,512]{1,0:T(8,128)}, f32[256,512]{1,0:T(8,128)}, bf16[1024,512]{1,0:T(8,128)(2,1)}, bf16[512,512]{1,0:T(8,128)(2,1)}, f32[1,512]{1,0:T(1,128)}) custom-call(bf16[256,512]{1,0:T(8,128)(2,1)} %node.7, bf16[256,512]{1,0:T(8,128)(2,1)} %get-tuple-element.50.total_in, bf16[1024,512]{1,0:T(8,128)(2,1)} %nw1.3, bf16[512,512]{1,0:T(8,128)(2,1)} %nw2.3, ...), custom_call_target="tpu_custom_call" | custom-call | flops 5500000256 | bytes 15000000 | tf_op jit(solution)/shard_map/node_mlp/pallas_call | solution.py:488
  48.8 4.9 %coarse_mlp.1 = (bf16[32,512]{1,0:T(8,128)(2,1)}, f32[32,512]{1,0:T(8,128)}, bf16[768,512]{1,0:T(8,128)(2,1)}, bf16[768,512]{1,0:T(8,128)(2,1)}, f32[1,512]{1,0:T(1,128)}) custom-call(s32[1]{0:T(128)} %bitcast.7.core, bf16[32,512]{1,0:T(8,128)(2,1)} %constant_dynamic-slice_fusion.1.rows, f32[32,512]{1,0:T(8,128)} %convert_reduce_fusion.1.total_in, ...), custom_call_target="tpu_custom_call" | custom-call | flops 5500000256 | bytes 15000000 | tf_op jit(solution)/shard_map/coarse_mlp/pallas_call | solution.py:554
  55.1 3.4 %all-to-all-start.3 = ((bf16[4,32,512]{2,1,0:T(8,128)(2,1)}), bf16[4,32,512]{2,1,0:T(8,128)(2,1)S(1)}, u32[]{:S(2)}, u32[]{:S(2)}) async-start(bf16[4,32,512]{2,1,0:T(8,128)(2,1)} %broadcast_in_dim.12), calls=%async_computation.3 | async-start | bytes 262144 | tf_op jit(solution)/shard_map/all_to_all | solution.py:328
  59.1 5.4 %all-to-all-done.3 = bf16[4,32,512]{2,1,0:T(8,128)(2,1)S(1)} async-done(((bf16[4,32,512]{2,1,0:T(8,128)(2,1)}), bf16[4,32,512]{2,1,0:T(8,128)(2,1)S(1)}, u32[]{:S(2)}, u32[]{:S(2)}) %all-to-all-start.3) | async-done | bytes 131104 | tf_op jit(solution)/shard_map/all_to_all | solution.py:328
  65.4 4.1 %all-to-all-start.4 = ((bf16[4,128,512]{2,1,0:T(8,128)(2,1)}), bf16[4,128,512]{2,1,0:T(8,128)(2,1)S(1)}, u32[]{:S(2)}, u32[]{:S(2)}) async-start(bf16[4,128,512]{2,1,0:T(8,128)(2,1)} %broadcast_in_dim.14), calls=%async_computation.4 | async-start | bytes 1048576 | tf_op jit(solution)/shard_map/all_to_all | solution.py:328
  69.5 9.0 %edge_cotangent.1 = (f32[1024,512]{1,0:T(8,128)}, bf16[1024,512]{1,0:T(8,128)(2,1)}, bf16[512,512]{1,0:T(8,128)(2,1)}, f32[1,512]{1,0:T(1,128)}) custom-call(s32[1,1024]{1,0:T(1,128)} %bitcast.34, bf16[1024,512]{1,0:T(8,128)(2,1)} %edge.5, f32[1024,512]{1,0:T(8,128)} %get-tuple-element.53.pre_ref, bf16[1024,512]{1,0:T(8,128)(2,1)} %ecot.1, ...), custom_call_target="tpu_custom_call" | custom-call | flops 8800000000 | bytes 24000000 | tf_op jit(solution)/shard_map/edge_cotangent/pallas_call | solution.py:499
  78.7 9.4 %edge_product.1 = (bf16[1536,512]{1,0:T(8,128)(2,1)}, f32[256,512]{1,0:T(8,128)}, bf16[128,512]{1,0:T(8,128)(2,1)}, bf16[1024,512]{1,0:T(8,128)(2,1)}) custom-call(s32[1,1024]{1,0:T(1,128)} %bitcast.32, s32[1,1024]{1,0:T(1,128)} %bitcast.35, bf16[1024,512]{1,0:T(8,128)(2,1)} %edge.5, bf16[1024,512]{1,0:T(8,128)(2,1)} %get-tuple-element.52.xs, ...), custom_call_target="tpu_custom_call" | custom-call | flops 9900000256 | bytes 27000000 | tf_op jit(solution)/shard_map/edge_product/pallas_call | solution.py:520
  88.9 8.2 %up_backward.1 = (f32[256,512]{1,0:T(8,128)}, f32[256,512]{1,0:T(8,128)}, bf16[1552,512]{1,0:T(8,128)(2,1)}, bf16[1552,512]{1,0:T(8,128)(2,1)}) custom-call(s32[1,256]{1,0:T(1,128)} %bitcast.43, s32[1,256]{1,0:T(1,128)} %bitcast.45, s32[2]{0:T(128)} %pad_add_fusion.place, bf16[256,512]{1,0:T(8,128)(2,1)} %up.3, bf16[256,512]{1,0:T(8,128)(2,1)} %get-tuple-element.57.xs, ...), custom_call_target="tpu_custom_call" | custom-call | flops 8800000000 | bytes 24000000 | tf_op jit(solution)/shard_map/up_backward/pallas_call | solution.py:571
  97.5 12.0 %all_to_all.69 = bf16[32,4,512]{2,1,0:T(4,128)(2,1)S(1)} all-to-all(bf16[32,4,512]{2,1,0:T(4,128)(2,1)S(1)} %reshape.126), channel_id=1, replica_groups=mesh['z'=4,'x'=2,'y'=2,'core'=2] {'z','x','y','core'}, dimensions={0} | all-to-all | bytes 262144 | tf_op jit(solution)/shard_map/all_to_all | solution.py:544
  110.7 3.4 %shard_map.258 = bf16[4,400,512]{2,1,0:T(8,128)(2,1)} custom-call(bf16[1552,512]{1,0:T(8,128)(2,1)} %get-tuple-element.76.keep, bf16[1552,512]{1,0:T(8,128)(2,1)} %copy-done.8), custom_call_target="tpu_custom_call" | custom-call | flops 3300000000 | bytes 9000000 | tf_op jit(solution)/shard_map/pallas_call | solution.py:380
  114.1 3.6 %all-to-all-start.6 = ((bf16[4,400,512]{2,1,0:T(8,128)(2,1)}), bf16[4,400,512]{2,1,0:T(8,128)(2,1)S(1)}, u32[]{:S(2)}, u32[]{:S(2)}) async-start(bf16[4,400,512]{2,1,0:T(8,128)(2,1)} %shard_map.258), calls=%async_computation.6 | async-start | bytes 3276800 | tf_op jit(solution)/shard_map/all_to_all | solution.py:328
  123.4 14.9 %all-to-all-done.6.got = bf16[4,400,512]{2,1,0:T(8,128)(2,1)S(1)} async-done(((bf16[4,400,512]{2,1,0:T(8,128)(2,1)}), bf16[4,400,512]{2,1,0:T(8,128)(2,1)S(1)}, u32[]{:S(2)}, u32[]{:S(2)}) %all-to-all-start.6) | async-done | bytes 1638432 | tf_op jit(solution)/shard_map/all_to_all | solution.py:328
  141.8 3.5 %all-to-all-start.7 = ((bf16[4,112,512]{2,1,0:T(8,128)(2,1)}), bf16[4,112,512]{2,1,0:T(8,128)(2,1)S(1)}, u32[]{:S(2)}, u32[]{:S(2)}) async-start(bf16[4,112,512]{2,1,0:T(8,128)(2,1)} %shard_map.259), calls=%async_computation.7 | async-start | bytes 917504 | tf_op jit(solution)/shard_map/all_to_all | solution.py:328
  150.8 15.7 %collective-permute-done.6.recv = bf16[192,512]{1,0:T(8,128)(2,1)S(1)} collective-permute-done((bf16[192,512]{1,0:T(8,128)(2,1)}, bf16[192,512]{1,0:T(8,128)(2,1)S(1)}, u32[]{:S(2)}, u32[]{:S(2)}) %collective-permute-start.6) | collective-permute-done | bytes 196640 | tf_op jit(solution)/shard_map/ppermute | solution.py:345
  171.3 3.5 %all-to-all-start.8 = ((bf16[4,96,512]{2,1,0:T(8,128)(2,1)}), bf16[4,96,512]{2,1,0:T(8,128)(2,1)S(1)}, u32[]{:S(2)}, u32[]{:S(2)}) async-start(bf16[4,96,512]{2,1,0:T(8,128)(2,1)} %broadcast_in_dim.15), calls=%async_computation.8 | async-start | bytes 786432 | tf_op jit(solution)/shard_map/all_to_all | solution.py:328
  188.3 3.8 %all-to-all-start.9 = ((bf16[4,384,512]{2,1,0:T(8,128)(2,1)}), bf16[4,384,512]{2,1,0:T(8,128)(2,1)S(1)}, u32[]{:S(2)}, u32[]{:S(2)}) async-start(bf16[4,384,512]{2,1,0:T(8,128)(2,1)} %broadcast_in_dim.34), calls=%async_computation.9 | async-start | bytes 3145728 | tf_op jit(solution)/shard_map/all_to_all | solution.py:328
  195.1 6.3 %collective-permute-done.11 = bf16[192,512]{1,0:T(8,128)(2,1)S(1)} collective-permute-done((bf16[192,512]{1,0:T(8,128)(2,1)S(1)}, bf16[192,512]{1,0:T(8,128)(2,1)S(1)}, u32[]{:S(2)}, u32[]{:S(2)}) %collective-permute-start.11) | collective-permute-done | bytes 196640 | tf_op jit(solution)/shard_map/ppermute | solution.py:345
  202.1 7.7 %collective-permute-done.12 = bf16[384,512]{1,0:T(8,128)(2,1)S(1)} collective-permute-done((bf16[384,512]{1,0:T(8,128)(2,1)S(1)}, bf16[384,512]{1,0:T(8,128)(2,1)S(1)}, u32[]{:S(2)}, u32[]{:S(2)}) %collective-permute-start.12) | collective-permute-done | bytes 393248 | tf_op jit(solution)/shard_map/ppermute | solution.py:345
  (95 shorter events, 66.1 us)
Async XLA Ops:
  5.6 17.5 %copy-start.2 = (bf16[512,512]{1,0:T(8,128)(2,1)S(1)}, bf16[512,512]{1,0:T(8,128)(2,1)}, u32[]{:S(2)}) copy-start(bf16[512,512]{1,0:T(8,128)(2,1)} %get-tuple-element.60) | copy-start | bytes 1572868
  5.6 17.5 %collective-permute-start = (bf16[512,512]{1,0:T(8,128)(2,1)}, bf16[512,512]{1,0:T(8,128)(2,1)S(1)}, u32[]{:S(2)}, u32[]{:S(2)}) collective-permute-start(bf16[512,512]{1,0:T(8,128)(2,1)} %get-tuple-element.61), channel_id=1, source_target_pairs={{0,1},{1,0},{2,3},{3,2},{4,5},{5,4},{6,7},{7,6},{8,9},{9,8},{10,11... | collective-permute-start | bytes 1572872 | tf_op jit(solution)/shard_map/ppermute | solution.py:345
  7.2 15.2 %all-to-all-start = ((bf16[32,4,512]{2,1,0:T(4,128)(2,1)}), bf16[32,4,512]{2,1,0:T(4,128)(2,1)S(1)}, u32[]{:S(2)}, u32[]{:S(2)}) async-start(bf16[32,4,512]{2,1,0:T(4,128)(2,1)} %reshape.120), calls=%async_computation | async-start | bytes 262144 | tf_op jit(solution)/shard_map/all_to_all | solution.py:451
  24.0 13.6 %all-to-all-start.1 = ((bf16[4,128,512]{2,1,0:T(8,128)(2,1)}), bf16[4,128,512]{2,1,0:T(8,128)(2,1)S(1)}, u32[]{:S(2)}, u32[]{:S(2)}) async-start(bf16[4,128,512]{2,1,0:T(8,128)(2,1)} %bitcast.8), calls=%async_computation.1 | async-start | bytes 1048576 | tf_op jit(solution)/shard_map/all_to_all | solution.py:328
  38.4 9.7 %all-to-all-start.2 = ((bf16[4,32,512]{2,1,0:T(8,128)(2,1)}), bf16[4,32,512]{2,1,0:T(8,128)(2,1)S(1)}, u32[]{:S(2)}, u32[]{:S(2)}) async-start(bf16[4,32,512]{2,1,0:T(8,128)(2,1)} %bitcast.9), calls=%async_computation.2 | async-start | bytes 262144 | tf_op jit(solution)/shard_map/all_to_all | solution.py:328
  55.1 9.5 %all-to-all-start.3 = ((bf16[4,32,512]{2,1,0:T(8,128)(2,1)}), bf16[4,32,512]{2,1,0:T(8,128)(2,1)S(1)}, u32[]{:S(2)}, u32[]{:S(2)}) async-start(bf16[4,32,512]{2,1,0:T(8,128)(2,1)} %broadcast_in_dim.12), calls=%async_computation.3 | async-start | bytes 262144 | tf_op jit(solution)/shard_map/all_to_all | solution.py:328
  65.4 13.2 %all-to-all-start.4 = ((bf16[4,128,512]{2,1,0:T(8,128)(2,1)}), bf16[4,128,512]{2,1,0:T(8,128)(2,1)S(1)}, u32[]{:S(2)}, u32[]{:S(2)}) async-start(bf16[4,128,512]{2,1,0:T(8,128)(2,1)} %broadcast_in_dim.14), calls=%async_computation.4 | async-start | bytes 1048576 | tf_op jit(solution)/shard_map/all_to_all | solution.py:328
  78.6 9.5 %collective-permute-start.1 = (bf16[512,512]{1,0:T(8,128)(2,1)S(1)}, bf16[512,512]{1,0:T(8,128)(2,1)S(1)}, u32[]{:S(2)}, u32[]{:S(2)}) collective-permute-start(bf16[512,512]{1,0:T(8,128)(2,1)S(1)} %bitcast.27), channel_id=1, source_target_pairs={{0,1},{1,0},{2,3},{3,2},{4,5},{5,4},{6,7},{7,6},{8,9},{9,8},{10,11... | collective-permute-start | bytes 1572872 | tf_op jit(solution)/shard_map/ppermute | solution.py:345
  97.1 12.5 %collective-permute-start.2 = (bf16[1552,512]{1,0:T(8,128)(2,1)}, bf16[1552,512]{1,0:T(8,128)(2,1)S(1)}, u32[]{:S(2)}, u32[]{:S(2)}) collective-permute-start(bf16[1552,512]{1,0:T(8,128)(2,1)} %get-tuple-element.73), channel_id=1, source_target_pairs={{0,1},{1,0},{2,3},{3,2},{4,5},{5,4},{6,7},{7,6},{8,9},{9,8},{10,11... | collective-permute-start | bytes 4767752 | tf_op jit(solution)/shard_map/ppermute | solution.py:345
  114.1 24.2 %all-to-all-start.6 = ((bf16[4,400,512]{2,1,0:T(8,128)(2,1)}), bf16[4,400,512]{2,1,0:T(8,128)(2,1)S(1)}, u32[]{:S(2)}, u32[]{:S(2)}) async-start(bf16[4,400,512]{2,1,0:T(8,128)(2,1)} %shard_map.258), calls=%async_computation.6 | async-start | bytes 3276800 | tf_op jit(solution)/shard_map/all_to_all | solution.py:328
  117.7 2.7 %collective-permute-start.4 = (bf16[768,512]{1,0:T(8,128)(2,1)}, bf16[768,512]{1,0:T(8,128)(2,1)}, u32[]{:S(2)}, u32[]{:S(2)}) collective-permute-start(bf16[768,512]{1,0:T(8,128)(2,1)} %get-tuple-element.81), channel_id=1, source_target_pairs={{0,1},{1,0},{2,3},{3,2},{4,5},{5,4},{6,7},{7,6},{8,9},{9,8},{10,11... | collective-permute-start | bytes 2359304 | tf_op jit(solution)/shard_map/ppermute | solution.py:345
  122.7 22.6 %collective-permute-start.5 = (bf16[384,512]{1,0:T(8,128)(2,1)}, bf16[384,512]{1,0:T(8,128)(2,1)S(1)}, u32[]{:S(2)}, u32[]{:S(2)}) collective-permute-start(bf16[384,512]{1,0:T(8,128)(2,1)} %get-tuple-element.83), channel_id=1, source_target_pairs={{0,8},{1,9},{2,10},{3,11},{4,12},{5,13},{6,14},{7,15},{8,0},{9,1},... | collective-permute-start | bytes 1179656 | tf_op jit(solution)/shard_map/ppermute | solution.py:345
  141.8 28.6 %all-to-all-start.7 = ((bf16[4,112,512]{2,1,0:T(8,128)(2,1)}), bf16[4,112,512]{2,1,0:T(8,128)(2,1)S(1)}, u32[]{:S(2)}, u32[]{:S(2)}) async-start(bf16[4,112,512]{2,1,0:T(8,128)(2,1)} %shard_map.259), calls=%async_computation.7 | async-start | bytes 917504 | tf_op jit(solution)/shard_map/all_to_all | solution.py:328
  148.0 18.6 %collective-permute-start.6 = (bf16[192,512]{1,0:T(8,128)(2,1)}, bf16[192,512]{1,0:T(8,128)(2,1)S(1)}, u32[]{:S(2)}, u32[]{:S(2)}) collective-permute-start(bf16[192,512]{1,0:T(8,128)(2,1)} %get-tuple-element.85), channel_id=1, source_target_pairs={{0,16},{1,17},{2,18},{3,19},{4,20},{5,21},{6,22},{7,23},{8,24},{9,... | collective-permute-start | bytes 589832 | tf_op jit(solution)/shard_map/ppermute | solution.py:345
  169.0 5.8 %collective-permute-start.7 = (bf16[96,512]{1,0:T(8,128)(2,1)}, bf16[96,512]{1,0:T(8,128)(2,1)S(1)}, u32[]{:S(2)}, u32[]{:S(2)}) collective-permute-start(bf16[96,512]{1,0:T(8,128)(2,1)} %get-tuple-element.87), channel_id=1, source_target_pairs={{0,2},{1,3},{2,0},{3,1},{4,6},{5,7},{6,4},{7,5},{8,10},{9,11},{10,... | collective-permute-start | bytes 294920 | tf_op jit(solution)/shard_map/ppermute | solution.py:345
  171.3 15.7 %all-to-all-start.8 = ((bf16[4,96,512]{2,1,0:T(8,128)(2,1)}), bf16[4,96,512]{2,1,0:T(8,128)(2,1)S(1)}, u32[]{:S(2)}, u32[]{:S(2)}) async-start(bf16[4,96,512]{2,1,0:T(8,128)(2,1)} %broadcast_in_dim.15), calls=%async_computation.8 | async-start | bytes 786432 | tf_op jit(solution)/shard_map/all_to_all | solution.py:328
  177.1 4.3 %collective-permute-start.8 = (bf16[48,512]{1,0:T(8,128)(2,1)}, bf16[48,512]{1,0:T(8,128)(2,1)S(1)}, u32[]{:S(2)}, u32[]{:S(2)}) collective-permute-start(bf16[48,512]{1,0:T(8,128)(2,1)} %get-tuple-element.89), channel_id=1, source_target_pairs={{0,4},{1,5},{2,6},{3,7},{4,0},{5,1},{6,2},{7,3},{8,12},{9,13},{10,... | collective-permute-start | bytes 147464 | tf_op jit(solution)/shard_map/ppermute | solution.py:345
  182.2 4.2 %collective-permute-start.9 = (bf16[48,512]{1,0:T(8,128)(2,1)S(1)}, bf16[48,512]{1,0:T(8,128)(2,1)S(1)}, u32[]{:S(2)}, u32[]{:S(2)}) collective-permute-start(bf16[48,512]{1,0:T(8,128)(2,1)S(1)} %add_convert_fusion.1), channel_id=1, source_target_pairs={{0,4},{1,5},{2,6},{3,7},{4,0},{5,1},{6,2},{7,3},{8,12},{9,13},{10,... | collective-permute-start | bytes 147464 | tf_op jit(solution)/shard_map/ppermute | solution.py:345
  186.3 5.8 %collective-permute-start.10 = (bf16[96,512]{1,0:T(8,128)(2,1)S(1)}, bf16[96,512]{1,0:T(8,128)(2,1)S(1)}, u32[]{:S(2)}, u32[]{:S(2)}) collective-permute-start(bf16[96,512]{1,0:T(8,128)(2,1)S(1)} %maximum_select_fusion.4), channel_id=1, source_target_pairs={{0,2},{1,3},{2,0},{3,1},{4,6},{5,7},{6,4},{7,5},{8,10},{9,11},{10,... | collective-permute-start | bytes 294920 | tf_op jit(solution)/shard_map/ppermute | solution.py:345
  188.3 21.9 %all-to-all-start.9 = ((bf16[4,384,512]{2,1,0:T(8,128)(2,1)}), bf16[4,384,512]{2,1,0:T(8,128)(2,1)S(1)}, u32[]{:S(2)}, u32[]{:S(2)}) async-start(bf16[4,384,512]{2,1,0:T(8,128)(2,1)} %broadcast_in_dim.34), calls=%async_computation.9 | async-start | bytes 3145728 | tf_op jit(solution)/shard_map/all_to_all | solution.py:328
  192.2 9.3 %collective-permute-start.11 = (bf16[192,512]{1,0:T(8,128)(2,1)S(1)}, bf16[192,512]{1,0:T(8,128)(2,1)S(1)}, u32[]{:S(2)}, u32[]{:S(2)}) collective-permute-start(bf16[192,512]{1,0:T(8,128)(2,1)S(1)} %maximum_select_fusion.3), channel_id=1, source_target_pairs={{0,16},{1,17},{2,18},{3,19},{4,20},{5,21},{6,22},{7,23},{8,24},{9,... | collective-permute-start | bytes 589832 | tf_op jit(solution)/shard_map/ppermute | solution.py:345
  201.6 8.2 %collective-permute-start.12 = (bf16[384,512]{1,0:T(8,128)(2,1)S(1)}, bf16[384,512]{1,0:T(8,128)(2,1)S(1)}, u32[]{:S(2)}, u32[]{:S(2)}) collective-permute-start(bf16[384,512]{1,0:T(8,128)(2,1)S(1)} %maximum_select_fusion.2), channel_id=1, source_target_pairs={{0,8},{1,9},{2,10},{3,11},{4,12},{5,13},{6,14},{7,15},{8,0},{9,1},... | collective-permute-start | bytes 1179656 | tf_op jit(solution)/shard_map/ppermute | solution.py:345
  210.1 3.1 %collective-permute-start.13 = (bf16[768,512]{1,0:T(8,128)(2,1)S(1)}, bf16[768,512]{1,0:T(8,128)(2,1)}, u32[]{:S(2)}, u32[]{:S(2)}) collective-permute-start(bf16[768,512]{1,0:T(8,128)(2,1)S(1)} %maximum_select_fusion.1), channel_id=1, source_target_pairs={{0,1},{1,0},{2,3},{3,2},{4,5},{5,4},{6,7},{7,6},{8,9},{9,8},{10,11... | collective-permute-start | bytes 2359304 | tf_op jit(solution)/shard_map/ppermute | solution.py:345
  210.2 9.0 %collective-permute-start.3 = (bf16[1536,512]{1,0:T(8,128)(2,1)S(1)}, bf16[1536,512]{1,0:T(8,128)(2,1)}, u32[]{:S(2)}, u32[]{:S(2)}) collective-permute-start(bf16[1536,512]{1,0:T(8,128)(2,1)S(1)} %bitcast.24), channel_id=1, source_target_pairs={{0,1},{1,0},{2,3},{3,2},{4,5},{5,4},{6,7},{7,6},{8,9},{9,8},{10,11... | collective-permute-start | bytes 4718600 | tf_op jit(solution)/shard_map/ppermute | solution.py:345
  (12 other events, 55.8 us)
where the time goes:
time: 229 us; the launch traced here: 226 us
  waiting for transfers between devices  66.6 us (29%)
  Pallas kernels  64.7 us (28%)
  starting transfers between devices  48.7 us (21%)
  other arithmetic  16.8 us (7%)
  local copies, waits for them, and re-layouts  13.1 us (6%)
  blocking collectives  12 us (5%)
  matrix products  2.72 us (1%)
    ppermute x14, waiting for transfers between devices, exchange(): return lax.ppermute(x, EVERYONE, [(i, i ^ mask) for i in range(devices)])  38.4 us
    all_to_all x8, starting transfers between devices, swap(): return lax.all_to_all(x, axes, 0, 0, tiled=True)  28.6 us
    all_to_all x8, waiting for transfers between devices, swap(): return lax.all_to_all(x, axes, 0, 0, tiled=True)  22 us
    ppermute x14, starting transfers between devices, exchange(): return lax.ppermute(x, EVERYONE, [(i, i ^ mask) for i in range(devices)])  13.2 us
    all_to_all x1, blocking collectives, per_device(): lax.all_to_all(returning.reshape(devices, slots, lat), EVERYONE, 0, 0, ti...  12 us
    pallas_call x1, Pallas kernels, per_device(): pl.pallas_call(edge_forward_kernel, grid=(steps,), in_specs=[index_spec,...  10.2 us
    pallas_call x1, Pallas kernels, per_device(): pl.pallas_call(edge_product_kernel, grid=(steps,), in_specs=[index_spec,...  9.37 us
    pallas_call x1, Pallas kernels, per_device(): pl.pallas_call(edge_cotangent_kernel, grid=(steps,), in_specs=[index_spec...  9.02 us
  transfers between devices with their start and end apart: 23, of which 10 were waited for; matrix products, arithmetic and copies ran while one was open for 7% of the time, Pallas kernels for 19%

commit v1 on v0

--- a/solution.py
+++ b/solution.py
@@ -1,3 +1,4 @@
+import functools
 import math
 
 import jax
@@ -12,7 +13,7 @@
 F32 = jnp.float32
 TAIL = 16
 EVERYONE = ("z", "x", "y", "core")
-VMEM_LIMIT = 56 * 1024 * 1024
+VMEM_LIMIT = 24 * 1024 * 1024
 
 
 def dot(a, b):
@@ -282,17 +283,21 @@
     count = after.shape[0]
     mine = pl.ds(pl.multiple_of(place[0] * count, 8), count)
     csum[mine, :] = csum[mine, :] + after[...]
-    pay[0:coarse] = csum[...].astype(BF)
-    start = coarse
-    for x in (up, xs, xr):
-        piece = slice(start - coarse, start - coarse + lat)
-        pay[start : start + lat] = (gw1[piece].astype(F32) + dot_lt(x[...], d_pre)).astype(BF)
-        start += lat
-    end = start + gw2.shape[0]
-    pay[start:end] = (gw2[...].astype(F32) + dot_lt(hidden, d_proj)).astype(BF)
-    if end < pay.shape[0]:
-        pay[end:] = jnp.zeros((pay.shape[0] - end, lat), BF)
     rows = pay.shape[0] // 2
+    first = [csum[...]]
+    second = [gw2[...].astype(F32) + dot_lt(hidden, d_proj)]
+    for k, x in enumerate((up, xs, xr)):
+        piece = slice(k * lat, (k + 1) * lat)
+        second.insert(k, gw1[piece].astype(F32) + dot_lt(x[...], d_pre))
+    w1_part = jnp.concatenate(second[:-1], axis=0)
+    for h in range(2):
+        start = h * rows
+        for full in (first[0], w1_part, second[-1]):
+            size = full.shape[0] // 2
+            pay[start : start + size] = full[h * size : (h + 1) * size].astype(BF)
+            start += size
+        if start < (h + 1) * rows:
+            pay[start : (h + 1) * rows] = jnp.zeros(((h + 1) * rows - start, lat), BF)
     split_rows(pay, core, keep_ref.at[0:rows], send_ref.at[0:rows])
     ids = lax.broadcasted_iota(jnp.int32, (TAIL, lat), 0)
     edge_row = jnp.broadcast_to(gg[...] + gain_part, (TAIL, lat))
@@ -300,6 +305,19 @@
     tail = jnp.where(ids == 0, edge_row, jnp.where(ids == 1, node_row, 0.0)).astype(BF)
     keep_ref[rows:] = tail
     send_ref[rows:] = tail
+
+
+def widen_kernel(core, half, coarse_ref, first_ref, second_ref, *, scale):
+    start = 0
+    for out_ref, factor in ((coarse_ref, None), (first_ref, scale), (second_ref, scale)):
+        rows = out_ref.shape[1]
+        values = half[start : start + rows].astype(F32)
+        out_ref[0] = values if factor is None else values * factor
+        start += rows
+
+
+def widen_other_kernel(core, half, c_in, f_in, s_in, coarse_ref, first_ref, second_ref, *, scale):
+    widen_kernel(core, half, coarse_ref, first_ref, second_ref, scale=scale)
 
 
 def params(*semantics):
@@ -391,8 +409,12 @@
 
 def bit_masks(devices):
     slow = devices // lax.axis_size("z")
-    order = [m for m in (1 << b for b in range(1, devices.bit_length())) if m < devices]
-    return [m for m in order if m >= slow] + [m for m in order if m < slow]
+    order = [1 << b for b in range(1, devices.bit_length() - 1)]
+    return (
+        [m for m in order if m == slow]
+        + [m for m in reversed(order) if m < slow]
+        + [m for m in order if m > slow]
+    )
 
 
 def halving_sum(keep, send):
@@ -585,10 +607,42 @@
     )
     block, gains, returned = reduce_with_tail(keep, send, returned)
     own_half, other_half = gather_halves(block)
-    first = core[0] == 0
-    edge_total = jnp.concatenate(
-        [jnp.where(first, own_half, other_half), jnp.where(first, other_half, own_half)], 0
-    )
+    edge_scale = 1.0 / math.sqrt((ecount + ucount) * devices)
+    node_scale = 1.0 / math.sqrt(n * devices + ccount)
+    halves = [ccount // 2, 3 * lat // 2, width // 2]
+    outs = tuple(jax.ShapeDtypeStruct((2, rows, lat), F32) for rows in halves)
+
+    def place_of(flip):
+        return [
+            pl.BlockSpec((1, rows, lat), lambda i, c: (c[0] ^ flip, 0, 0)) for rows in halves
+        ]
+
+    half_spec = pl.BlockSpec(own_half.shape, lambda i, c: (0, 0))
+    written = pl.pallas_call(
+        functools.partial(widen_kernel, scale=edge_scale),
+        grid_spec=pltpu.PrefetchScalarGridSpec(
+            num_scalar_prefetch=1, grid=(1,), in_specs=[half_spec], out_specs=place_of(0)
+        ),
+        out_shape=outs,
+        compiler_params=params("arbitrary"),
+        cost_estimate=cost(2.5),
+        name="widen_own",
+    )(core, own_half)
+    written = pl.pallas_call(
+        functools.partial(widen_other_kernel, scale=edge_scale),
+        grid_spec=pltpu.PrefetchScalarGridSpec(
+            num_scalar_prefetch=1,
+            grid=(1,),
+            in_specs=[half_spec] + [pl.BlockSpec(memory_space=pl.ANY)] * 3,
+            out_specs=place_of(1),
+        ),
+        out_shape=outs,
+        input_output_aliases={2: 0, 3: 1, 4: 2},
+        compiler_params=params("arbitrary"),
+        cost_estimate=cost(2.5),
+        name="widen_other",
+    )(core, other_half, *written)
+    grad_coarse, grad_edge_in, grad_edge_out = (a.reshape(-1, lat) for a in written)
 
     grad_nodes = (
         grad_n
@@ -596,19 +650,18 @@
         + up_node_part
         + lax.dot_general(hot_send, returned, (((0,), (0,)), ((), ())), preferred_element_type=F32)
     )
-    edge_scale = 1.0 / math.sqrt((ecount + ucount) * devices)
-    node_scale = 1.0 / math.sqrt(n * devices + ccount)
-    in_end = ccount + 3 * lat
+    grad_node_in = node_total[: 2 * lat].astype(F32) * node_scale
+    grad_node_out = node_total[2 * lat : 2 * lat + width].astype(F32) * node_scale
     return (
         grad_nodes,
-        edge_total[:ccount].astype(F32),
+        grad_coarse,
         grad_e,
         grad_u,
-        edge_total[ccount:in_end].astype(F32) * edge_scale,
-        edge_total[in_end : in_end + width].astype(F32) * edge_scale,
+        grad_edge_in,
+        grad_edge_out,
         gains[0] * edge_scale,
-        node_total[: 2 * lat].astype(F32) * node_scale,
-        node_total[2 * lat : 2 * lat + width].astype(F32) * node_scale,
+        grad_node_in,
+        grad_node_out,
         gains[1] * node_scale,
     )
 

time: 229 us -> 237 us (1.035)
  local copies, waits for them, and re-layouts: 13.1 us -> 54.1 us
  Pallas kernels: 64.7 us -> 39 us
  other arithmetic: 16.8 us -> 11.9 us
  waiting for transfers between devices: 66.6 us -> 64.1 us
    unnamed x27 -> x141, local copies, waits for them, and re-layouts: 5.27 us -> 49.6 us
    ppermute x14, waiting for transfers between devices: 38.4 us -> 31.5 us  [exchange(): return lax.ppermute(x, EVERYONE, [(i, i ^ mask) for i in range(devices)])]
    pallas_call x4, Pallas kernels: 7.56 us -> 3.15 us  [halving_sum(): pl.pallas_call(fold_split_kernel, in_specs=[pl.BlockSpec(memory_space=plt...]
    pallas_call x1, Pallas kernels: 9.37 us -> 5.47 us  [per_device(): pl.pallas_call(edge_product_kernel, grid=(steps,), in_specs=[index_spec,...]
    pallas_call x2, Pallas kernels: 5.81 us -> 1.98 us  [reduce_with_tail(): pl.pallas_call(kernel, out_shape=jax.ShapeDtypeStruct((count, part + TAIL...]
    pallas_call x0 -> x2, Pallas kernels: none -> 3.62 us  [the longest x1 1.81 us: per_device(): pl.pallas_call(functools.partial(widen_other_kernel, scale=edge_scale), g...]
    pallas_call x1, Pallas kernels: 10.2 us -> 6.86 us  [per_device(): pl.pallas_call(edge_forward_kernel, grid=(steps,), in_specs=[index_spec,...]
    mul x4 -> x2, other arithmetic: 5.96 us -> 2.73 us  [the longest x1 1.62 us: per_device(): grad_node_in = node_total[:2 * lat].astype(F32) * node_scale]
  transfers between devices with their start and end apart: 23 -> 23, of which waited for: 10 -> 11; matrix products, arithmetic and copies ran while one was open for 7% -> 6% of each run, Pallas kernels for 19% -> 11%
where the time goes in v1:
time: 237 us; the launch traced here: 235 us
  waiting for transfers between devices  64.1 us (27%)
  local copies, waits for them, and re-layouts  54.1 us (23%)
  starting transfers between devices  50.2 us (21%)
  Pallas kernels  39 us (16%)
  blocking collectives  12 us (5%)
  other arithmetic  11.9 us (5%)
  matrix products  2.56 us (1%)
    unnamed x141, local copies, waits for them, and re-layouts  49.6 us
    ppermute x14, waiting for transfers between devices, exchange(): return lax.ppermute(x, EVERYONE, [(i, i ^ mask) for i in range(devices)])  31.5 us
    all_to_all x8, starting transfers between devices, swap(): return lax.all_to_all(x, axes, 0, 0, tiled=True)  30 us
    all_to_all x8, waiting for transfers between devices, swap(): return lax.all_to_all(x, axes, 0, 0, tiled=True)  24.5 us
    ppermute x14, starting transfers between devices, exchange(): return lax.ppermute(x, EVERYONE, [(i, i ^ mask) for i in range(devices)])  13.2 us
    all_to_all x1, blocking collectives, per_device(): lax.all_to_all(returning.reshape(devices, slots, lat), EVERYONE, 0, 0, ti...  12 us
    all_to_all x1, waiting for transfers between devices, per_device(): lax.all_to_all(outgoing.reshape(devices, slots, lat), EVERYONE, 0, 0, til...  8.09 us
    all_to_all x1, starting transfers between devices, per_device(): lax.all_to_all(outgoing.reshape(devices, slots, lat), EVERYONE, 0, 0, til...  6.95 us
  transfers between devices with their start and end apart: 23, of which 11 were waited for; matrix products, arithmetic and copies ran while one was open for 6% of the time, Pallas kernels for 11%

profile of v1, /device:TPU:0, one launch (start us, length us, event | category | flops | bytes accessed | tf_op | source)
XLA Modules:
  0.0 235.1 jit_solution(7966325370271285120)
XLA Ops:
  14.9 6.9 %all-to-all-start = ((bf16[32,4,512]{2,1,0:T(4,128)(2,1)}), bf16[32,4,512]{2,1,0:T(4,128)(2,1)S(1)}, u32[]{:S(2)}, u32[]{:S(2)}) async-start(bf16[32,4,512]{2,1,0:T(4,128)(2,1)} %reshape.129), calls=%async_computation | async-start | bytes 262144 | tf_op jit(solution)/shard_map/all_to_all | solution.py:473
  21.9 8.1 %all-to-all-done = bf16[32,4,512]{2,1,0:T(4,128)(2,1)S(1)} async-done(((bf16[32,4,512]{2,1,0:T(4,128)(2,1)}), bf16[32,4,512]{2,1,0:T(4,128)(2,1)S(1)}, u32[]{:S(2)}, u32[]{:S(2)}) %all-to-all-start) | async-done | bytes 131104 | tf_op jit(solution)/shard_map/all_to_all | solution.py:473
  32.0 3.5 %all-to-all-start.1 = ((bf16[4,128,512]{2,1,0:T(8,128)(2,1)}), bf16[4,128,512]{2,1,0:T(8,128)(2,1)S(1)}, u32[]{:S(2)}, u32[]{:S(2)}) async-start(bf16[4,128,512]{2,1,0:T(8,128)(2,1)} %bitcast.44), calls=%async_computation.1 | async-start | bytes 1048576 | tf_op jit(solution)/shard_map/all_to_all | solution.py:346
  39.2 6.9 %edge_forward.1 = (f32[1024,512]{1,0:T(8,128)S(1)}, bf16[1024,512]{1,0:T(8,128)(2,1)S(1)}, bf16[256,512]{1,0:T(8,128)(2,1)S(1)}) custom-call(s32[1,1024]{1,0:T(1,128)S(1)} %bitcast.29, s32[1,1024]{1,0:T(1,128)S(1)} %bitcast.31, bf16[1024,512]{1,0:T(8,128)(2,1)S(1)} %copy-done.17, bf16[256,512]{1,0:T(8,128)(2,1)S(1)} %copy-done.6, ...), custom_call_target="tpu_custom_call" | custom-call | flops 9900000256 | bytes 27000000 | tf_op jit(solution)/shard_map/edge_forward/pallas_call | solution.py:497
  49.8 3.3 %all-to-all-start.2 = ((bf16[4,32,512]{2,1,0:T(8,128)(2,1)}), bf16[4,32,512]{2,1,0:T(8,128)(2,1)S(1)}, u32[]{:S(2)}, u32[]{:S(2)}) async-start(bf16[4,32,512]{2,1,0:T(8,128)(2,1)} %bitcast.9), calls=%async_computation.2 | async-start | bytes 262144 | tf_op jit(solution)/shard_map/all_to_all | solution.py:346
  68.6 5.0 %all-to-all-start.3 = ((bf16[4,32,512]{2,1,0:T(8,128)(2,1)}), bf16[4,32,512]{2,1,0:T(8,128)(2,1)S(1)}, u32[]{:S(2)}, u32[]{:S(2)}) async-start(bf16[4,32,512]{2,1,0:T(8,128)(2,1)} %broadcast_in_dim.12), calls=%async_computation.3 | async-start | bytes 262144 | tf_op jit(solution)/shard_map/all_to_all | solution.py:346
  73.7 6.0 %all-to-all-done.3 = bf16[4,32,512]{2,1,0:T(8,128)(2,1)S(1)} async-done(((bf16[4,32,512]{2,1,0:T(8,128)(2,1)}), bf16[4,32,512]{2,1,0:T(8,128)(2,1)S(1)}, u32[]{:S(2)}, u32[]{:S(2)}) %all-to-all-start.3) | async-done | bytes 131104 | tf_op jit(solution)/shard_map/all_to_all | solution.py:346
  80.5 4.1 %all-to-all-start.4 = ((bf16[4,128,512]{2,1,0:T(8,128)(2,1)}), bf16[4,128,512]{2,1,0:T(8,128)(2,1)S(1)}, u32[]{:S(2)}, u32[]{:S(2)}) async-start(bf16[4,128,512]{2,1,0:T(8,128)(2,1)} %broadcast_in_dim.14), calls=%async_computation.4 | async-start | bytes 1048576 | tf_op jit(solution)/shard_map/all_to_all | solution.py:346
  91.0 6.5 %edge_cotangent.1 = (f32[1024,512]{1,0:T(8,128)}, bf16[1024,512]{1,0:T(8,128)(2,1)S(1)}, bf16[512,512]{1,0:T(8,128)(2,1)S(1)}, f32[1,512]{1,0:T(1,128)S(1)}) custom-call(s32[1,1024]{1,0:T(1,128)S(1)} %bitcast.32, bf16[1024,512]{1,0:T(8,128)(2,1)S(1)} %copy-done.18, f32[1024,512]{1,0:T(8,128)S(1)} %copy-done.49, bf16[1024,512]{1,0:T(8,128)(2,1)S(1)} %copy-done.16, ...), custom_call_target="tpu_custom_call" | custom-call | flops 8800000000 | bytes 24000000 | tf_op jit(solution)/shard_map/edge_cotangent/pallas_call | solution.py:521
  104.4 5.5 %edge_product.1 = (bf16[1536,512]{1,0:T(8,128)(2,1)S(1)}, f32[256,512]{1,0:T(8,128)S(1)}, bf16[128,512]{1,0:T(8,128)(2,1)S(1)}, bf16[1024,512]{1,0:T(8,128)(2,1)S(1)}) custom-call(s32[1,1024]{1,0:T(1,128)S(1)} %bitcast.30, s32[1,1024]{1,0:T(1,128)S(1)} %bitcast.33, bf16[1024,512]{1,0:T(8,128)(2,1)S(1)} %copy-done.19, bf16[1024,512]{1,0:T(8,128)(2,1)S(1)} %copy-done.59, ...), custom_call_target="tpu_custom_call" | custom-call | flops 9900000256 | bytes 27000000 | tf_op jit(solution)/shard_map/edge_product/pallas_call | solution.py:542
  110.8 5.0 %up_backward.1 = (f32[256,512]{1,0:T(8,128)}, f32[256,512]{1,0:T(8,128)S(1)}, bf16[1552,512]{1,0:T(8,128)(2,1)S(1)}, bf16[1552,512]{1,0:T(8,128)(2,1)}) custom-call(s32[1,256]{1,0:T(1,128)S(1)} %bitcast.41, s32[1,256]{1,0:T(1,128)S(1)} %bitcast.43, s32[2]{0:T(128)S(1)} %pad_add_fusion.place, bf16[256,512]{1,0:T(8,128)(2,1)S(1)} %copy-done.29, ...), custom_call_target="tpu_custom_call" | custom-call | flops 8800000000 | bytes 24000000 | tf_op jit(solution)/shard_map/up_backward/pallas_call | solution.py:593
  118.3 12.0 %all_to_all.68 = bf16[32,4,512]{2,1,0:T(4,128)(2,1)S(1)} all-to-all(bf16[32,4,512]{2,1,0:T(4,128)(2,1)S(1)} %reshape.135), channel_id=1, replica_groups=mesh['z'=4,'x'=2,'y'=2,'core'=2] {'z','x','y','core'}, dimensions={0} | all-to-all | bytes 262144 | tf_op jit(solution)/shard_map/all_to_all | solution.py:566
  134.7 3.6 %all-to-all-start.6 = ((bf16[4,400,512]{2,1,0:T(8,128)(2,1)}), bf16[4,400,512]{2,1,0:T(8,128)(2,1)S(1)}, u32[]{:S(2)}, u32[]{:S(2)}) async-start(bf16[4,400,512]{2,1,0:T(8,128)(2,1)} %copy-done.1), calls=%async_computation.6 | async-start | bytes 3276800 | tf_op jit(solution)/shard_map/all_to_all | solution.py:346
  145.5 13.4 %all-to-all-done.6.got = bf16[4,400,512]{2,1,0:T(8,128)(2,1)S(1)} async-done(((bf16[4,400,512]{2,1,0:T(8,128)(2,1)}), bf16[4,400,512]{2,1,0:T(8,128)(2,1)S(1)}, u32[]{:S(2)}, u32[]{:S(2)}) %all-to-all-start.6) | async-done | bytes 1638432 | tf_op jit(solution)/shard_map/all_to_all | solution.py:346
  159.8 3.5 %all-to-all-start.7 = ((bf16[4,112,512]{2,1,0:T(8,128)(2,1)}), bf16[4,112,512]{2,1,0:T(8,128)(2,1)S(1)}, u32[]{:S(2)}, u32[]{:S(2)}) async-start(bf16[4,112,512]{2,1,0:T(8,128)(2,1)} %copy-done.4), calls=%async_computation.7 | async-start | bytes 917504 | tf_op jit(solution)/shard_map/all_to_all | solution.py:346
  166.9 5.1 %collective-permute-done.6.recv = bf16[192,512]{1,0:T(8,128)(2,1)S(1)} collective-permute-done((bf16[192,512]{1,0:T(8,128)(2,1)S(1)}, bf16[192,512]{1,0:T(8,128)(2,1)S(1)}, u32[]{:S(2)}, u32[]{:S(2)}) %collective-permute-start.6) | collective-permute-done | bytes 196640 | tf_op jit(solution)/shard_map/ppermute | solution.py:363
  173.2 3.5 %collective-permute-done.7.recv = bf16[96,512]{1,0:T(8,128)(2,1)S(1)} collective-permute-done((bf16[96,512]{1,0:T(8,128)(2,1)S(1)}, bf16[96,512]{1,0:T(8,128)(2,1)S(1)}, u32[]{:S(2)}, u32[]{:S(2)}) %collective-permute-start.7) | collective-permute-done | bytes 98336 | tf_op jit(solution)/shard_map/ppermute | solution.py:363
  180.3 3.5 %all-to-all-start.8 = ((bf16[4,96,512]{2,1,0:T(8,128)(2,1)}), bf16[4,96,512]{2,1,0:T(8,128)(2,1)S(1)}, u32[]{:S(2)}, u32[]{:S(2)}) async-start(bf16[4,96,512]{2,1,0:T(8,128)(2,1)} %broadcast_in_dim.15), calls=%async_computation.8 | async-start | bytes 786432 | tf_op jit(solution)/shard_map/all_to_all | solution.py:346
  183.8 2.9 %collective-permute-start.9 = (bf16[48,512]{1,0:T(8,128)(2,1)S(1)}, bf16[48,512]{1,0:T(8,128)(2,1)S(1)}, u32[]{:S(2)}, u32[]{:S(2)}) collective-permute-start(bf16[48,512]{1,0:T(8,128)(2,1)S(1)} %add_convert_fusion.1), channel_id=1, source_target_pairs={{0,16},{1,17},{2,18},{3,19},{4,20},{5,21},{6,22},{7,23},{8,24},{9,... | collective-permute-start | bytes 147464 | tf_op jit(solution)/shard_map/ppermute | solution.py:363
  186.7 8.4 %collective-permute-done.9 = bf16[48,512]{1,0:T(8,128)(2,1)S(1)} collective-permute-done((bf16[48,512]{1,0:T(8,128)(2,1)S(1)}, bf16[48,512]{1,0:T(8,128)(2,1)S(1)}, u32[]{:S(2)}, u32[]{:S(2)}) %collective-permute-start.9) | collective-permute-done | bytes 49184 | tf_op jit(solution)/shard_map/ppermute | solution.py:363
  195.9 3.9 %collective-permute-done.10 = bf16[96,512]{1,0:T(8,128)(2,1)S(1)} collective-permute-done((bf16[96,512]{1,0:T(8,128)(2,1)S(1)}, bf16[96,512]{1,0:T(8,128)(2,1)S(1)}, u32[]{:S(2)}, u32[]{:S(2)}) %collective-permute-start.10) | collective-permute-done | bytes 98336 | tf_op jit(solution)/shard_map/ppermute | solution.py:363
  203.2 3.6 %all-to-all-start.9 = ((bf16[4,384,512]{2,1,0:T(8,128)(2,1)}), bf16[4,384,512]{2,1,0:T(8,128)(2,1)S(1)}, u32[]{:S(2)}, u32[]{:S(2)}) async-start(bf16[4,384,512]{2,1,0:T(8,128)(2,1)} %broadcast_in_dim.34), calls=%async_computation.9 | async-start | bytes 3145728 | tf_op jit(solution)/shard_map/all_to_all | solution.py:346
  208.5 7.8 %collective-permute-done.12 = bf16[384,512]{1,0:T(8,128)(2,1)S(1)} collective-permute-done((bf16[384,512]{1,0:T(8,128)(2,1)S(1)}, bf16[384,512]{1,0:T(8,128)(2,1)S(1)}, u32[]{:S(2)}, u32[]{:S(2)}) %collective-permute-start.12) | collective-permute-done | bytes 393248 | tf_op jit(solution)/shard_map/ppermute | solution.py:363
  217.5 5.1 %all-to-all-done.9 = bf16[4,384,512]{2,1,0:T(8,128)(2,1)S(1)} async-done(((bf16[4,384,512]{2,1,0:T(8,128)(2,1)}), bf16[4,384,512]{2,1,0:T(8,128)(2,1)S(1)}, u32[]{:S(2)}, u32[]{:S(2)}) %all-to-all-start.9) | async-done | bytes 1572896 | tf_op jit(solution)/shard_map/all_to_all | solution.py:346
  (207 shorter events, 96.9 us)
Async XLA Ops:
  0.6 21.2 %copy-start = (bf16[1024,512]{1,0:T(8,128)(2,1)S(1)}, bf16[1024,512]{1,0:T(8,128)(2,1)}, u32[]{:S(2)}) copy-start(bf16[1024,512]{1,0:T(8,128)(2,1)} %param.30) | copy-start | bytes 3145732
  13.2 16.8 %collective-permute-start = (bf16[512,512]{1,0:T(8,128)(2,1)}, bf16[512,512]{1,0:T(8,128)(2,1)}, u32[]{:S(2)}, u32[]{:S(2)}) collective-permute-start(bf16[512,512]{1,0:T(8,128)(2,1)} %get-tuple-element.67), channel_id=1, source_target_pairs={{0,1},{1,0},{2,3},{3,2},{4,5},{5,4},{6,7},{7,6},{8,9},{9,8},{10,11... | collective-permute-start | bytes 1572872 | tf_op jit(solution)/shard_map/ppermute | solution.py:363
  14.9 15.2 %all-to-all-start = ((bf16[32,4,512]{2,1,0:T(4,128)(2,1)}), bf16[32,4,512]{2,1,0:T(4,128)(2,1)S(1)}, u32[]{:S(2)}, u32[]{:S(2)}) async-start(bf16[32,4,512]{2,1,0:T(4,128)(2,1)} %reshape.129), calls=%async_computation | async-start | bytes 262144 | tf_op jit(solution)/shard_map/all_to_all | solution.py:473
  32.0 17.1 %all-to-all-start.1 = ((bf16[4,128,512]{2,1,0:T(8,128)(2,1)}), bf16[4,128,512]{2,1,0:T(8,128)(2,1)S(1)}, u32[]{:S(2)}, u32[]{:S(2)}) async-start(bf16[4,128,512]{2,1,0:T(8,128)(2,1)} %bitcast.44), calls=%async_computation.1 | async-start | bytes 1048576 | tf_op jit(solution)/shard_map/all_to_all | solution.py:346
  49.8 11.1 %all-to-all-start.2 = ((bf16[4,32,512]{2,1,0:T(8,128)(2,1)}), bf16[4,32,512]{2,1,0:T(8,128)(2,1)S(1)}, u32[]{:S(2)}, u32[]{:S(2)}) async-start(bf16[4,32,512]{2,1,0:T(8,128)(2,1)} %bitcast.9), calls=%async_computation.2 | async-start | bytes 262144 | tf_op jit(solution)/shard_map/all_to_all | solution.py:346
  68.6 11.1 %all-to-all-start.3 = ((bf16[4,32,512]{2,1,0:T(8,128)(2,1)}), bf16[4,32,512]{2,1,0:T(8,128)(2,1)S(1)}, u32[]{:S(2)}, u32[]{:S(2)}) async-start(bf16[4,32,512]{2,1,0:T(8,128)(2,1)} %broadcast_in_dim.12), calls=%async_computation.3 | async-start | bytes 262144 | tf_op jit(solution)/shard_map/all_to_all | solution.py:346
  80.5 18.7 %all-to-all-start.4 = ((bf16[4,128,512]{2,1,0:T(8,128)(2,1)}), bf16[4,128,512]{2,1,0:T(8,128)(2,1)S(1)}, u32[]{:S(2)}, u32[]{:S(2)}) async-start(bf16[4,128,512]{2,1,0:T(8,128)(2,1)} %broadcast_in_dim.14), calls=%async_computation.4 | async-start | bytes 1048576 | tf_op jit(solution)/shard_map/all_to_all | solution.py:346
  99.2 11.4 %collective-permute-start.1 = (bf16[512,512]{1,0:T(8,128)(2,1)S(1)}, bf16[512,512]{1,0:T(8,128)(2,1)S(1)}, u32[]{:S(2)}, u32[]{:S(2)}) collective-permute-start(bf16[512,512]{1,0:T(8,128)(2,1)S(1)} %bitcast.27), channel_id=1, source_target_pairs={{0,1},{1,0},{2,3},{3,2},{4,5},{5,4},{6,7},{7,6},{8,9},{9,8},{10,11... | collective-permute-start | bytes 1572872 | tf_op jit(solution)/shard_map/ppermute | solution.py:363
  117.7 12.6 %collective-permute-start.2 = (bf16[1552,512]{1,0:T(8,128)(2,1)}, bf16[1552,512]{1,0:T(8,128)(2,1)}, u32[]{:S(2)}, u32[]{:S(2)}) collective-permute-start(bf16[1552,512]{1,0:T(8,128)(2,1)} %get-tuple-element.79), channel_id=1, source_target_pairs={{0,1},{1,0},{2,3},{3,2},{4,5},{5,4},{6,7},{7,6},{8,9},{9,8},{10,11... | collective-permute-start | bytes 4767752 | tf_op jit(solution)/shard_map/ppermute | solution.py:363
  134.7 24.2 %all-to-all-start.6 = ((bf16[4,400,512]{2,1,0:T(8,128)(2,1)}), bf16[4,400,512]{2,1,0:T(8,128)(2,1)S(1)}, u32[]{:S(2)}, u32[]{:S(2)}) async-start(bf16[4,400,512]{2,1,0:T(8,128)(2,1)} %copy-done.1), calls=%async_computation.6 | async-start | bytes 3276800 | tf_op jit(solution)/shard_map/all_to_all | solution.py:346
  138.2 2.7 %collective-permute-start.4 = (bf16[768,512]{1,0:T(8,128)(2,1)}, bf16[768,512]{1,0:T(8,128)(2,1)}, u32[]{:S(2)}, u32[]{:S(2)}) collective-permute-start(bf16[768,512]{1,0:T(8,128)(2,1)} %copy-done.20), channel_id=1, source_target_pairs={{0,1},{1,0},{2,3},{3,2},{4,5},{5,4},{6,7},{7,6},{8,9},{9,8},{10,11... | collective-permute-start | bytes 2359304 | tf_op jit(solution)/shard_map/ppermute | solution.py:363
  144.8 18.5 %collective-permute-start.5 = (bf16[384,512]{1,0:T(8,128)(2,1)}, bf16[384,512]{1,0:T(8,128)(2,1)}, u32[]{:S(2)}, u32[]{:S(2)}) collective-permute-start(bf16[384,512]{1,0:T(8,128)(2,1)} %get-tuple-element.95), channel_id=1, source_target_pairs={{0,8},{1,9},{2,10},{3,11},{4,12},{5,13},{6,14},{7,15},{8,0},{9,1},... | collective-permute-start | bytes 1179656 | tf_op jit(solution)/shard_map/ppermute | solution.py:363
  159.8 19.6 %all-to-all-start.7 = ((bf16[4,112,512]{2,1,0:T(8,128)(2,1)}), bf16[4,112,512]{2,1,0:T(8,128)(2,1)S(1)}, u32[]{:S(2)}, u32[]{:S(2)}) async-start(bf16[4,112,512]{2,1,0:T(8,128)(2,1)} %copy-done.4), calls=%async_computation.7 | async-start | bytes 917504 | tf_op jit(solution)/shard_map/all_to_all | solution.py:346
  165.4 6.6 %collective-permute-start.6 = (bf16[192,512]{1,0:T(8,128)(2,1)S(1)}, bf16[192,512]{1,0:T(8,128)(2,1)S(1)}, u32[]{:S(2)}, u32[]{:S(2)}) collective-permute-start(bf16[192,512]{1,0:T(8,128)(2,1)S(1)} %get-tuple-element.97), channel_id=1, source_target_pairs={{0,4},{1,5},{2,6},{3,7},{4,0},{5,1},{6,2},{7,3},{8,12},{9,13},{10,... | collective-permute-start | bytes 589832 | tf_op jit(solution)/shard_map/ppermute | solution.py:363
  172.0 4.7 %collective-permute-start.7 = (bf16[96,512]{1,0:T(8,128)(2,1)S(1)}, bf16[96,512]{1,0:T(8,128)(2,1)S(1)}, u32[]{:S(2)}, u32[]{:S(2)}) collective-permute-start(bf16[96,512]{1,0:T(8,128)(2,1)S(1)} %get-tuple-element.99), channel_id=1, source_target_pairs={{0,2},{1,3},{2,0},{3,1},{4,6},{5,7},{6,4},{7,5},{8,10},{9,11},{10,... | collective-permute-start | bytes 294920 | tf_op jit(solution)/shard_map/ppermute | solution.py:363
  176.7 7.0 %collective-permute-start.8 = (bf16[48,512]{1,0:T(8,128)(2,1)S(1)}, bf16[48,512]{1,0:T(8,128)(2,1)S(1)}, u32[]{:S(2)}, u32[]{:S(2)}) collective-permute-start(bf16[48,512]{1,0:T(8,128)(2,1)S(1)} %get-tuple-element.101), channel_id=1, source_target_pairs={{0,16},{1,17},{2,18},{3,19},{4,20},{5,21},{6,22},{7,23},{8,24},{9,... | collective-permute-start | bytes 147464 | tf_op jit(solution)/shard_map/ppermute | solution.py:363
  180.3 21.7 %all-to-all-start.8 = ((bf16[4,96,512]{2,1,0:T(8,128)(2,1)}), bf16[4,96,512]{2,1,0:T(8,128)(2,1)S(1)}, u32[]{:S(2)}, u32[]{:S(2)}) async-start(bf16[4,96,512]{2,1,0:T(8,128)(2,1)} %broadcast_in_dim.15), calls=%async_computation.8 | async-start | bytes 786432 | tf_op jit(solution)/shard_map/all_to_all | solution.py:346
  183.8 11.3 %collective-permute-start.9 = (bf16[48,512]{1,0:T(8,128)(2,1)S(1)}, bf16[48,512]{1,0:T(8,128)(2,1)S(1)}, u32[]{:S(2)}, u32[]{:S(2)}) collective-permute-start(bf16[48,512]{1,0:T(8,128)(2,1)S(1)} %add_convert_fusion.1), channel_id=1, source_target_pairs={{0,16},{1,17},{2,18},{3,19},{4,20},{5,21},{6,22},{7,23},{8,24},{9,... | collective-permute-start | bytes 147464 | tf_op jit(solution)/shard_map/ppermute | solution.py:363
  195.1 4.7 %collective-permute-start.10 = (bf16[96,512]{1,0:T(8,128)(2,1)S(1)}, bf16[96,512]{1,0:T(8,128)(2,1)S(1)}, u32[]{:S(2)}, u32[]{:S(2)}) collective-permute-start(bf16[96,512]{1,0:T(8,128)(2,1)S(1)} %maximum_select_fusion.4), channel_id=1, source_target_pairs={{0,2},{1,3},{2,0},{3,1},{4,6},{5,7},{6,4},{7,5},{8,10},{9,11},{10,... | collective-permute-start | bytes 294920 | tf_op jit(solution)/shard_map/ppermute | solution.py:363
  199.8 7.4 %collective-permute-start.11 = (bf16[192,512]{1,0:T(8,128)(2,1)S(1)}, bf16[192,512]{1,0:T(8,128)(2,1)}, u32[]{:S(2)}, u32[]{:S(2)}) collective-permute-start(bf16[192,512]{1,0:T(8,128)(2,1)S(1)} %maximum_select_fusion.3), channel_id=1, source_target_pairs={{0,4},{1,5},{2,6},{3,7},{4,0},{5,1},{6,2},{7,3},{8,12},{9,13},{10,... | collective-permute-start | bytes 589832 | tf_op jit(solution)/shard_map/ppermute | solution.py:363
  203.2 19.3 %all-to-all-start.9 = ((bf16[4,384,512]{2,1,0:T(8,128)(2,1)}), bf16[4,384,512]{2,1,0:T(8,128)(2,1)S(1)}, u32[]{:S(2)}, u32[]{:S(2)}) async-start(bf16[4,384,512]{2,1,0:T(8,128)(2,1)} %broadcast_in_dim.34), calls=%async_computation.9 | async-start | bytes 3145728 | tf_op jit(solution)/shard_map/all_to_all | solution.py:346
  208.4 7.8 %collective-permute-start.12 = (bf16[384,512]{1,0:T(8,128)(2,1)S(1)}, bf16[384,512]{1,0:T(8,128)(2,1)S(1)}, u32[]{:S(2)}, u32[]{:S(2)}) collective-permute-start(bf16[384,512]{1,0:T(8,128)(2,1)S(1)} %maximum_select_fusion.2), channel_id=1, source_target_pairs={{0,8},{1,9},{2,10},{3,11},{4,12},{5,13},{6,14},{7,15},{8,0},{9,1},... | collective-permute-start | bytes 1179656 | tf_op jit(solution)/shard_map/ppermute | solution.py:363
  217.5 7.4 %collective-permute-start.13 = (bf16[768,512]{1,0:T(8,128)(2,1)}, bf16[768,512]{1,0:T(8,128)(2,1)}, u32[]{:S(2)}, u32[]{:S(2)}) collective-permute-start(bf16[768,512]{1,0:T(8,128)(2,1)} %maximum_select_fusion.1), channel_id=1, source_target_pairs={{0,1},{1,0},{2,3},{3,2},{4,5},{5,4},{6,7},{7,6},{8,9},{9,8},{10,11... | collective-permute-start | bytes 2359304 | tf_op jit(solution)/shard_map/ppermute | solution.py:363
  222.5 10.8 %collective-permute-start.3 = (bf16[1536,512]{1,0:T(8,128)(2,1)S(1)}, bf16[1536,512]{1,0:T(8,128)(2,1)S(1)}, u32[]{:S(2)}, u32[]{:S(2)}) collective-permute-start(bf16[1536,512]{1,0:T(8,128)(2,1)S(1)} %bitcast.25), channel_id=1, source_target_pairs={{0,1},{1,0},{2,3},{3,2},{4,5},{5,4},{6,7},{7,6},{8,9},{9,8},{10,11... | collective-permute-start | bytes 4718600 | tf_op jit(solution)/shard_map/ppermute | solution.py:363
  (69 other events, 228.7 us)

commit v2 on v1

--- a/solution.py
+++ b/solution.py
@@ -108,13 +108,22 @@
 
 
 def up_forward_kernel(
-    us, ur, core, up, node, coarse, w1, w2, gain, p_ref, xs_ref, xr_ref, keep_ref, send_ref, part
+    us, ur, core, up, gain, node_far, coarse_far, w1_far, w2_far,
+    p_ref, xs_ref, xr_ref, keep_ref, send_ref, part, node, coarse, w1, w2, sems,
 ):
+    loads = loads_of((node_far, coarse_far, w1_far, w2_far), (node, coarse, w1, w2), sems)
+    for load in loads:
+        load.start()
     lat = up.shape[1]
-    xs = dot_lt(onehot_t(us[...], node.shape[0]), node[...]).astype(BF)
+    hot_s = onehot_t(us[...], node.shape[0])
     hot_r = onehot_t(ur[...], coarse.shape[0])
+    loads[0].wait()
+    xs = dot_lt(hot_s, node[...]).astype(BF)
+    loads[1].wait()
     xr = dot_lt(hot_r, coarse[...]).astype(BF)
+    loads[2].wait()
     pre = dot(up[...], w1[0:lat]) + dot(xs, w1[lat : 2 * lat]) + dot(xr, w1[2 * lat :])
+    loads[3].wait()
     normed, _ = normalise(dot(hidden_of(pre), w2[...]))
     new = (up[...].astype(F32) + normed * gain[...]).astype(BF)
     p_ref[...] = pre
@@ -125,16 +134,22 @@
 
 
 def edge_forward_kernel(
-    es, er, edge, node, halo, coarse, w1, w2, gain, p_ref, xs_ref, total_ref, acc
+    es, er, edge, halo, gain, node_far, coarse_far, w1_far, w2_far, p_ref, xs_ref, total_ref,
+    acc, node, coarse, w1, w2, sems,
 ):
     step = pl.program_id(0)
     lat = edge.shape[1]
     n = node.shape[0]
     imports = halo.shape[0]
+    loads = loads_of((node_far, coarse_far, w1_far, w2_far), (node, coarse, w1, w2), sems)
 
     @pl.when(step == 0)
     def _():
+        for load in loads:
+            load.start()
         acc[...] = jnp.zeros_like(acc)
+        for load in loads[:3]:
+            load.wait()
 
     sender = es[...]
     xs = (
@@ -145,9 +160,14 @@
     hot_r = onehot_t(er[...], n)
     xr = dot_lt(hot_r, node[...]).astype(BF)
     pre = dot(edge[...], w1[0:lat]) + dot(xs, w1[lat : 2 * lat]) + dot(xr, w1[2 * lat :])
+    p_ref[...] = pre
+
+    @pl.when(step == 0)
+    def _():
+        loads[3].wait()
+
     normed, _ = normalise(dot(hidden_of(pre), w2[...]))
     new = (edge[...].astype(F32) + normed * gain[...]).astype(BF)
-    p_ref[...] = pre
     xs_ref[...] = xs
     acc[...] += dot(hot_r, new)
 
@@ -157,12 +177,18 @@
 
 
 def node_kernel(
-    node, total_in, nw1, nw2, ngain, ncot, fg_ref, gn_ref, ngw1_ref, ngw2_ref, ngg_ref
+    node, total_in, ngain, ncot, nw1_far, nw2_far, fg_ref, gn_ref, ngw1_ref, ngw2_ref, ngg_ref,
+    nw1, nw2, sems,
 ):
+    loads = loads_of((nw1_far, nw2_far), (nw1, nw2), sems)
+    for load in loads:
+        load.start()
     lat = node.shape[1]
     total = total_in[...]
+    loads[0].wait()
     node_pre = dot(node[...], nw1[0:lat]) + dot(total, nw1[lat:])
     hidden = hidden_of(node_pre)
+    loads[1].wait()
     node_normed, inv_std = normalise(dot(hidden, nw2[...]))
     cot = ncot[...].astype(F32)
     gain_part, d_proj, d_pre = grad_to_pre(
@@ -177,24 +203,34 @@
 
 
 def edge_cotangent_kernel(
-    er, edge, pre_ref, ecot, fg, w1, w2, gain, ge_ref, dp_ref, gw2_out, gg_ref, gw2
+    er, pre_ref, ecot, fg, gain, w1_far, w2_far, ge_ref, dp_ref, gw2_out, gg_ref,
+    gw2, w1, w2, sems,
 ):
     step = pl.program_id(0)
-    lat = edge.shape[1]
+    lat = ecot.shape[1]
+    loads = loads_of((w1_far.at[0:lat], w2_far), (w1, w2), sems)
 
     @pl.when(step == 0)
     def _():
+        for load in loads:
+            load.start()
         gw2[...] = jnp.zeros_like(gw2)
         gg_ref[...] = jnp.zeros_like(gg_ref)
 
     cot = ecot[...].astype(F32) + gather_f32(onehot_t(er[...], fg.shape[0]), fg[...])
     pre = pre_ref[...]
     hidden = hidden_of(pre)
+
+    @pl.when(step == 0)
+    def _():
+        for load in loads:
+            load.wait()
+
     normed, inv_std = normalise(dot(hidden, w2[...]))
     gain_part, d_proj, d_pre = grad_to_pre(pre, normed, inv_std, cot, gain[...], w2[...])
     gg_ref[...] += gain_part
     gw2[...] += dot_lt(hidden, d_proj)
-    ge_ref[...] = cot + dot_rt(d_pre, w1[0:lat])
+    ge_ref[...] = cot + dot_rt(d_pre, w1[...])
     dp_ref[...] = d_pre
 
     @pl.when(step == pl.num_programs(0) - 1)
@@ -203,15 +239,19 @@
 
 
 def edge_product_kernel(
-    es, er, edge, xs, dp, node, w1, gw1_out, np_ref, ret_ref, cp_ref, sum_s, sum_r, gw1
+    es, er, edge, xs, dp, node_far, w1_far, gw1_out, np_ref, ret_ref, cp_ref,
+    sum_s, sum_r, gw1, node, w1, sems,
 ):
     step = pl.program_id(0)
     lat = edge.shape[1]
     n = node.shape[0]
     imports = ret_ref.shape[0]
+    loads = loads_of((node_far, w1_far.at[lat : 3 * lat]), (node, w1), sems)
 
     @pl.when(step == 0)
     def _():
+        for load in loads:
+            load.start()
         sum_s[...] = jnp.zeros_like(sum_s)
         sum_r[...] = jnp.zeros_like(sum_r)
         gw1[...] = jnp.zeros_like(gw1)
@@ -224,29 +264,40 @@
 
     @pl.when(step == pl.num_programs(0) - 1)
     def _():
-        w_s = w1[lat : 2 * lat]
+        for load in loads:
+            load.wait()
+        w_s = w1[0:lat]
         recv = sum_r[...].astype(BF)
         gw1_out[0 : 2 * lat] = gw1[...].astype(BF)
         gw1_out[2 * lat :] = dot_lt(node[...], recv).astype(BF)
-        np_ref[...] = dot_rt(sum_s[0:n].astype(BF), w_s) + dot_rt(recv, w1[2 * lat :])
+        np_ref[...] = dot_rt(sum_s[0:n].astype(BF), w_s) + dot_rt(recv, w1[lat:])
         ret_ref[...] = dot_rt(sum_s[n : n + imports].astype(BF), w_s).astype(BF)
         cp_ref[...] = dot_rt(sum_s[n + imports :].astype(BF), w_s).astype(BF)
 
 
 def coarse_kernel(
-    core, rows, total_in, ccot, nw1, nw2, ngain, ngw1, ngw2, ngg,
-    cg_ref, after_ref, keep_ref, send_ref, gg_ref, pay,
+    core, rows, total_in, ccot, ngain, ngg, nw1_far, nw2_far, ngw1_far, ngw2_far,
+    cg_ref, after_ref, keep_ref, send_ref, gg_ref, pay, nw1, nw2, ngw1, ngw2, sems,
 ):
+    loads = loads_of(
+        (nw1_far, nw2_far, ngw1_far, ngw2_far), (nw1, nw2, ngw1, ngw2), sems
+    )
+    for load in loads:
+        load.start()
     lat = rows.shape[1]
     used = ngw1.shape[0] + ngw2.shape[0]
     total = total_in[...].astype(BF)
+    loads[0].wait()
     pre = dot(rows[...], nw1[0:lat]) + dot(total, nw1[lat:])
     hidden = hidden_of(pre)
+    loads[1].wait()
     normed, inv_std = normalise(dot(hidden, nw2[...]))
     cot = ccot[...].astype(F32)
     gain_part, d_proj, d_pre = grad_to_pre(pre, normed, inv_std, cot, ngain[...], nw2[...])
     cg_ref[...] = dot_rt(d_pre, nw1[lat:]).astype(BF)
     after_ref[...] = cot + dot_rt(d_pre, nw1[0:lat])
+    loads[2].wait()
+    loads[3].wait()
     pay[0:lat] = ngw1[0:lat].astype(F32) + dot_lt(rows[...], d_pre)
     pay[lat : 2 * lat] = ngw1[lat:].astype(F32) + dot_lt(total, d_pre)
     pay[2 * lat : used] = ngw2[...].astype(F32) + dot_lt(hidden, d_proj)
@@ -257,9 +308,15 @@
 
 
 def up_backward_kernel(
-    us, ur, place, up, xs, xr, pre_ref, ucot, cg_own, cg_other, w1, w2, gain, gw1, gw2, gg, ngg,
-    cp, after, gu_ref, np_ref, keep_ref, send_ref, csum, pay,
+    us, ur, place, up, xs, xr, pre_ref, ucot, cg_own, cg_other, gain, gg, ngg, after,
+    w2_far, w1_far, cp_far, gw2_far, gw1_far, gu_ref, np_ref, keep_far, send_far,
+    csum, pay, w2, w1, cp, gw2, gw1, sems, out_sems,
 ):
+    loads = loads_of(
+        (w2_far, w1_far, cp_far, gw2_far, gw1_far), (w2, w1, cp, gw2, gw1), sems
+    )
+    for load in loads:
+        load.start()
     lat = up.shape[1]
     half = cg_own.shape[0]
     coarse = csum.shape[0]
@@ -274,37 +331,70 @@
     )
     pre = pre_ref[...]
     hidden = hidden_of(pre)
+    loads[0].wait()
     normed, inv_std = normalise(dot(hidden, w2[...]))
     gain_part, d_proj, d_pre = grad_to_pre(pre, normed, inv_std, cot, gain[...], w2[...])
+    loads[1].wait()
     gu_ref[...] = cot + dot_rt(d_pre, w1[0:lat])
     send = dot(onehot_t(us[...], np_ref.shape[0]), d_pre).astype(BF)
     np_ref[...] = dot_rt(send, w1[lat : 2 * lat])
+    loads[2].wait()
     csum[...] = cp[...].astype(F32) + dot_rt(dot(hot_r, d_pre).astype(BF), w1[2 * lat :])
     count = after.shape[0]
     mine = pl.ds(pl.multiple_of(place[0] * count, 8), count)
     csum[mine, :] = csum[mine, :] + after[...]
-    rows = pay.shape[0] // 2
-    first = [csum[...]]
-    second = [gw2[...].astype(F32) + dot_lt(hidden, d_proj)]
-    for k, x in enumerate((up, xs, xr)):
-        piece = slice(k * lat, (k + 1) * lat)
-        second.insert(k, gw1[piece].astype(F32) + dot_lt(x[...], d_pre))
-    w1_part = jnp.concatenate(second[:-1], axis=0)
-    for h in range(2):
-        start = h * rows
-        for full in (first[0], w1_part, second[-1]):
-            size = full.shape[0] // 2
-            pay[start : start + size] = full[h * size : (h + 1) * size].astype(BF)
-            start += size
-        if start < (h + 1) * rows:
-            pay[start : (h + 1) * rows] = jnp.zeros(((h + 1) * rows - start, lat), BF)
-    split_rows(pay, core, keep_ref.at[0:rows], send_ref.at[0:rows])
+    rows = pay.shape[0] // 2 - TAIL
+    c_half, h_half, w_half = coarse // 2, gw1.shape[0] // 2, gw2.shape[0] // 2
+
+    def send_piece(start, size):
+        for h in range(2):
+            src = pay.at[pl.ds(h * (rows + TAIL) + start, size)]
+
+            @pl.when(core == h)
+            def _():
+                pltpu.make_async_copy(
+                    src, keep_far.at[pl.ds(start, size)], out_sems.at[0]
+                ).start()
+
+            @pl.when(core != h)
+            def _():
+                pltpu.make_async_copy(
+                    src, send_far.at[pl.ds(start, size)], out_sems.at[1]
+                ).start()
+
+    def put(start, size, full):
+        for h in range(2):
+            at = h * (rows + TAIL) + start
+            pay[at : at + size] = full[h * size : (h + 1) * size].astype(BF)
+
+    put(0, c_half, csum)
+    send_piece(0, c_half)
+    loads[3].wait()
+    put(c_half + h_half, w_half, gw2[...].astype(F32) + dot_lt(hidden, d_proj))
+    send_piece(c_half + h_half, w_half)
+    loads[4].wait()
+    w1_part = jnp.concatenate(
+        [
+            gw1[k * lat : (k + 1) * lat].astype(F32) + dot_lt(x[...], d_pre)
+            for k, x in enumerate((up, xs, xr))
+        ],
+        axis=0,
+    )
+    put(c_half, h_half, w1_part)
+    send_piece(c_half, h_half)
+    used = c_half + h_half + w_half
     ids = lax.broadcasted_iota(jnp.int32, (TAIL, lat), 0)
     edge_row = jnp.broadcast_to(gg[...] + gain_part, (TAIL, lat))
     node_row = jnp.broadcast_to(ngg[...], (TAIL, lat))
     tail = jnp.where(ids == 0, edge_row, jnp.where(ids == 1, node_row, 0.0)).astype(BF)
-    keep_ref[rows:] = tail
-    send_ref[rows:] = tail
+    for h in range(2):
+        at = h * (rows + TAIL)
+        if used < rows:
+            pay[at + used : at + rows] = jnp.zeros((rows - used, lat), BF)
+        pay[at + rows : at + rows + TAIL] = tail
+    send_piece(used, rows + TAIL - used)
+    for k, out_far in enumerate((keep_far, send_far)):
+        pltpu.make_async_copy(pay.at[pl.ds(0, rows + TAIL)], out_far, out_sems.at[k]).wait()
 
 
 def widen_kernel(core, half, coarse_ref, first_ref, second_ref, *, scale):
@@ -336,8 +426,30 @@
     return jax.ShapeDtypeStruct((rows, cols), dtype)
 
 
-def whole(arr):
-    return pl.BlockSpec(arr.shape, lambda i: (0,) * len(arr.shape))
+def far(rows, cols, dtype):
+    return pltpu.HBM((rows, cols), dtype)
+
+
+def in_far(*arrays):
+    return [pltpu.with_memory_space_constraint(a, pltpu.HBM) for a in arrays]
+
+
+IN_VMEM = pl.BlockSpec(memory_space=pltpu.VMEM)
+IN_SMEM = pl.BlockSpec(memory_space=pltpu.SMEM)
+IN_HBM = pl.BlockSpec(memory_space=pl.ANY)
+
+
+def loads_of(sources, targets, sems):
+    return [
+        pltpu.make_async_copy(src, dst, sems.at[k])
+        for k, (src, dst) in enumerate(zip(sources, targets))
+    ]
+
+
+def buffers(*arrays):
+    return [pltpu.VMEM(a.shape, a.dtype) for a in arrays] + [
+        pltpu.SemaphoreType.DMA((len(arrays),))
+    ]
 
 
 def swap(x, axes, count):
@@ -391,13 +503,13 @@
     rows = keep.shape[0] - TAIL
     got = exchange(send, 1)
     got, wait_for = lax.optimization_barrier((got, wait_for))
-    x = (keep, got)
+    x = (*in_far(keep), got)
     for axes, kernel in zip(GROUPS[1:], (fold_pair_kernel, fold_group_kernel)):
         count = lax.axis_size(axes)
         part = rows // count
         x = pl.pallas_call(
             kernel,
-            out_shape=jax.ShapeDtypeStruct((count, part + TAIL, cols), BF),
+            out_shape=pltpu.HBM((count, part + TAIL, cols), BF),
             compiler_params=params(),
             cost_estimate=cost(3.0),
         )(*x)
@@ -429,11 +541,11 @@
             fold_split_kernel,
             in_specs=[pl.BlockSpec(memory_space=pltpu.SMEM)]
             + [pl.BlockSpec(memory_space=pltpu.VMEM)] * 2,
-            out_shape=(shape(rows // 2, cols, BF),) * 2,
+            out_shape=(far(rows // 2, cols, BF), shape(rows // 2, cols, BF)),
             compiler_params=params(),
             cost_estimate=cost(1.0),
             name="fold_split",
-        )(bit, keep, got)
+        )(bit, *in_far(keep), got)
     got = exchange(send, masks[-1])
     x = (keep.astype(F32) + got.astype(F32)).astype(BF)
     for mask in reversed(masks):
@@ -459,13 +571,11 @@
     ucount = up.shape[0]
     devices, slots = send_rows.shape[1], send_rows.shape[2]
     imports = devices * slots
-    es, er = edge_sender.reshape(1, ecount), edge_receiver.reshape(1, ecount)
-    us, ur = up_sender.reshape(1, ucount), up_receiver.reshape(1, ucount)
-    gain_row, ngain_row = gain.reshape(1, lat), ngain.reshape(1, lat)
+    es, er = in_far(edge_sender.reshape(1, ecount), edge_receiver.reshape(1, ecount))
+    us, ur = in_far(up_sender.reshape(1, ucount), up_receiver.reshape(1, ucount))
+    gain_row, ngain_row = in_far(gain.reshape(1, lat), ngain.reshape(1, lat))
     own = owner_index()
     core = lax.axis_index("core").reshape(1)
-    in_vmem = pl.BlockSpec(memory_space=pltpu.VMEM)
-    in_smem = pl.BlockSpec(memory_space=pltpu.SMEM)
 
     table = send_rows.reshape(imports)
     hot_send = (table[:, None] == jnp.arange(n, dtype=jnp.int32)[None, :]).astype(BF)
@@ -476,16 +586,16 @@
 
     up_pre, up_xs, up_xr, keep, send = pl.pallas_call(
         up_forward_kernel,
-        in_specs=[in_vmem] * 2 + [in_smem] + [in_vmem] * 6,
+        in_specs=[IN_VMEM] * 2 + [IN_SMEM] + [IN_VMEM] * 2 + [IN_HBM] * 4,
         out_shape=(
-            shape(ucount, width, F32), shape(ucount, lat, BF), shape(ucount, lat, BF),
-            shape(ccount // 2, lat, BF), shape(ccount // 2, lat, BF),
+            far(ucount, width, F32), far(ucount, lat, BF), far(ucount, lat, BF),
+            far(ccount // 2, lat, BF), shape(ccount // 2, lat, BF),
         ),
-        scratch_shapes=[pltpu.VMEM((ccount, lat), F32)],
+        scratch_shapes=[pltpu.VMEM((ccount, lat), F32)] + buffers(node, coarse, w1, w2),
         compiler_params=params(),
         cost_estimate=cost(5.0),
         name="up_forward",
-    )(us, ur, core, up, node, coarse, w1, w2, gain_row)
+    )(us, ur, core, *in_far(up), gain_row, *in_far(node, coarse, w1, w2))
 
     coarse_total = reduce_rows(keep, send)
 
@@ -497,47 +607,49 @@
     pre, xs, fine_total = pl.pallas_call(
         edge_forward_kernel,
         grid=(steps,),
-        in_specs=[index_spec, index_spec, rows_spec]
-        + [whole(a) for a in (node, halo, coarse, w1, w2, gain_row)],
+        in_specs=[index_spec, index_spec, rows_spec] + [IN_VMEM] * 2 + [IN_HBM] * 4,
         out_specs=[pl.BlockSpec((tile, width), lambda i: (i, 0)), rows_spec, fixed(n, lat)],
-        out_shape=(shape(ecount, width, F32), shape(ecount, lat, BF), shape(n, lat, BF)),
-        scratch_shapes=[pltpu.VMEM((n, lat), F32)],
+        out_shape=(far(ecount, width, F32), far(ecount, lat, BF), far(n, lat, BF)),
+        scratch_shapes=[pltpu.VMEM((n, lat), F32)] + buffers(node, coarse, w1, w2),
         compiler_params=params("arbitrary"),
         cost_estimate=cost(9.0),
         name="edge_forward",
-    )(es, er, edge, node, halo, coarse, w1, w2, gain_row)
+    )(es, er, *in_far(edge), halo, gain_row, *in_far(node, coarse, w1, w2))
 
     fine_grad, grad_n, ngw1, ngw2, ngg = pl.pallas_call(
         node_kernel,
+        in_specs=[IN_VMEM] * 4 + [IN_HBM] * 2,
+        scratch_shapes=buffers(nw1, nw2),
         out_shape=(
-            shape(n, lat, F32), shape(n, lat, F32), shape(2 * lat, width, BF),
-            shape(width, lat, BF), shape(1, lat, F32),
+            far(n, lat, F32), far(n, lat, F32), far(2 * lat, width, BF),
+            far(width, lat, BF), shape(1, lat, F32),
         ),
         compiler_params=params(),
         cost_estimate=cost(5.0),
         name="node_mlp",
-    )(node, fine_total, nw1, nw2, ngain_row, ncot)
+    )(*in_far(node, fine_total), ngain_row, *in_far(ncot, nw1, nw2))
 
     grad_e, d_pre, gw2, gg = pl.pallas_call(
         edge_cotangent_kernel,
         grid=(steps,),
-        in_specs=[
-            index_spec, rows_spec, pl.BlockSpec((tile, width), lambda i: (i, 0)), rows_spec,
-        ]
-        + [whole(a) for a in (fine_grad, w1, w2, gain_row)],
+        in_specs=[index_spec, pl.BlockSpec((tile, width), lambda i: (i, 0)), rows_spec]
+        + [IN_VMEM] * 2
+        + [IN_HBM] * 2,
         out_specs=[
             rows_spec, pl.BlockSpec((tile, width), lambda i: (i, 0)), fixed(width, lat),
             fixed(1, lat),
         ],
         out_shape=(
-            shape(ecount, lat, F32), shape(ecount, width, BF), shape(width, lat, BF),
+            far(ecount, lat, F32), far(ecount, width, BF), far(width, lat, BF),
             shape(1, lat, F32),
         ),
-        scratch_shapes=[pltpu.VMEM((width, lat), F32)],
+        scratch_shapes=[pltpu.VMEM((width, lat), F32)] + buffers(far(lat, width, BF), w2),
         compiler_params=params("arbitrary"),
         cost_estimate=cost(8.0),
         name="edge_cotangent",
-    )(er, edge, pre, ecot, fine_grad, w1, w2, gain_row)
+    )(
+        er, *in_far(pre, ecot, fine_grad), gain_row, *in_far(w1, w2)
+    )
 
     gw1, node_part, returning, coarse_local = pl.pallas_call(
         edge_product_kernel,
@@ -546,22 +658,23 @@
             index_spec, index_spec, rows_spec, rows_spec,
             pl.BlockSpec((tile, width), lambda i: (i, 0)),
         ]
-        + [whole(a) for a in (node, w1)],
+        + [IN_HBM] * 2,
         out_specs=[
             fixed(3 * lat, width), fixed(n, lat), fixed(imports, lat), fixed(ccount, lat),
         ],
         out_shape=(
-            shape(3 * lat, width, BF), shape(n, lat, F32), shape(imports, lat, BF),
-            shape(ccount, lat, BF),
+            far(3 * lat, width, BF), far(n, lat, F32), shape(imports, lat, BF),
+            far(ccount, lat, BF),
         ),
         scratch_shapes=[
             pltpu.VMEM((n + imports + ccount, width), F32), pltpu.VMEM((n, width), F32),
             pltpu.VMEM((2 * lat, width), F32),
-        ],
+        ]
+        + buffers(node, far(2 * lat, width, BF)),
         compiler_params=params("arbitrary"),
         cost_estimate=cost(9.0),
         name="edge_product",
-    )(es, er, edge, xs, d_pre, node, w1)
+    )(es, er, *in_far(edge, xs, d_pre, node, w1))
 
     returned = lax.all_to_all(
         returning.reshape(devices, slots, lat), EVERYONE, 0, 0, tiled=True
@@ -575,16 +688,19 @@
     node_rows = padded_rows(2 * lat + width, devices)
     coarse_grad, coarse_after, node_keep, node_send, ngg_sum = pl.pallas_call(
         coarse_kernel,
-        in_specs=[in_smem] + [in_vmem] * 9,
+        in_specs=[IN_SMEM] + [IN_VMEM] * 5 + [IN_HBM] * 4,
         out_shape=(
-            shape(padded, lat, BF), shape(padded, lat, F32), shape(node_rows // 2, lat, BF),
+            shape(padded, lat, BF), far(padded, lat, F32), far(node_rows // 2, lat, BF),
             shape(node_rows // 2, lat, BF), shape(1, lat, F32),
         ),
-        scratch_shapes=[pltpu.VMEM((node_rows, lat), F32)],
+        scratch_shapes=[pltpu.VMEM((node_rows, lat), F32)] + buffers(nw1, nw2, ngw1, ngw2),
         compiler_params=params(),
         cost_estimate=cost(5.0),
         name="coarse_mlp",
-    )(core, own_coarse, pad(coarse_total), own_cot, nw1, nw2, ngain_row, ngw1, ngw2, ngg)
+    )(
+        core, own_coarse, pad(coarse_total), own_cot, ngain_row, ngg,
+        *in_far(nw1, nw2, ngw1, ngw2),
+    )
     cg_own, cg_other = gather_halves(coarse_grad[:mine])
 
     node_total = halving_sum(node_keep, node_send)
@@ -592,25 +708,31 @@
     edge_rows = padded_rows(ccount + 3 * lat + width, devices)
     grad_u, up_node_part, keep, send = pl.pallas_call(
         up_backward_kernel,
-        in_specs=[in_vmem] * 2 + [in_smem] + [in_vmem] * 16,
+        in_specs=[IN_VMEM] * 2 + [IN_SMEM] + [IN_VMEM] * 11 + [IN_HBM] * 5,
+        out_specs=[IN_VMEM] * 2 + [IN_HBM] * 2,
         out_shape=(
-            shape(ucount, lat, F32), shape(n, lat, F32), shape(edge_rows // 2 + TAIL, lat, BF),
-            shape(edge_rows // 2 + TAIL, lat, BF),
+            far(ucount, lat, F32), far(n, lat, F32), far(edge_rows // 2 + TAIL, lat, BF),
+            far(edge_rows // 2 + TAIL, lat, BF),
         ),
-        scratch_shapes=[pltpu.VMEM((ccount, lat), F32), pltpu.VMEM((edge_rows, lat), BF)],
+        scratch_shapes=[
+            pltpu.VMEM((ccount, lat), F32), pltpu.VMEM((edge_rows + 2 * TAIL, lat), BF),
+        ]
+        + buffers(w2, w1, coarse_local, gw2, gw1)
+        + [pltpu.SemaphoreType.DMA((2,))],
         compiler_params=params(),
         cost_estimate=cost(8.0),
         name="up_backward",
     )(
-        us, ur, jnp.stack([own, core[0]]), up, up_xs, up_xr, up_pre, ucot, cg_own, cg_other,
-        w1, w2, gain_row, gw1, gw2, gg, ngg_sum, coarse_local, coarse_after[:mine],
+        us, ur, jnp.stack([own, core[0]]), *in_far(up, up_xs, up_xr, up_pre, ucot), cg_own,
+        cg_other, gain_row, gg, ngg_sum, *in_far(coarse_after[:mine]),
+        *in_far(w2, w1, coarse_local, gw2, gw1),
     )
     block, gains, returned = reduce_with_tail(keep, send, returned)
     own_half, other_half = gather_halves(block)
     edge_scale = 1.0 / math.sqrt((ecount + ucount) * devices)
     node_scale = 1.0 / math.sqrt(n * devices + ccount)
     halves = [ccount // 2, 3 * lat // 2, width // 2]
-    outs = tuple(jax.ShapeDtypeStruct((2, rows, lat), F32) for rows in halves)
+    outs = tuple(pltpu.HBM((2, rows, lat), F32) for rows in halves)
 
     def place_of(flip):
         return [
@@ -641,7 +763,7 @@
         compiler_params=params("arbitrary"),
         cost_estimate=cost(2.5),
         name="widen_other",
-    )(core, other_half, *written)
+    )(core, other_half, *in_far(*written))
     grad_coarse, grad_edge_in, grad_edge_out = (a.reshape(-1, lat) for a in written)
 
     grad_nodes = (

time: 237 us -> 219 us (0.924)
  local copies, waits for them, and re-layouts: 54.1 us -> 7.58 us
  Pallas kernels: 39 us -> 68.8 us
  other arithmetic: 11.9 us -> 8.33 us
  waiting for transfers between devices: 64.1 us -> 67.6 us
    unnamed x141 -> x19, local copies, waits for them, and re-layouts: 49.6 us -> 1.69 us
    pallas_call x6, Pallas kernels: 13.5 us -> 28.3 us  [the longest x1 8.5 us: per_device(): pl.pallas_call(up_backward_kernel, in_specs=[IN_VMEM] * 2 + [IN_SMEM] + [...]
    all_to_all x8, waiting for transfers between devices: 24.5 us -> 28.9 us  [swap(): return lax.all_to_all(x, axes, 0, 0, tiled=True)]
    pallas_call x1, Pallas kernels: 6.86 us -> 11.2 us  [per_device(): pl.pallas_call(edge_forward_kernel, grid=(steps,), in_specs=[index_spec,...]
    pallas_call x4, Pallas kernels: 3.15 us -> 7.06 us  [halving_sum(): pl.pallas_call(fold_split_kernel, in_specs=[pl.BlockSpec(memory_space=plt...]
    pallas_call x1, Pallas kernels: 6.47 us -> 10 us  [per_device(): pl.pallas_call(edge_cotangent_kernel, grid=(steps,), in_specs=[index_spec...]
    pallas_call x1, Pallas kernels: 5.47 us -> 8.65 us  [per_device(): pl.pallas_call(edge_product_kernel, grid=(steps,), in_specs=[index_spec,...]
    select_n x5, other arithmetic: 4.89 us -> 2.38 us  [halving_sum(): jnp.where(place & mask > 0, jnp.concatenate([other, x], 0), jnp.concatena...]
  transfers between devices with their start and end apart: 23 -> 23, of which waited for: 11 -> 12; matrix products, arithmetic and copies ran while one was open for 6% -> 6% of each run, Pallas kernels for 11% -> 21%
where the time goes in v2:
time: 219 us; the launch traced here: 218 us
  Pallas kernels  68.8 us (31%)
  waiting for transfers between devices  67.6 us (31%)
  starting transfers between devices  49.6 us (23%)
  blocking collectives  12 us (5%)
  other arithmetic  8.33 us (4%)
  local copies, waits for them, and re-layouts  7.58 us (3%)
  matrix products  2.72 us (1%)
    ppermute x14, waiting for transfers between devices, exchange(): return lax.ppermute(x, EVERYONE, [(i, i ^ mask) for i in range(devices)])  31.3 us
    all_to_all x8, starting transfers between devices, swap(): return lax.all_to_all(x, axes, 0, 0, tiled=True)  29.4 us
    all_to_all x8, waiting for transfers between devices, swap(): return lax.all_to_all(x, axes, 0, 0, tiled=True)  28.9 us
    ppermute x14, starting transfers between devices, exchange(): return lax.ppermute(x, EVERYONE, [(i, i ^ mask) for i in range(devices)])  13.2 us
    all_to_all x1, blocking collectives, per_device(): lax.all_to_all(returning.reshape(devices, slots, lat), EVERYONE, 0, 0, ti...  12 us
    pallas_call x1, Pallas kernels, per_device(): pl.pallas_call(edge_forward_kernel, grid=(steps,), in_specs=[index_spec,...  11.2 us
    pallas_call x1, Pallas kernels, per_device(): pl.pallas_call(edge_cotangent_kernel, grid=(steps,), in_specs=[index_spec...  10 us
    pallas_call x1, Pallas kernels, per_device(): pl.pallas_call(edge_product_kernel, grid=(steps,), in_specs=[index_spec,...  8.65 us
  transfers between devices with their start and end apart: 23, of which 12 were waited for; matrix products, arithmetic and copies ran while one was open for 6% of the time, Pallas kernels for 21%

profile of v2, /device:TPU:0, one launch (start us, length us, event | category | flops | bytes accessed | tf_op | source)
XLA Modules:
  0.0 217.7 jit_solution(16643285985779703911)
XLA Ops:
  0.7 5.4 %up_forward.1 = (f32[256,512]{1,0:T(8,128)}, bf16[256,512]{1,0:T(8,128)(2,1)}, bf16[256,512]{1,0:T(8,128)(2,1)}, bf16[512,512]{1,0:T(8,128)(2,1)}, bf16[512,512]{1,0:T(8,128)(2,1)S(1)}) custom-call(s32[1,256]{1,0:T(1,128)} %bitcast.44, s32[1,256]{1,0:T(1,128)} %bitcast.46, s32[1]{0:T(128)} %bitcast.7.core, bf16[256,512]{1,0:T(8,128)(2,1)} %up.3, ...), custom_call_target="tpu_custom_call" | custom-call | flops 5500000256 | bytes 15000000 | tf_op jit(solution)/shard_map/up_forward/pallas_call | solution.py:587
  7.8 6.9 %all-to-all-start = ((bf16[32,4,512]{2,1,0:T(4,128)(2,1)}), bf16[32,4,512]{2,1,0:T(4,128)(2,1)S(1)}, u32[]{:S(2)}, u32[]{:S(2)}) async-start(bf16[32,4,512]{2,1,0:T(4,128)(2,1)} %reshape.129), calls=%async_computation | async-start | bytes 262144 | tf_op jit(solution)/shard_map/all_to_all | solution.py:583
  15.5 7.4 %all-to-all-done = bf16[32,4,512]{2,1,0:T(4,128)(2,1)S(1)} async-done(((bf16[32,4,512]{2,1,0:T(4,128)(2,1)}), bf16[32,4,512]{2,1,0:T(4,128)(2,1)S(1)}, u32[]{:S(2)}, u32[]{:S(2)}) %all-to-all-start) | async-done | bytes 131104 | tf_op jit(solution)/shard_map/all_to_all | solution.py:583
  23.9 3.5 %all-to-all-start.1 = ((bf16[4,128,512]{2,1,0:T(8,128)(2,1)}), bf16[4,128,512]{2,1,0:T(8,128)(2,1)S(1)}, u32[]{:S(2)}, u32[]{:S(2)}) async-start(bf16[4,128,512]{2,1,0:T(8,128)(2,1)} %bitcast.8), calls=%async_computation.1 | async-start | bytes 1048576 | tf_op jit(solution)/shard_map/all_to_all | solution.py:458
  27.4 11.2 %edge_forward.1 = (f32[1024,512]{1,0:T(8,128)}, bf16[1024,512]{1,0:T(8,128)(2,1)}, bf16[256,512]{1,0:T(8,128)(2,1)}) custom-call(s32[1,1024]{1,0:T(1,128)} %bitcast.33, s32[1,1024]{1,0:T(1,128)} %bitcast.35, bf16[1024,512]{1,0:T(8,128)(2,1)} %edge.3, bf16[128,512]{1,0:T(8,128)(2,1)S(1)} %reshape.130.halo, f32[1,512]{1,0:T(1,128)} %bitcast.41, ...), custom_call_target="tpu_custom_call" | custom-call | flops 9900000256 | bytes 27000000 | tf_op jit(solution)/shard_map/edge_forward/pallas_call | solution.py:607
  42.7 5.6 %node_mlp.1 = (f32[256,512]{1,0:T(8,128)}, f32[256,512]{1,0:T(8,128)}, bf16[1024,512]{1,0:T(8,128)(2,1)}, bf16[512,512]{1,0:T(8,128)(2,1)}, f32[1,512]{1,0:T(1,128)S(1)}) custom-call(bf16[256,512]{1,0:T(8,128)(2,1)} %node_far.5, bf16[256,512]{1,0:T(8,128)(2,1)} %get-tuple-element.56.total_in, f32[1,512]{1,0:T(1,128)} %bitcast.38, bf16[256,512]{1,0:T(8,128)(2,1)} %ncot.1, ...), custom_call_target="tpu_custom_call" | custom-call | flops 5500000256 | bytes 15000000 | tf_op jit(solution)/shard_map/node_mlp/pallas_call | solution.py:619
  49.1 4.9 %coarse_mlp.1 = (bf16[32,512]{1,0:T(8,128)(2,1)S(1)}, f32[32,512]{1,0:T(8,128)}, bf16[768,512]{1,0:T(8,128)(2,1)}, bf16[768,512]{1,0:T(8,128)(2,1)S(1)}, f32[1,512]{1,0:T(1,128)S(1)}) custom-call(s32[1]{0:T(128)} %bitcast.7.core, bf16[32,512]{1,0:T(8,128)(2,1)S(1)} %constant_dynamic-slice_fusion.1.rows, f32[32,512]{1,0:T(8,128)S(1)} %convert_reduce_fusion.1.total_in, ...), custom_call_target="tpu_custom_call" | custom-call | flops 5500000256 | bytes 15000000 | tf_op jit(solution)/shard_map/coarse_mlp/pallas_call | solution.py:689
  55.6 4.3 %all-to-all-start.3 = ((bf16[4,32,512]{2,1,0:T(8,128)(2,1)}), bf16[4,32,512]{2,1,0:T(8,128)(2,1)S(1)}, u32[]{:S(2)}, u32[]{:S(2)}) async-start(bf16[4,32,512]{2,1,0:T(8,128)(2,1)} %broadcast_in_dim.12), calls=%async_computation.3 | async-start | bytes 262144 | tf_op jit(solution)/shard_map/all_to_all | solution.py:458
  59.9 6.0 %all-to-all-done.3 = bf16[4,32,512]{2,1,0:T(8,128)(2,1)S(1)} async-done(((bf16[4,32,512]{2,1,0:T(8,128)(2,1)}), bf16[4,32,512]{2,1,0:T(8,128)(2,1)S(1)}, u32[]{:S(2)}, u32[]{:S(2)}) %all-to-all-start.3) | async-done | bytes 131104 | tf_op jit(solution)/shard_map/all_to_all | solution.py:458
  66.8 4.1 %all-to-all-start.4 = ((bf16[4,128,512]{2,1,0:T(8,128)(2,1)}), bf16[4,128,512]{2,1,0:T(8,128)(2,1)S(1)}, u32[]{:S(2)}, u32[]{:S(2)}) async-start(bf16[4,128,512]{2,1,0:T(8,128)(2,1)} %broadcast_in_dim.14), calls=%async_computation.4 | async-start | bytes 1048576 | tf_op jit(solution)/shard_map/all_to_all | solution.py:458
  70.9 10.0 %edge_cotangent.1 = (f32[1024,512]{1,0:T(8,128)}, bf16[1024,512]{1,0:T(8,128)(2,1)}, bf16[512,512]{1,0:T(8,128)(2,1)}, f32[1,512]{1,0:T(1,128)S(1)}) custom-call(s32[1,1024]{1,0:T(1,128)} %bitcast.36, f32[1024,512]{1,0:T(8,128)} %get-tuple-element.59.pre_ref, bf16[1024,512]{1,0:T(8,128)(2,1)} %ecot.1, f32[256,512]{1,0:T(8,128)} %get-tuple-element.60.fg, ...), custom_call_target="tpu_custom_call" | custom-call | flops 8800000000 | bytes 24000000 | tf_op jit(solution)/shard_map/edge_cotangent/pallas_call | solution.py:632
  81.0 8.6 %edge_product.1 = (bf16[1536,512]{1,0:T(8,128)(2,1)}, f32[256,512]{1,0:T(8,128)}, bf16[128,512]{1,0:T(8,128)(2,1)S(1)}, bf16[1024,512]{1,0:T(8,128)(2,1)}) custom-call(s32[1,1024]{1,0:T(1,128)} %bitcast.34, s32[1,1024]{1,0:T(1,128)} %bitcast.37, bf16[1024,512]{1,0:T(8,128)(2,1)} %edge.3, bf16[1024,512]{1,0:T(8,128)(2,1)} %get-tuple-element.58.xs, ...), custom_call_target="tpu_custom_call" | custom-call | flops 9900000256 | bytes 27000000 | tf_op jit(solution)/shard_map/edge_product/pallas_call | solution.py:654
  89.7 8.5 %up_backward.1 = (f32[256,512]{1,0:T(8,128)}, f32[256,512]{1,0:T(8,128)}, bf16[1552,512]{1,0:T(8,128)(2,1)}, bf16[1552,512]{1,0:T(8,128)(2,1)}) custom-call(s32[1,256]{1,0:T(1,128)} %bitcast.45, s32[1,256]{1,0:T(1,128)} %bitcast.47, s32[2]{0:T(128)S(1)} %pad_add_fusion.place, bf16[256,512]{1,0:T(8,128)(2,1)} %up.3, bf16[256,512]{1,0:T(8,128)(2,1)} %get-tuple-element.63.xs, ...), custom_call_target="tpu_custom_call" | custom-call | flops 8800000000 | bytes 24000000 | tf_op jit(solution)/shard_map/up_backward/pallas_call | solution.py:709
  98.8 12.0 %all_to_all.68 = bf16[32,4,512]{2,1,0:T(4,128)(2,1)S(1)} all-to-all(bf16[32,4,512]{2,1,0:T(4,128)(2,1)S(1)} %reshape.135), channel_id=1, replica_groups=mesh['z'=4,'x'=2,'y'=2,'core'=2] {'z','x','y','core'}, dimensions={0} | all-to-all | bytes 262144 | tf_op jit(solution)/shard_map/all_to_all | solution.py:679
  114.4 3.7 %all-to-all-start.6 = ((bf16[4,400,512]{2,1,0:T(8,128)(2,1)}), bf16[4,400,512]{2,1,0:T(8,128)(2,1)S(1)}, u32[]{:S(2)}, u32[]{:S(2)}) async-start(bf16[4,400,512]{2,1,0:T(8,128)(2,1)} %shard_map.258), calls=%async_computation.6 | async-start | bytes 3276800 | tf_op jit(solution)/shard_map/all_to_all | solution.py:458
  123.5 15.2 %all-to-all-done.6.got = bf16[4,400,512]{2,1,0:T(8,128)(2,1)S(1)} async-done(((bf16[4,400,512]{2,1,0:T(8,128)(2,1)}), bf16[4,400,512]{2,1,0:T(8,128)(2,1)S(1)}, u32[]{:S(2)}, u32[]{:S(2)}) %all-to-all-start.6) | async-done | bytes 1638432 | tf_op jit(solution)/shard_map/all_to_all | solution.py:458
  139.7 3.5 %all-to-all-start.7 = ((bf16[4,112,512]{2,1,0:T(8,128)(2,1)}), bf16[4,112,512]{2,1,0:T(8,128)(2,1)S(1)}, u32[]{:S(2)}, u32[]{:S(2)}) async-start(bf16[4,112,512]{2,1,0:T(8,128)(2,1)} %shard_map.259), calls=%async_computation.7 | async-start | bytes 917504 | tf_op jit(solution)/shard_map/all_to_all | solution.py:458
  146.3 5.1 %collective-permute-done.6.recv = bf16[192,512]{1,0:T(8,128)(2,1)S(1)} collective-permute-done((bf16[192,512]{1,0:T(8,128)(2,1)S(1)}, bf16[192,512]{1,0:T(8,128)(2,1)S(1)}, u32[]{:S(2)}, u32[]{:S(2)}) %collective-permute-start.6) | collective-permute-done | bytes 196640 | tf_op jit(solution)/shard_map/ppermute | solution.py:475
  154.1 3.5 %collective-permute-done.7.recv = bf16[96,512]{1,0:T(8,128)(2,1)S(1)} collective-permute-done((bf16[96,512]{1,0:T(8,128)(2,1)S(1)}, bf16[96,512]{1,0:T(8,128)(2,1)S(1)}, u32[]{:S(2)}, u32[]{:S(2)}) %collective-permute-start.7) | collective-permute-done | bytes 98336 | tf_op jit(solution)/shard_map/ppermute | solution.py:475
  169.7 8.4 %collective-permute-done.9 = bf16[48,512]{1,0:T(8,128)(2,1)S(1)} collective-permute-done((bf16[48,512]{1,0:T(8,128)(2,1)S(1)}, bf16[48,512]{1,0:T(8,128)(2,1)S(1)}, u32[]{:S(2)}, u32[]{:S(2)}) %collective-permute-start.9) | collective-permute-done | bytes 49184 | tf_op jit(solution)/shard_map/ppermute | solution.py:475
  178.9 3.9 %collective-permute-done.10 = bf16[96,512]{1,0:T(8,128)(2,1)S(1)} collective-permute-done((bf16[96,512]{1,0:T(8,128)(2,1)S(1)}, bf16[96,512]{1,0:T(8,128)(2,1)S(1)}, u32[]{:S(2)}, u32[]{:S(2)}) %collective-permute-start.10) | collective-permute-done | bytes 98336 | tf_op jit(solution)/shard_map/ppermute | solution.py:475
  186.3 3.6 %all-to-all-start.9 = ((bf16[4,384,512]{2,1,0:T(8,128)(2,1)}), bf16[4,384,512]{2,1,0:T(8,128)(2,1)S(1)}, u32[]{:S(2)}, u32[]{:S(2)}) async-start(bf16[4,384,512]{2,1,0:T(8,128)(2,1)} %broadcast_in_dim.34), calls=%async_computation.9 | async-start | bytes 3145728 | tf_op jit(solution)/shard_map/all_to_all | solution.py:458
  190.5 7.8 %collective-permute-done.12 = bf16[384,512]{1,0:T(8,128)(2,1)S(1)} collective-permute-done((bf16[384,512]{1,0:T(8,128)(2,1)S(1)}, bf16[384,512]{1,0:T(8,128)(2,1)S(1)}, u32[]{:S(2)}, u32[]{:S(2)}) %collective-permute-start.12) | collective-permute-done | bytes 393248 | tf_op jit(solution)/shard_map/ppermute | solution.py:475
  198.7 6.9 %all-to-all-done.9 = bf16[4,384,512]{2,1,0:T(8,128)(2,1)S(1)} async-done(((bf16[4,384,512]{2,1,0:T(8,128)(2,1)}), bf16[4,384,512]{2,1,0:T(8,128)(2,1)S(1)}, u32[]{:S(2)}, u32[]{:S(2)}) %all-to-all-start.9) | async-done | bytes 1572896 | tf_op jit(solution)/shard_map/all_to_all | solution.py:458
  (85 shorter events, 56.7 us)
Async XLA Ops:
  6.1 16.9 %copy-start.3 = (bf16[512,512]{1,0:T(8,128)(2,1)S(1)}, bf16[512,512]{1,0:T(8,128)(2,1)}, u32[]{:S(2)}) copy-start(bf16[512,512]{1,0:T(8,128)(2,1)} %get-tuple-element.66) | copy-start | bytes 1572868
  6.1 16.9 %collective-permute-start = (bf16[512,512]{1,0:T(8,128)(2,1)S(1)}, bf16[512,512]{1,0:T(8,128)(2,1)S(1)}, u32[]{:S(2)}, u32[]{:S(2)}) collective-permute-start(bf16[512,512]{1,0:T(8,128)(2,1)S(1)} %get-tuple-element.67), channel_id=1, source_target_pairs={{0,1},{1,0},{2,3},{3,2},{4,5},{5,4},{6,7},{7,6},{8,9},{9,8},{10,11... | collective-permute-start | bytes 1572872 | tf_op jit(solution)/shard_map/ppermute | solution.py:475
  7.8 15.2 %all-to-all-start = ((bf16[32,4,512]{2,1,0:T(4,128)(2,1)}), bf16[32,4,512]{2,1,0:T(4,128)(2,1)S(1)}, u32[]{:S(2)}, u32[]{:S(2)}) async-start(bf16[32,4,512]{2,1,0:T(4,128)(2,1)} %reshape.129), calls=%async_computation | async-start | bytes 262144 | tf_op jit(solution)/shard_map/all_to_all | solution.py:583
  23.9 14.7 %all-to-all-start.1 = ((bf16[4,128,512]{2,1,0:T(8,128)(2,1)}), bf16[4,128,512]{2,1,0:T(8,128)(2,1)S(1)}, u32[]{:S(2)}, u32[]{:S(2)}) async-start(bf16[4,128,512]{2,1,0:T(8,128)(2,1)} %bitcast.8), calls=%async_computation.1 | async-start | bytes 1048576 | tf_op jit(solution)/shard_map/all_to_all | solution.py:458
  39.4 9.7 %all-to-all-start.2 = ((bf16[4,32,512]{2,1,0:T(8,128)(2,1)}), bf16[4,32,512]{2,1,0:T(8,128)(2,1)S(1)}, u32[]{:S(2)}, u32[]{:S(2)}) async-start(bf16[4,32,512]{2,1,0:T(8,128)(2,1)} %bitcast.9), calls=%async_computation.2 | async-start | bytes 262144 | tf_op jit(solution)/shard_map/all_to_all | solution.py:458
  55.6 10.4 %all-to-all-start.3 = ((bf16[4,32,512]{2,1,0:T(8,128)(2,1)}), bf16[4,32,512]{2,1,0:T(8,128)(2,1)S(1)}, u32[]{:S(2)}, u32[]{:S(2)}) async-start(bf16[4,32,512]{2,1,0:T(8,128)(2,1)} %broadcast_in_dim.12), calls=%async_computation.3 | async-start | bytes 262144 | tf_op jit(solution)/shard_map/all_to_all | solution.py:458
  66.8 14.1 %all-to-all-start.4 = ((bf16[4,128,512]{2,1,0:T(8,128)(2,1)}), bf16[4,128,512]{2,1,0:T(8,128)(2,1)S(1)}, u32[]{:S(2)}, u32[]{:S(2)}) async-start(bf16[4,128,512]{2,1,0:T(8,128)(2,1)} %broadcast_in_dim.14), calls=%async_computation.4 | async-start | bytes 1048576 | tf_op jit(solution)/shard_map/all_to_all | solution.py:458
  80.9 8.7 %collective-permute-start.1 = (bf16[512,512]{1,0:T(8,128)(2,1)S(1)}, bf16[512,512]{1,0:T(8,128)(2,1)S(1)}, u32[]{:S(2)}, u32[]{:S(2)}) collective-permute-start(bf16[512,512]{1,0:T(8,128)(2,1)S(1)} %bitcast.27), channel_id=1, source_target_pairs={{0,1},{1,0},{2,3},{3,2},{4,5},{5,4},{6,7},{7,6},{8,9},{9,8},{10,11... | collective-permute-start | bytes 1572872 | tf_op jit(solution)/shard_map/ppermute | solution.py:475
  98.2 13.3 %collective-permute-start.2 = (bf16[1552,512]{1,0:T(8,128)(2,1)}, bf16[1552,512]{1,0:T(8,128)(2,1)S(1)}, u32[]{:S(2)}, u32[]{:S(2)}) collective-permute-start(bf16[1552,512]{1,0:T(8,128)(2,1)} %get-tuple-element.79), channel_id=1, source_target_pairs={{0,1},{1,0},{2,3},{3,2},{4,5},{5,4},{6,7},{7,6},{8,9},{9,8},{10,11... | collective-permute-start | bytes 4767752 | tf_op jit(solution)/shard_map/ppermute | solution.py:475
  114.4 24.3 %all-to-all-start.6 = ((bf16[4,400,512]{2,1,0:T(8,128)(2,1)}), bf16[4,400,512]{2,1,0:T(8,128)(2,1)S(1)}, u32[]{:S(2)}, u32[]{:S(2)}) async-start(bf16[4,400,512]{2,1,0:T(8,128)(2,1)} %shard_map.258), calls=%async_computation.6 | async-start | bytes 3276800 | tf_op jit(solution)/shard_map/all_to_all | solution.py:458
  118.1 2.5 %collective-permute-start.4 = (bf16[768,512]{1,0:T(8,128)(2,1)S(1)}, bf16[768,512]{1,0:T(8,128)(2,1)}, u32[]{:S(2)}, u32[]{:S(2)}) collective-permute-start(bf16[768,512]{1,0:T(8,128)(2,1)S(1)} %copy-done.2), channel_id=1, source_target_pairs={{0,1},{1,0},{2,3},{3,2},{4,5},{5,4},{6,7},{7,6},{8,9},{9,8},{10,11... | collective-permute-start | bytes 2359304 | tf_op jit(solution)/shard_map/ppermute | solution.py:475
  122.8 20.3 %collective-permute-start.5 = (bf16[384,512]{1,0:T(8,128)(2,1)S(1)}, bf16[384,512]{1,0:T(8,128)(2,1)S(1)}, u32[]{:S(2)}, u32[]{:S(2)}) collective-permute-start(bf16[384,512]{1,0:T(8,128)(2,1)S(1)} %get-tuple-element.95), channel_id=1, source_target_pairs={{0,8},{1,9},{2,10},{3,11},{4,12},{5,13},{6,14},{7,15},{8,0},{9,1},... | collective-permute-start | bytes 1179656 | tf_op jit(solution)/shard_map/ppermute | solution.py:475
  139.7 22.1 %all-to-all-start.7 = ((bf16[4,112,512]{2,1,0:T(8,128)(2,1)}), bf16[4,112,512]{2,1,0:T(8,128)(2,1)S(1)}, u32[]{:S(2)}, u32[]{:S(2)}) async-start(bf16[4,112,512]{2,1,0:T(8,128)(2,1)} %shard_map.259), calls=%async_computation.7 | async-start | bytes 917504 | tf_op jit(solution)/shard_map/all_to_all | solution.py:458
  144.9 6.5 %collective-permute-start.6 = (bf16[192,512]{1,0:T(8,128)(2,1)S(1)}, bf16[192,512]{1,0:T(8,128)(2,1)S(1)}, u32[]{:S(2)}, u32[]{:S(2)}) collective-permute-start(bf16[192,512]{1,0:T(8,128)(2,1)S(1)} %get-tuple-element.97), channel_id=1, source_target_pairs={{0,4},{1,5},{2,6},{3,7},{4,0},{5,1},{6,2},{7,3},{8,12},{9,13},{10,... | collective-permute-start | bytes 589832 | tf_op jit(solution)/shard_map/ppermute | solution.py:475
  153.0 4.6 %collective-permute-start.7 = (bf16[96,512]{1,0:T(8,128)(2,1)S(1)}, bf16[96,512]{1,0:T(8,128)(2,1)S(1)}, u32[]{:S(2)}, u32[]{:S(2)}) collective-permute-start(bf16[96,512]{1,0:T(8,128)(2,1)S(1)} %get-tuple-element.99), channel_id=1, source_target_pairs={{0,2},{1,3},{2,0},{3,1},{4,6},{5,7},{6,4},{7,5},{8,10},{9,11},{10,... | collective-permute-start | bytes 294920 | tf_op jit(solution)/shard_map/ppermute | solution.py:475
  159.1 7.6 %collective-permute-start.8 = (bf16[48,512]{1,0:T(8,128)(2,1)S(1)}, bf16[48,512]{1,0:T(8,128)(2,1)S(1)}, u32[]{:S(2)}, u32[]{:S(2)}) collective-permute-start(bf16[48,512]{1,0:T(8,128)(2,1)S(1)} %get-tuple-element.101), channel_id=1, source_target_pairs={{0,16},{1,17},{2,18},{3,19},{4,20},{5,21},{6,22},{7,23},{8,24},{9,... | collective-permute-start | bytes 147464 | tf_op jit(solution)/shard_map/ppermute | solution.py:475
  163.3 21.7 %all-to-all-start.8 = ((bf16[4,96,512]{2,1,0:T(8,128)(2,1)}), bf16[4,96,512]{2,1,0:T(8,128)(2,1)S(1)}, u32[]{:S(2)}, u32[]{:S(2)}) async-start(bf16[4,96,512]{2,1,0:T(8,128)(2,1)} %broadcast_in_dim.15), calls=%async_computation.8 | async-start | bytes 786432 | tf_op jit(solution)/shard_map/all_to_all | solution.py:458
  166.8 11.3 %collective-permute-start.9 = (bf16[48,512]{1,0:T(8,128)(2,1)S(1)}, bf16[48,512]{1,0:T(8,128)(2,1)S(1)}, u32[]{:S(2)}, u32[]{:S(2)}) collective-permute-start(bf16[48,512]{1,0:T(8,128)(2,1)S(1)} %add_convert_fusion.1), channel_id=1, source_target_pairs={{0,16},{1,17},{2,18},{3,19},{4,20},{5,21},{6,22},{7,23},{8,24},{9,... | collective-permute-start | bytes 147464 | tf_op jit(solution)/shard_map/ppermute | solution.py:475
  178.1 4.7 %collective-permute-start.10 = (bf16[96,512]{1,0:T(8,128)(2,1)S(1)}, bf16[96,512]{1,0:T(8,128)(2,1)S(1)}, u32[]{:S(2)}, u32[]{:S(2)}) collective-permute-start(bf16[96,512]{1,0:T(8,128)(2,1)S(1)} %maximum_select_fusion.4), channel_id=1, source_target_pairs={{0,2},{1,3},{2,0},{3,1},{4,6},{5,7},{6,4},{7,5},{8,10},{9,11},{10,... | collective-permute-start | bytes 294920 | tf_op jit(solution)/shard_map/ppermute | solution.py:475
  182.8 7.4 %collective-permute-start.11 = (bf16[192,512]{1,0:T(8,128)(2,1)S(1)}, bf16[192,512]{1,0:T(8,128)(2,1)S(1)}, u32[]{:S(2)}, u32[]{:S(2)}) collective-permute-start(bf16[192,512]{1,0:T(8,128)(2,1)S(1)} %maximum_select_fusion.3), channel_id=1, source_target_pairs={{0,4},{1,5},{2,6},{3,7},{4,0},{5,1},{6,2},{7,3},{8,12},{9,13},{10,... | collective-permute-start | bytes 589832 | tf_op jit(solution)/shard_map/ppermute | solution.py:475
  186.3 19.3 %all-to-all-start.9 = ((bf16[4,384,512]{2,1,0:T(8,128)(2,1)}), bf16[4,384,512]{2,1,0:T(8,128)(2,1)S(1)}, u32[]{:S(2)}, u32[]{:S(2)}) async-start(bf16[4,384,512]{2,1,0:T(8,128)(2,1)} %broadcast_in_dim.34), calls=%async_computation.9 | async-start | bytes 3145728 | tf_op jit(solution)/shard_map/all_to_all | solution.py:458
  190.4 7.8 %collective-permute-start.12 = (bf16[384,512]{1,0:T(8,128)(2,1)S(1)}, bf16[384,512]{1,0:T(8,128)(2,1)S(1)}, u32[]{:S(2)}, u32[]{:S(2)}) collective-permute-start(bf16[384,512]{1,0:T(8,128)(2,1)S(1)} %maximum_select_fusion.2), channel_id=1, source_target_pairs={{0,8},{1,9},{2,10},{3,11},{4,12},{5,13},{6,14},{7,15},{8,0},{9,1},... | collective-permute-start | bytes 1179656 | tf_op jit(solution)/shard_map/ppermute | solution.py:475
  198.6 9.5 %collective-permute-start.13 = (bf16[768,512]{1,0:T(8,128)(2,1)S(1)}, bf16[768,512]{1,0:T(8,128)(2,1)}, u32[]{:S(2)}, u32[]{:S(2)}) collective-permute-start(bf16[768,512]{1,0:T(8,128)(2,1)S(1)} %maximum_select_fusion.1), channel_id=1, source_target_pairs={{0,1},{1,0},{2,3},{3,2},{4,5},{5,4},{6,7},{7,6},{8,9},{9,8},{10,11... | collective-permute-start | bytes 2359304 | tf_op jit(solution)/shard_map/ppermute | solution.py:475
  205.5 10.3 %collective-permute-start.3 = (bf16[1536,512]{1,0:T(8,128)(2,1)S(1)}, bf16[1536,512]{1,0:T(8,128)(2,1)S(1)}, u32[]{:S(2)}, u32[]{:S(2)}) collective-permute-start(bf16[1536,512]{1,0:T(8,128)(2,1)S(1)} %bitcast.25), channel_id=1, source_target_pairs={{0,1},{1,0},{2,3},{3,2},{4,5},{5,4},{6,7},{7,6},{8,9},{9,8},{10,11... | collective-permute-start | bytes 4718600 | tf_op jit(solution)/shard_map/ppermute | solution.py:475
  (8 other events, 55.7 us)

commit v3 on v2

--- a/solution.py
+++ b/solution.py
@@ -134,40 +134,59 @@
 
 
 def edge_forward_kernel(
-    es, er, edge, halo, gain, node_far, coarse_far, w1_far, w2_far, p_ref, xs_ref, total_ref,
-    acc, node, coarse, w1, w2, sems,
+    es, er, edge, halo, gain, w1_far, w2_far, node_far, coarse_far, p_ref, xs_ref, total_ref,
+    acc, w1, w2, node, coarse, sems,
 ):
     step = pl.program_id(0)
     lat = edge.shape[1]
     n = node.shape[0]
     imports = halo.shape[0]
-    loads = loads_of((node_far, coarse_far, w1_far, w2_far), (node, coarse, w1, w2), sems)
+    parts = [slice(k * lat, (k + 1) * lat) for k in (0, 2, 1)]
+    first, last, middle = (
+        pltpu.make_async_copy(w1_far.at[part], w1.at[part], sems.at[k])
+        for k, part in enumerate(parts)
+    )
+    node_load = pltpu.make_async_copy(node_far, node, sems.at[3])
+    coarse_load = pltpu.make_async_copy(coarse_far, coarse, sems.at[4])
+    w2_load = pltpu.make_async_copy(w2_far, w2, sems.at[5])
 
     @pl.when(step == 0)
     def _():
-        for load in loads:
+        for load in (first, node_load, last, coarse_load, middle, w2_load):
             load.start()
         acc[...] = jnp.zeros_like(acc)
-        for load in loads[:3]:
-            load.wait()
 
     sender = es[...]
-    xs = (
-        dot_lt(onehot_t(sender, n), node[...])
-        + dot_lt(onehot_t(sender, imports, n), halo[...])
-        + dot_lt(onehot_t(sender, coarse.shape[0], n + imports), coarse[...])
-    ).astype(BF)
     hot_r = onehot_t(er[...], n)
-    xr = dot_lt(hot_r, node[...]).astype(BF)
-    pre = dot(edge[...], w1[0:lat]) + dot(xs, w1[lat : 2 * lat]) + dot(xr, w1[2 * lat :])
-    p_ref[...] = pre
 
     @pl.when(step == 0)
     def _():
-        loads[3].wait()
-
+        first.wait()
+
+    pre = dot(edge[...], w1[0:lat])
+
+    @pl.when(step == 0)
+    def _():
+        node_load.wait()
+        last.wait()
+
+    pre += dot(dot_lt(hot_r, node[...]).astype(BF), w1[2 * lat :])
+    xs = dot_lt(onehot_t(sender, n), node[...]) + dot_lt(
+        onehot_t(sender, imports, n), halo[...]
+    )
+    hot_c = onehot_t(sender, coarse.shape[0], n + imports)
+
+    @pl.when(step == 0)
+    def _():
+        coarse_load.wait()
+        middle.wait()
+        w2_load.wait()
+
+    xs = (xs + dot_lt(hot_c, coarse[...])).astype(BF)
+    pre += dot(xs, w1[lat : 2 * lat])
     normed, _ = normalise(dot(hidden_of(pre), w2[...]))
     new = (edge[...].astype(F32) + normed * gain[...]).astype(BF)
+    p_ref[...] = pre
     xs_ref[...] = xs
     acc[...] += dot(hot_r, new)
 
@@ -202,75 +221,58 @@
     fg_ref[...] = dot_rt(d_pre, nw1[lat:])
 
 
-def edge_cotangent_kernel(
-    er, pre_ref, ecot, fg, gain, w1_far, w2_far, ge_ref, dp_ref, gw2_out, gg_ref,
-    gw2, w1, w2, sems,
-):
-    step = pl.program_id(0)
-    lat = ecot.shape[1]
-    loads = loads_of((w1_far.at[0:lat], w2_far), (w1, w2), sems)
-
-    @pl.when(step == 0)
-    def _():
-        for load in loads:
-            load.start()
-        gw2[...] = jnp.zeros_like(gw2)
-        gg_ref[...] = jnp.zeros_like(gg_ref)
-
-    cot = ecot[...].astype(F32) + gather_f32(onehot_t(er[...], fg.shape[0]), fg[...])
-    pre = pre_ref[...]
-    hidden = hidden_of(pre)
-
-    @pl.when(step == 0)
-    def _():
-        for load in loads:
-            load.wait()
-
-    normed, inv_std = normalise(dot(hidden, w2[...]))
-    gain_part, d_proj, d_pre = grad_to_pre(pre, normed, inv_std, cot, gain[...], w2[...])
-    gg_ref[...] += gain_part
-    gw2[...] += dot_lt(hidden, d_proj)
-    ge_ref[...] = cot + dot_rt(d_pre, w1[...])
-    dp_ref[...] = d_pre
-
-    @pl.when(step == pl.num_programs(0) - 1)
-    def _():
-        gw2_out[...] = gw2[...].astype(BF)
-
-
-def edge_product_kernel(
-    es, er, edge, xs, dp, node_far, w1_far, gw1_out, np_ref, ret_ref, cp_ref,
-    sum_s, sum_r, gw1, node, w1, sems,
+def edge_backward_kernel(
+    es, er, edge, xs, pre_ref, ecot, gain, w2_far, fg_far, w1_far, node_far,
+    ge_ref, gw1_out, gw2_out, gg_ref, np_ref, ret_ref, cp_ref,
+    sum_s, sum_r, gw1, gw2, w2, fg, w1, node, sems,
 ):
     step = pl.program_id(0)
     lat = edge.shape[1]
     n = node.shape[0]
     imports = ret_ref.shape[0]
-    loads = loads_of((node_far, w1_far.at[lat : 3 * lat]), (node, w1), sems)
+    loads = loads_of((w2_far, fg_far, w1_far, node_far), (w2, fg, w1, node), sems)
 
     @pl.when(step == 0)
     def _():
         for load in loads:
             load.start()
-        sum_s[...] = jnp.zeros_like(sum_s)
-        sum_r[...] = jnp.zeros_like(sum_r)
-        gw1[...] = jnp.zeros_like(gw1)
-
-    d_pre = dp[...]
+        for ref in (sum_s, sum_r, gw1, gw2, gg_ref):
+            ref[...] = jnp.zeros_like(ref)
+
+    hot_r = onehot_t(er[...], n)
+    pre = pre_ref[...]
+    hidden = hidden_of(pre)
+
+    @pl.when(step == 0)
+    def _():
+        loads[0].wait()
+
+    normed, inv_std = normalise(dot(hidden, w2[...]))
+
+    @pl.when(step == 0)
+    def _():
+        loads[1].wait()
+        loads[2].wait()
+
+    cot = ecot[...].astype(F32) + gather_f32(hot_r, fg[...])
+    gain_part, d_proj, d_pre = grad_to_pre(pre, normed, inv_std, cot, gain[...], w2[...])
+    gg_ref[...] += gain_part
+    ge_ref[...] = cot + dot_rt(d_pre, w1[0:lat])
+    gw2[...] += dot_lt(hidden, d_proj)
     gw1[0:lat] += dot_lt(edge[...], d_pre)
     gw1[lat:] += dot_lt(xs[...], d_pre)
-    sum_r[...] += dot(onehot_t(er[...], n), d_pre)
+    sum_r[...] += dot(hot_r, d_pre)
     sum_s[...] += dot(onehot_t(es[...], sum_s.shape[0]), d_pre)
 
     @pl.when(step == pl.num_programs(0) - 1)
     def _():
-        for load in loads:
-            load.wait()
-        w_s = w1[0:lat]
+        loads[3].wait()
+        w_s = w1[lat : 2 * lat]
         recv = sum_r[...].astype(BF)
+        gw2_out[...] = gw2[...].astype(BF)
         gw1_out[0 : 2 * lat] = gw1[...].astype(BF)
         gw1_out[2 * lat :] = dot_lt(node[...], recv).astype(BF)
-        np_ref[...] = dot_rt(sum_s[0:n].astype(BF), w_s) + dot_rt(recv, w1[lat:])
+        np_ref[...] = dot_rt(sum_s[0:n].astype(BF), w_s) + dot_rt(recv, w1[2 * lat :])
         ret_ref[...] = dot_rt(sum_s[n : n + imports].astype(BF), w_s).astype(BF)
         cp_ref[...] = dot_rt(sum_s[n + imports :].astype(BF), w_s).astype(BF)
 
@@ -610,11 +612,13 @@
         in_specs=[index_spec, index_spec, rows_spec] + [IN_VMEM] * 2 + [IN_HBM] * 4,
         out_specs=[pl.BlockSpec((tile, width), lambda i: (i, 0)), rows_spec, fixed(n, lat)],
         out_shape=(far(ecount, width, F32), far(ecount, lat, BF), far(n, lat, BF)),
-        scratch_shapes=[pltpu.VMEM((n, lat), F32)] + buffers(node, coarse, w1, w2),
+        scratch_shapes=[pltpu.VMEM((n, lat), F32)]
+        + buffers(w1, w2, node, coarse)[:-1]
+        + [pltpu.SemaphoreType.DMA((6,))],
         compiler_params=params("arbitrary"),
         cost_estimate=cost(9.0),
         name="edge_forward",
-    )(es, er, *in_far(edge), halo, gain_row, *in_far(node, coarse, w1, w2))
+    )(es, er, *in_far(edge), halo, gain_row, *in_far(w1, w2, node, coarse))
 
     fine_grad, grad_n, ngw1, ngw2, ngg = pl.pallas_call(
         node_kernel,
@@ -629,52 +633,33 @@
         name="node_mlp",
     )(*in_far(node, fine_total), ngain_row, *in_far(ncot, nw1, nw2))
 
-    grad_e, d_pre, gw2, gg = pl.pallas_call(
-        edge_cotangent_kernel,
-        grid=(steps,),
-        in_specs=[index_spec, pl.BlockSpec((tile, width), lambda i: (i, 0)), rows_spec]
-        + [IN_VMEM] * 2
-        + [IN_HBM] * 2,
-        out_specs=[
-            rows_spec, pl.BlockSpec((tile, width), lambda i: (i, 0)), fixed(width, lat),
-            fixed(1, lat),
-        ],
-        out_shape=(
-            far(ecount, lat, F32), far(ecount, width, BF), far(width, lat, BF),
-            shape(1, lat, F32),
-        ),
-        scratch_shapes=[pltpu.VMEM((width, lat), F32)] + buffers(far(lat, width, BF), w2),
-        compiler_params=params("arbitrary"),
-        cost_estimate=cost(8.0),
-        name="edge_cotangent",
-    )(
-        er, *in_far(pre, ecot, fine_grad), gain_row, *in_far(w1, w2)
-    )
-
-    gw1, node_part, returning, coarse_local = pl.pallas_call(
-        edge_product_kernel,
+    grad_e, gw1, gw2, gg, node_part, returning, coarse_local = pl.pallas_call(
+        edge_backward_kernel,
         grid=(steps,),
         in_specs=[
             index_spec, index_spec, rows_spec, rows_spec,
-            pl.BlockSpec((tile, width), lambda i: (i, 0)),
+            pl.BlockSpec((tile, width), lambda i: (i, 0)), rows_spec,
         ]
-        + [IN_HBM] * 2,
+        + [IN_VMEM]
+        + [IN_HBM] * 4,
         out_specs=[
-            fixed(3 * lat, width), fixed(n, lat), fixed(imports, lat), fixed(ccount, lat),
+            rows_spec, fixed(3 * lat, width), fixed(width, lat), fixed(1, lat), fixed(n, lat),
+            fixed(imports, lat), fixed(ccount, lat),
         ],
         out_shape=(
-            far(3 * lat, width, BF), far(n, lat, F32), shape(imports, lat, BF),
+            far(ecount, lat, F32), far(3 * lat, width, BF), far(width, lat, BF),
+            shape(1, lat, F32), far(n, lat, F32), shape(imports, lat, BF),
             far(ccount, lat, BF),
         ),
         scratch_shapes=[
             pltpu.VMEM((n + imports + ccount, width), F32), pltpu.VMEM((n, width), F32),
-            pltpu.VMEM((2 * lat, width), F32),
+            pltpu.VMEM((2 * lat, width), F32), pltpu.VMEM((width, lat), F32),
         ]
-        + buffers(node, far(2 * lat, width, BF)),
+        + buffers(w2, fine_grad, w1, node),
         compiler_params=params("arbitrary"),
-        cost_estimate=cost(9.0),
-        name="edge_product",
-    )(es, er, *in_far(edge, xs, d_pre, node, w1))
+        cost_estimate=cost(15.0),
+        name="edge_backward",
+    )(es, er, *in_far(edge, xs, pre, ecot), gain_row, *in_far(w2, fine_grad, w1, node))
 
     returned = lax.all_to_all(
         returning.reshape(devices, slots, lat), EVERYONE, 0, 0, tiled=True

time: 219 us -> 222 us (1.014)
  blocking collectives: 12 us -> 21.6 us
  starting transfers between devices: 49.6 us -> 45.3 us
    all_to_all x0 -> x1, blocking collectives: none -> 10.2 us  [swap(): return lax.all_to_all(x, axes, 0, 0, tiled=True)]
    all_to_all x8 -> x7, starting transfers between devices: 29.4 us -> 25.1 us  [swap(): return lax.all_to_all(x, axes, 0, 0, tiled=True)]
    pallas_call x2 -> x1, Pallas kernels: 18.7 us -> 15.8 us  [per_device(): pl.pallas_call(edge_backward_kernel, grid=(steps,), in_specs=[index_spec,...]
    all_to_all x8 -> x7, waiting for transfers between devices: 28.9 us -> 29.4 us  [swap(): return lax.all_to_all(x, axes, 0, 0, tiled=True)]
  transfers between devices with their start and end apart: 23 -> 22, of which waited for: 12 -> 12; matrix products, arithmetic and copies ran while one was open for 6% -> 6% of each run, Pallas kernels for 21% -> 19%
where the time goes in v3:
time: 222 us; the launch traced here: 221 us
  waiting for transfers between devices  68.1 us (31%)
  Pallas kernels  66.6 us (30%)
  starting transfers between devices  45.3 us (20%)
  blocking collectives  21.6 us (10%)
  other arithmetic  8.39 us (4%)
  local copies, waits for them, and re-layouts  6.92 us (3%)
  matrix products  2.72 us (1%)
    ppermute x14, waiting for transfers between devices, exchange(): return lax.ppermute(x, EVERYONE, [(i, i ^ mask) for i in range(devices)])  31.3 us
    all_to_all x7, waiting for transfers between devices, swap(): return lax.all_to_all(x, axes, 0, 0, tiled=True)  29.4 us
    all_to_all x7, starting transfers between devices, swap(): return lax.all_to_all(x, axes, 0, 0, tiled=True)  25.1 us
    pallas_call x1, Pallas kernels, per_device(): pl.pallas_call(edge_backward_kernel, grid=(steps,), in_specs=[index_spec,...  15.8 us
    ppermute x14, starting transfers between devices, exchange(): return lax.ppermute(x, EVERYONE, [(i, i ^ mask) for i in range(devices)])  13.2 us
    pallas_call x1, Pallas kernels, per_device(): pl.pallas_call(edge_forward_kernel, grid=(steps,), in_specs=[index_spec,...  11.8 us
    all_to_all x1, blocking collectives, per_device(): lax.all_to_all(returning.reshape(devices, slots, lat), EVERYONE, 0, 0, ti...  11.4 us
    all_to_all x1, blocking collectives, swap(): return lax.all_to_all(x, axes, 0, 0, tiled=True)  10.2 us
  transfers between devices with their start and end apart: 22, of which 12 were waited for; matrix products, arithmetic and copies ran while one was open for 6% of the time, Pallas kernels for 19%

profile of v3, /device:TPU:0, one launch (start us, length us, event | category | flops | bytes accessed | tf_op | source)
XLA Modules:
  0.0 220.6 jit_solution(9028769791878738643)
XLA Ops:
  0.7 5.4 %up_forward.1 = (f32[256,512]{1,0:T(8,128)}, bf16[256,512]{1,0:T(8,128)(2,1)}, bf16[256,512]{1,0:T(8,128)(2,1)}, bf16[512,512]{1,0:T(8,128)(2,1)}, bf16[512,512]{1,0:T(8,128)(2,1)S(1)}) custom-call(s32[1,256]{1,0:T(1,128)} %bitcast.43, s32[1,256]{1,0:T(1,128)} %bitcast.45, s32[1]{0:T(128)} %bitcast.7.core, bf16[256,512]{1,0:T(8,128)(2,1)} %up.3, ...), custom_call_target="tpu_custom_call" | custom-call | flops 5500000256 | bytes 15000000 | tf_op jit(solution)/shard_map/up_forward/pallas_call | solution.py:589
  7.8 6.9 %all-to-all-start = ((bf16[32,4,512]{2,1,0:T(4,128)(2,1)}), bf16[32,4,512]{2,1,0:T(4,128)(2,1)S(1)}, u32[]{:S(2)}, u32[]{:S(2)}) async-start(bf16[32,4,512]{2,1,0:T(4,128)(2,1)} %reshape.129), calls=%async_computation | async-start | bytes 262144 | tf_op jit(solution)/shard_map/all_to_all | solution.py:585
  15.5 7.4 %all-to-all-done = bf16[32,4,512]{2,1,0:T(4,128)(2,1)S(1)} async-done(((bf16[32,4,512]{2,1,0:T(4,128)(2,1)}), bf16[32,4,512]{2,1,0:T(4,128)(2,1)S(1)}, u32[]{:S(2)}, u32[]{:S(2)}) %all-to-all-start) | async-done | bytes 131104 | tf_op jit(solution)/shard_map/all_to_all | solution.py:585
  23.9 3.5 %all-to-all-start.1 = ((bf16[4,128,512]{2,1,0:T(8,128)(2,1)}), bf16[4,128,512]{2,1,0:T(8,128)(2,1)S(1)}, u32[]{:S(2)}, u32[]{:S(2)}) async-start(bf16[4,128,512]{2,1,0:T(8,128)(2,1)} %bitcast.8), calls=%async_computation.1 | async-start | bytes 1048576 | tf_op jit(solution)/shard_map/all_to_all | solution.py:460
  27.4 11.8 %edge_forward.1 = (f32[1024,512]{1,0:T(8,128)}, bf16[1024,512]{1,0:T(8,128)(2,1)}, bf16[256,512]{1,0:T(8,128)(2,1)}) custom-call(s32[1,1024]{1,0:T(1,128)} %bitcast.33, s32[1,1024]{1,0:T(1,128)} %bitcast.35, bf16[1024,512]{1,0:T(8,128)(2,1)} %edge.3, bf16[128,512]{1,0:T(8,128)(2,1)S(1)} %reshape.130.halo, f32[1,512]{1,0:T(1,128)} %bitcast.40, ...), custom_call_target="tpu_custom_call" | custom-call | flops 9900000256 | bytes 27000000 | tf_op jit(solution)/shard_map/edge_forward/pallas_call | solution.py:609
  43.3 5.6 %node_mlp.1 = (f32[256,512]{1,0:T(8,128)}, f32[256,512]{1,0:T(8,128)}, bf16[1024,512]{1,0:T(8,128)(2,1)}, bf16[512,512]{1,0:T(8,128)(2,1)}, f32[1,512]{1,0:T(1,128)S(1)}) custom-call(bf16[256,512]{1,0:T(8,128)(2,1)} %node_far.5, bf16[256,512]{1,0:T(8,128)(2,1)} %get-tuple-element.55.total_in, f32[1,512]{1,0:T(1,128)} %bitcast.37, bf16[256,512]{1,0:T(8,128)(2,1)} %ncot.1, ...), custom_call_target="tpu_custom_call" | custom-call | flops 5500000256 | bytes 15000000 | tf_op jit(solution)/shard_map/node_mlp/pallas_call | solution.py:623
  49.7 4.9 %coarse_mlp.1 = (bf16[32,512]{1,0:T(8,128)(2,1)S(1)}, f32[32,512]{1,0:T(8,128)}, bf16[768,512]{1,0:T(8,128)(2,1)}, bf16[768,512]{1,0:T(8,128)(2,1)S(1)}, f32[1,512]{1,0:T(1,128)S(1)}) custom-call(s32[1]{0:T(128)} %bitcast.7.core, bf16[32,512]{1,0:T(8,128)(2,1)S(1)} %constant_dynamic-slice_fusion.1.rows, f32[32,512]{1,0:T(8,128)S(1)} %convert_reduce_fusion.1.total_in, ...), custom_call_target="tpu_custom_call" | custom-call | flops 5500000256 | bytes 15000000 | tf_op jit(solution)/shard_map/coarse_mlp/pallas_call | solution.py:674
  55.5 10.2 %all_to_all.68 = bf16[4,32,512]{2,1,0:T(8,128)(2,1)S(1)} all-to-all(bf16[4,32,512]{2,1,0:T(8,128)(2,1)S(1)} %broadcast_in_dim.12), channel_id=1, replica_groups=mesh['z'=4,'x'=2,'y'=2,'core'=2] {'z'}, dimensions={0} | all-to-all | bytes 262144 | tf_op jit(solution)/shard_map/all_to_all | solution.py:460
  66.5 4.1 %all-to-all-start.4 = ((bf16[4,128,512]{2,1,0:T(8,128)(2,1)}), bf16[4,128,512]{2,1,0:T(8,128)(2,1)S(1)}, u32[]{:S(2)}, u32[]{:S(2)}) async-start(bf16[4,128,512]{2,1,0:T(8,128)(2,1)} %broadcast_in_dim.14), calls=%async_computation.4 | async-start | bytes 1048576 | tf_op jit(solution)/shard_map/all_to_all | solution.py:460
  70.7 6.5 %all-to-all-done.4 = bf16[4,128,512]{2,1,0:T(8,128)(2,1)S(1)} async-done(((bf16[4,128,512]{2,1,0:T(8,128)(2,1)}), bf16[4,128,512]{2,1,0:T(8,128)(2,1)S(1)}, u32[]{:S(2)}, u32[]{:S(2)}) %all-to-all-start.4) | async-done | bytes 524320 | tf_op jit(solution)/shard_map/all_to_all | solution.py:460
  77.2 15.8 %edge_backward.1 = (f32[1024,512]{1,0:T(8,128)}, bf16[1536,512]{1,0:T(8,128)(2,1)}, bf16[512,512]{1,0:T(8,128)(2,1)}, f32[1,512]{1,0:T(1,128)S(1)}, f32[256,512]...) custom-call(s32[1,1024]{1,0:T(1,128)} %bitcast.34, s32[1,1024]{1,0:T(1,128)} %bitcast.36, ...), custom_call_target="tpu_custom_call" | custom-call | flops 16499999744 | bytes 45000000 | tf_op jit(solution)/shard_map/edge_backward/pallas_call | solution.py:636
  93.1 8.5 %up_backward.1 = (f32[256,512]{1,0:T(8,128)}, f32[256,512]{1,0:T(8,128)}, bf16[1552,512]{1,0:T(8,128)(2,1)}, bf16[1552,512]{1,0:T(8,128)(2,1)}) custom-call(s32[1,256]{1,0:T(1,128)} %bitcast.44, s32[1,256]{1,0:T(1,128)} %bitcast.46, s32[2]{0:T(128)S(1)} %pad_add_fusion.place, bf16[256,512]{1,0:T(8,128)(2,1)} %up.3, bf16[256,512]{1,0:T(8,128)(2,1)} %get-tuple-element.61.xs, ...), custom_call_target="tpu_custom_call" | custom-call | flops 8800000000 | bytes 24000000 | tf_op jit(solution)/shard_map/up_backward/pallas_call | solution.py:694
  102.2 11.4 %all_to_all.69 = bf16[32,4,512]{2,1,0:T(4,128)(2,1)S(1)} all-to-all(bf16[32,4,512]{2,1,0:T(4,128)(2,1)S(1)} %reshape.135), channel_id=1, replica_groups=mesh['z'=4,'x'=2,'y'=2,'core'=2] {'z','x','y','core'}, dimensions={0} | all-to-all | bytes 262144 | tf_op jit(solution)/shard_map/all_to_all | solution.py:664
  117.3 3.7 %all-to-all-start.6 = ((bf16[4,400,512]{2,1,0:T(8,128)(2,1)}), bf16[4,400,512]{2,1,0:T(8,128)(2,1)S(1)}, u32[]{:S(2)}, u32[]{:S(2)}) async-start(bf16[4,400,512]{2,1,0:T(8,128)(2,1)} %shard_map.258), calls=%async_computation.6 | async-start | bytes 3276800 | tf_op jit(solution)/shard_map/all_to_all | solution.py:460
  126.3 15.2 %all-to-all-done.6.got = bf16[4,400,512]{2,1,0:T(8,128)(2,1)S(1)} async-done(((bf16[4,400,512]{2,1,0:T(8,128)(2,1)}), bf16[4,400,512]{2,1,0:T(8,128)(2,1)S(1)}, u32[]{:S(2)}, u32[]{:S(2)}) %all-to-all-start.6) | async-done | bytes 1638432 | tf_op jit(solution)/shard_map/all_to_all | solution.py:460
  142.5 3.5 %all-to-all-start.7 = ((bf16[4,112,512]{2,1,0:T(8,128)(2,1)}), bf16[4,112,512]{2,1,0:T(8,128)(2,1)S(1)}, u32[]{:S(2)}, u32[]{:S(2)}) async-start(bf16[4,112,512]{2,1,0:T(8,128)(2,1)} %shard_map.259), calls=%async_computation.7 | async-start | bytes 917504 | tf_op jit(solution)/shard_map/all_to_all | solution.py:460
  149.2 5.1 %collective-permute-done.6.recv = bf16[192,512]{1,0:T(8,128)(2,1)S(1)} collective-permute-done((bf16[192,512]{1,0:T(8,128)(2,1)S(1)}, bf16[192,512]{1,0:T(8,128)(2,1)S(1)}, u32[]{:S(2)}, u32[]{:S(2)}) %collective-permute-start.6) | collective-permute-done | bytes 196640 | tf_op jit(solution)/shard_map/ppermute | solution.py:477
  157.0 3.5 %collective-permute-done.7.recv = bf16[96,512]{1,0:T(8,128)(2,1)S(1)} collective-permute-done((bf16[96,512]{1,0:T(8,128)(2,1)S(1)}, bf16[96,512]{1,0:T(8,128)(2,1)S(1)}, u32[]{:S(2)}, u32[]{:S(2)}) %collective-permute-start.7) | collective-permute-done | bytes 98336 | tf_op jit(solution)/shard_map/ppermute | solution.py:477
  166.1 3.5 %all-to-all-start.8 = ((bf16[4,96,512]{2,1,0:T(8,128)(2,1)}), bf16[4,96,512]{2,1,0:T(8,128)(2,1)S(1)}, u32[]{:S(2)}, u32[]{:S(2)}) async-start(bf16[4,96,512]{2,1,0:T(8,128)(2,1)} %broadcast_in_dim.15), calls=%async_computation.8 | async-start | bytes 786432 | tf_op jit(solution)/shard_map/all_to_all | solution.py:460
  172.6 8.4 %collective-permute-done.9 = bf16[48,512]{1,0:T(8,128)(2,1)S(1)} collective-permute-done((bf16[48,512]{1,0:T(8,128)(2,1)S(1)}, bf16[48,512]{1,0:T(8,128)(2,1)S(1)}, u32[]{:S(2)}, u32[]{:S(2)}) %collective-permute-start.9) | collective-permute-done | bytes 49184 | tf_op jit(solution)/shard_map/ppermute | solution.py:477
  181.8 3.9 %collective-permute-done.10 = bf16[96,512]{1,0:T(8,128)(2,1)S(1)} collective-permute-done((bf16[96,512]{1,0:T(8,128)(2,1)S(1)}, bf16[96,512]{1,0:T(8,128)(2,1)S(1)}, u32[]{:S(2)}, u32[]{:S(2)}) %collective-permute-start.10) | collective-permute-done | bytes 98336 | tf_op jit(solution)/shard_map/ppermute | solution.py:477
  189.1 3.6 %all-to-all-start.9 = ((bf16[4,384,512]{2,1,0:T(8,128)(2,1)}), bf16[4,384,512]{2,1,0:T(8,128)(2,1)S(1)}, u32[]{:S(2)}, u32[]{:S(2)}) async-start(bf16[4,384,512]{2,1,0:T(8,128)(2,1)} %broadcast_in_dim.34), calls=%async_computation.9 | async-start | bytes 3145728 | tf_op jit(solution)/shard_map/all_to_all | solution.py:460
  193.3 7.8 %collective-permute-done.12 = bf16[384,512]{1,0:T(8,128)(2,1)S(1)} collective-permute-done((bf16[384,512]{1,0:T(8,128)(2,1)S(1)}, bf16[384,512]{1,0:T(8,128)(2,1)S(1)}, u32[]{:S(2)}, u32[]{:S(2)}) %collective-permute-start.12) | collective-permute-done | bytes 393248 | tf_op jit(solution)/shard_map/ppermute | solution.py:477
  201.5 6.9 %all-to-all-done.9 = bf16[4,384,512]{2,1,0:T(8,128)(2,1)S(1)} async-done(((bf16[4,384,512]{2,1,0:T(8,128)(2,1)}), bf16[4,384,512]{2,1,0:T(8,128)(2,1)S(1)}, u32[]{:S(2)}, u32[]{:S(2)}) %all-to-all-start.9) | async-done | bytes 1572896 | tf_op jit(solution)/shard_map/all_to_all | solution.py:460
  (83 shorter events, 52.6 us)
Async XLA Ops:
  6.1 16.9 %copy-start.3 = (bf16[512,512]{1,0:T(8,128)(2,1)S(1)}, bf16[512,512]{1,0:T(8,128)(2,1)}, u32[]{:S(2)}) copy-start(bf16[512,512]{1,0:T(8,128)(2,1)} %get-tuple-element.64) | copy-start | bytes 1572868
  6.1 16.9 %collective-permute-start = (bf16[512,512]{1,0:T(8,128)(2,1)S(1)}, bf16[512,512]{1,0:T(8,128)(2,1)S(1)}, u32[]{:S(2)}, u32[]{:S(2)}) collective-permute-start(bf16[512,512]{1,0:T(8,128)(2,1)S(1)} %get-tuple-element.65), channel_id=1, source_target_pairs={{0,1},{1,0},{2,3},{3,2},{4,5},{5,4},{6,7},{7,6},{8,9},{9,8},{10,11... | collective-permute-start | bytes 1572872 | tf_op jit(solution)/shard_map/ppermute | solution.py:477
  7.8 15.2 %all-to-all-start = ((bf16[32,4,512]{2,1,0:T(4,128)(2,1)}), bf16[32,4,512]{2,1,0:T(4,128)(2,1)S(1)}, u32[]{:S(2)}, u32[]{:S(2)}) async-start(bf16[32,4,512]{2,1,0:T(4,128)(2,1)} %reshape.129), calls=%async_computation | async-start | bytes 262144 | tf_op jit(solution)/shard_map/all_to_all | solution.py:585
  23.9 15.3 %all-to-all-start.1 = ((bf16[4,128,512]{2,1,0:T(8,128)(2,1)}), bf16[4,128,512]{2,1,0:T(8,128)(2,1)S(1)}, u32[]{:S(2)}, u32[]{:S(2)}) async-start(bf16[4,128,512]{2,1,0:T(8,128)(2,1)} %bitcast.8), calls=%async_computation.1 | async-start | bytes 1048576 | tf_op jit(solution)/shard_map/all_to_all | solution.py:460
  40.0 9.7 %all-to-all-start.2 = ((bf16[4,32,512]{2,1,0:T(8,128)(2,1)}), bf16[4,32,512]{2,1,0:T(8,128)(2,1)S(1)}, u32[]{:S(2)}, u32[]{:S(2)}) async-start(bf16[4,32,512]{2,1,0:T(8,128)(2,1)} %bitcast.9), calls=%async_computation.2 | async-start | bytes 262144 | tf_op jit(solution)/shard_map/all_to_all | solution.py:460
  66.5 10.7 %all-to-all-start.4 = ((bf16[4,128,512]{2,1,0:T(8,128)(2,1)}), bf16[4,128,512]{2,1,0:T(8,128)(2,1)S(1)}, u32[]{:S(2)}, u32[]{:S(2)}) async-start(bf16[4,128,512]{2,1,0:T(8,128)(2,1)} %broadcast_in_dim.14), calls=%async_computation.4 | async-start | bytes 1048576 | tf_op jit(solution)/shard_map/all_to_all | solution.py:460
  77.2 15.8 %collective-permute-start.1 = (bf16[512,512]{1,0:T(8,128)(2,1)S(1)}, bf16[512,512]{1,0:T(8,128)(2,1)S(1)}, u32[]{:S(2)}, u32[]{:S(2)}) collective-permute-start(bf16[512,512]{1,0:T(8,128)(2,1)S(1)} %bitcast.27), channel_id=1, source_target_pairs={{0,1},{1,0},{2,3},{3,2},{4,5},{5,4},{6,7},{7,6},{8,9},{9,8},{10,11... | collective-permute-start | bytes 1572872 | tf_op jit(solution)/shard_map/ppermute | solution.py:477
  101.6 12.7 %collective-permute-start.2 = (bf16[1552,512]{1,0:T(8,128)(2,1)}, bf16[1552,512]{1,0:T(8,128)(2,1)S(1)}, u32[]{:S(2)}, u32[]{:S(2)}) collective-permute-start(bf16[1552,512]{1,0:T(8,128)(2,1)} %get-tuple-element.77), channel_id=1, source_target_pairs={{0,1},{1,0},{2,3},{3,2},{4,5},{5,4},{6,7},{7,6},{8,9},{9,8},{10,11... | collective-permute-start | bytes 4767752 | tf_op jit(solution)/shard_map/ppermute | solution.py:477
  117.3 24.3 %all-to-all-start.6 = ((bf16[4,400,512]{2,1,0:T(8,128)(2,1)}), bf16[4,400,512]{2,1,0:T(8,128)(2,1)S(1)}, u32[]{:S(2)}, u32[]{:S(2)}) async-start(bf16[4,400,512]{2,1,0:T(8,128)(2,1)} %shard_map.258), calls=%async_computation.6 | async-start | bytes 3276800 | tf_op jit(solution)/shard_map/all_to_all | solution.py:460
  121.0 2.5 %collective-permute-start.4 = (bf16[768,512]{1,0:T(8,128)(2,1)S(1)}, bf16[768,512]{1,0:T(8,128)(2,1)}, u32[]{:S(2)}, u32[]{:S(2)}) collective-permute-start(bf16[768,512]{1,0:T(8,128)(2,1)S(1)} %copy-done.2), channel_id=1, source_target_pairs={{0,1},{1,0},{2,3},{3,2},{4,5},{5,4},{6,7},{7,6},{8,9},{9,8},{10,11... | collective-permute-start | bytes 2359304 | tf_op jit(solution)/shard_map/ppermute | solution.py:477
  125.7 20.3 %collective-permute-start.5 = (bf16[384,512]{1,0:T(8,128)(2,1)S(1)}, bf16[384,512]{1,0:T(8,128)(2,1)S(1)}, u32[]{:S(2)}, u32[]{:S(2)}) collective-permute-start(bf16[384,512]{1,0:T(8,128)(2,1)S(1)} %get-tuple-element.93), channel_id=1, source_target_pairs={{0,8},{1,9},{2,10},{3,11},{4,12},{5,13},{6,14},{7,15},{8,0},{9,1},... | collective-permute-start | bytes 1179656 | tf_op jit(solution)/shard_map/ppermute | solution.py:477
  142.5 22.1 %all-to-all-start.7 = ((bf16[4,112,512]{2,1,0:T(8,128)(2,1)}), bf16[4,112,512]{2,1,0:T(8,128)(2,1)S(1)}, u32[]{:S(2)}, u32[]{:S(2)}) async-start(bf16[4,112,512]{2,1,0:T(8,128)(2,1)} %shard_map.259), calls=%async_computation.7 | async-start | bytes 917504 | tf_op jit(solution)/shard_map/all_to_all | solution.py:460
  147.7 6.5 %collective-permute-start.6 = (bf16[192,512]{1,0:T(8,128)(2,1)S(1)}, bf16[192,512]{1,0:T(8,128)(2,1)S(1)}, u32[]{:S(2)}, u32[]{:S(2)}) collective-permute-start(bf16[192,512]{1,0:T(8,128)(2,1)S(1)} %get-tuple-element.95), channel_id=1, source_target_pairs={{0,4},{1,5},{2,6},{3,7},{4,0},{5,1},{6,2},{7,3},{8,12},{9,13},{10,... | collective-permute-start | bytes 589832 | tf_op jit(solution)/shard_map/ppermute | solution.py:477
  155.9 4.6 %collective-permute-start.7 = (bf16[96,512]{1,0:T(8,128)(2,1)S(1)}, bf16[96,512]{1,0:T(8,128)(2,1)S(1)}, u32[]{:S(2)}, u32[]{:S(2)}) collective-permute-start(bf16[96,512]{1,0:T(8,128)(2,1)S(1)} %get-tuple-element.97), channel_id=1, source_target_pairs={{0,2},{1,3},{2,0},{3,1},{4,6},{5,7},{6,4},{7,5},{8,10},{9,11},{10,... | collective-permute-start | bytes 294920 | tf_op jit(solution)/shard_map/ppermute | solution.py:477
  162.0 7.6 %collective-permute-start.8 = (bf16[48,512]{1,0:T(8,128)(2,1)S(1)}, bf16[48,512]{1,0:T(8,128)(2,1)S(1)}, u32[]{:S(2)}, u32[]{:S(2)}) collective-permute-start(bf16[48,512]{1,0:T(8,128)(2,1)S(1)} %get-tuple-element.99), channel_id=1, source_target_pairs={{0,16},{1,17},{2,18},{3,19},{4,20},{5,21},{6,22},{7,23},{8,24},{9,... | collective-permute-start | bytes 147464 | tf_op jit(solution)/shard_map/ppermute | solution.py:477
  166.1 21.7 %all-to-all-start.8 = ((bf16[4,96,512]{2,1,0:T(8,128)(2,1)}), bf16[4,96,512]{2,1,0:T(8,128)(2,1)S(1)}, u32[]{:S(2)}, u32[]{:S(2)}) async-start(bf16[4,96,512]{2,1,0:T(8,128)(2,1)} %broadcast_in_dim.15), calls=%async_computation.8 | async-start | bytes 786432 | tf_op jit(solution)/shard_map/all_to_all | solution.py:460
  169.7 11.3 %collective-permute-start.9 = (bf16[48,512]{1,0:T(8,128)(2,1)S(1)}, bf16[48,512]{1,0:T(8,128)(2,1)S(1)}, u32[]{:S(2)}, u32[]{:S(2)}) collective-permute-start(bf16[48,512]{1,0:T(8,128)(2,1)S(1)} %add_convert_fusion.1), channel_id=1, source_target_pairs={{0,16},{1,17},{2,18},{3,19},{4,20},{5,21},{6,22},{7,23},{8,24},{9,... | collective-permute-start | bytes 147464 | tf_op jit(solution)/shard_map/ppermute | solution.py:477
  181.0 4.7 %collective-permute-start.10 = (bf16[96,512]{1,0:T(8,128)(2,1)S(1)}, bf16[96,512]{1,0:T(8,128)(2,1)S(1)}, u32[]{:S(2)}, u32[]{:S(2)}) collective-permute-start(bf16[96,512]{1,0:T(8,128)(2,1)S(1)} %maximum_select_fusion.4), channel_id=1, source_target_pairs={{0,2},{1,3},{2,0},{3,1},{4,6},{5,7},{6,4},{7,5},{8,10},{9,11},{10,... | collective-permute-start | bytes 294920 | tf_op jit(solution)/shard_map/ppermute | solution.py:477
  185.7 7.4 %collective-permute-start.11 = (bf16[192,512]{1,0:T(8,128)(2,1)S(1)}, bf16[192,512]{1,0:T(8,128)(2,1)S(1)}, u32[]{:S(2)}, u32[]{:S(2)}) collective-permute-start(bf16[192,512]{1,0:T(8,128)(2,1)S(1)} %maximum_select_fusion.3), channel_id=1, source_target_pairs={{0,4},{1,5},{2,6},{3,7},{4,0},{5,1},{6,2},{7,3},{8,12},{9,13},{10,... | collective-permute-start | bytes 589832 | tf_op jit(solution)/shard_map/ppermute | solution.py:477
  189.1 19.3 %all-to-all-start.9 = ((bf16[4,384,512]{2,1,0:T(8,128)(2,1)}), bf16[4,384,512]{2,1,0:T(8,128)(2,1)S(1)}, u32[]{:S(2)}, u32[]{:S(2)}) async-start(bf16[4,384,512]{2,1,0:T(8,128)(2,1)} %broadcast_in_dim.34), calls=%async_computation.9 | async-start | bytes 3145728 | tf_op jit(solution)/shard_map/all_to_all | solution.py:460
  192.7 15.7 %copy-start.4 = (bf16[128,512]{1,0:T(8,128)(2,1)S(1)}, bf16[128,512]{1,0:T(8,128)(2,1)}, u32[]{:S(2)}) copy-start(bf16[128,512]{1,0:T(8,128)(2,1)} %reshape.136) | copy-start | bytes 393220
  193.3 7.8 %collective-permute-start.12 = (bf16[384,512]{1,0:T(8,128)(2,1)S(1)}, bf16[384,512]{1,0:T(8,128)(2,1)S(1)}, u32[]{:S(2)}, u32[]{:S(2)}) collective-permute-start(bf16[384,512]{1,0:T(8,128)(2,1)S(1)} %maximum_select_fusion.2), channel_id=1, source_target_pairs={{0,8},{1,9},{2,10},{3,11},{4,12},{5,13},{6,14},{7,15},{8,0},{9,1},... | collective-permute-start | bytes 1179656 | tf_op jit(solution)/shard_map/ppermute | solution.py:477
  201.4 9.5 %collective-permute-start.13 = (bf16[768,512]{1,0:T(8,128)(2,1)S(1)}, bf16[768,512]{1,0:T(8,128)(2,1)}, u32[]{:S(2)}, u32[]{:S(2)}) collective-permute-start(bf16[768,512]{1,0:T(8,128)(2,1)S(1)} %maximum_select_fusion.1), channel_id=1, source_target_pairs={{0,1},{1,0},{2,3},{3,2},{4,5},{5,4},{6,7},{7,6},{8,9},{9,8},{10,11... | collective-permute-start | bytes 2359304 | tf_op jit(solution)/shard_map/ppermute | solution.py:477
  208.4 10.4 %collective-permute-start.3 = (bf16[1536,512]{1,0:T(8,128)(2,1)S(1)}, bf16[1536,512]{1,0:T(8,128)(2,1)S(1)}, u32[]{:S(2)}, u32[]{:S(2)}) collective-permute-start(bf16[1536,512]{1,0:T(8,128)(2,1)S(1)} %bitcast.25), channel_id=1, source_target_pairs={{0,1},{1,0},{2,3},{3,2},{4,5},{5,4},{6,7},{7,6},{8,9},{9,8},{10,11... | collective-permute-start | bytes 4718600 | tf_op jit(solution)/shard_map/ppermute | solution.py:477
  (7 other events, 40.0 us)

commit v4 on v3

--- a/solution.py
+++ b/solution.py
@@ -14,6 +14,7 @@
 TAIL = 16
 EVERYONE = ("z", "x", "y", "core")
 VMEM_LIMIT = 24 * 1024 * 1024
+BIG_VMEM_LIMIT = 50 * 1024 * 1024
 
 
 def dot(a, b):
@@ -133,66 +134,57 @@
     split_rows(part, core[0], keep_ref, send_ref)
 
 
+def store_out(staging, target, sem):
+    copy = pltpu.make_async_copy(staging, target, sem)
+    copy.start()
+    return copy
+
+
 def edge_forward_kernel(
-    es, er, edge, halo, gain, w1_far, w2_far, node_far, coarse_far, p_ref, xs_ref, total_ref,
-    acc, w1, w2, node, coarse, sems,
+    es, er, halo, gain, w1_far, edge_far, node_far, coarse_far, w2_far,
+    p_far, xs_far, total_ref, w1, edge, node, coarse, w2, pre_out, xs_out, sems, out_sems,
 ):
-    step = pl.program_id(0)
     lat = edge.shape[1]
     n = node.shape[0]
     imports = halo.shape[0]
-    parts = [slice(k * lat, (k + 1) * lat) for k in (0, 2, 1)]
     first, last, middle = (
-        pltpu.make_async_copy(w1_far.at[part], w1.at[part], sems.at[k])
-        for k, part in enumerate(parts)
-    )
-    node_load = pltpu.make_async_copy(node_far, node, sems.at[3])
-    coarse_load = pltpu.make_async_copy(coarse_far, coarse, sems.at[4])
-    w2_load = pltpu.make_async_copy(w2_far, w2, sems.at[5])
-
-    @pl.when(step == 0)
-    def _():
-        for load in (first, node_load, last, coarse_load, middle, w2_load):
-            load.start()
-        acc[...] = jnp.zeros_like(acc)
-
+        pltpu.make_async_copy(
+            w1_far.at[k * lat : (k + 1) * lat], w1.at[k * lat : (k + 1) * lat], sems.at[5 + k]
+        )
+        for k in (0, 2, 1)
+    )
+    edge_load, node_load, coarse_load, w2_load = loads_of(
+        (edge_far, node_far, coarse_far, w2_far), (edge, node, coarse, w2), sems
+    )
+    for load in (node_load, last, edge_load, first, coarse_load, middle, w2_load):
+        load.start()
     sender = es[...]
     hot_r = onehot_t(er[...], n)
-
-    @pl.when(step == 0)
-    def _():
-        first.wait()
-
-    pre = dot(edge[...], w1[0:lat])
-
-    @pl.when(step == 0)
-    def _():
-        node_load.wait()
-        last.wait()
-
-    pre += dot(dot_lt(hot_r, node[...]).astype(BF), w1[2 * lat :])
-    xs = dot_lt(onehot_t(sender, n), node[...]) + dot_lt(
-        onehot_t(sender, imports, n), halo[...]
-    )
+    hot_n = onehot_t(sender, n)
+    node_load.wait()
+    xr = dot_lt(hot_r, node[...]).astype(BF)
+    xs = dot_lt(hot_n, node[...]) + dot_lt(onehot_t(sender, imports, n), halo[...])
+    last.wait()
+    pre = dot(xr, w1[2 * lat :])
+    edge_load.wait()
+    first.wait()
+    pre += dot(edge[...], w1[0:lat])
     hot_c = onehot_t(sender, coarse.shape[0], n + imports)
-
-    @pl.when(step == 0)
-    def _():
-        coarse_load.wait()
-        middle.wait()
-        w2_load.wait()
-
+    coarse_load.wait()
     xs = (xs + dot_lt(hot_c, coarse[...])).astype(BF)
+    xs_out[...] = xs
+    outs = [store_out(xs_out, xs_far, out_sems.at[0])]
+    middle.wait()
     pre += dot(xs, w1[lat : 2 * lat])
-    normed, _ = normalise(dot(hidden_of(pre), w2[...]))
+    pre_out[...] = pre
+    outs.append(store_out(pre_out, p_far, out_sems.at[1]))
+    hidden = hidden_of(pre)
+    w2_load.wait()
+    normed, _ = normalise(dot(hidden, w2[...]))
     new = (edge[...].astype(F32) + normed * gain[...]).astype(BF)
-    p_ref[...] = pre
-    xs_ref[...] = xs
-    acc[...] += dot(hot_r, new)
-
-    @pl.when(step == pl.num_programs(0) - 1)
-    def _():
-        total_ref[...] = acc[...].astype(BF)
+    total_ref[...] = dot(hot_r, new).astype(BF)
+    for out in outs:
+        out.wait()
 
 
 def node_kernel(
@@ -222,59 +214,56 @@
 
 
 def edge_backward_kernel(
-    es, er, edge, xs, pre_ref, ecot, gain, w2_far, fg_far, w1_far, node_far,
-    ge_ref, gw1_out, gw2_out, gg_ref, np_ref, ret_ref, cp_ref,
-    sum_s, sum_r, gw1, gw2, w2, fg, w1, node, sems,
+    es, er, gain, pre_far, w2_far, ecot_far, fg_far, w1_far, edge_far, xs_far, node_far,
+    gg_ref, ret_ref, ge_far, gw1_far, gw2_far, np_far, cp_far,
+    pre, w2, ecot, fg, w1, edge, xs, node, sems, ge, gw1, gw2, np_out, cp, out_sems,
 ):
-    step = pl.program_id(0)
     lat = edge.shape[1]
     n = node.shape[0]
     imports = ret_ref.shape[0]
-    loads = loads_of((w2_far, fg_far, w1_far, node_far), (w2, fg, w1, node), sems)
-
-    @pl.when(step == 0)
-    def _():
-        for load in loads:
-            load.start()
-        for ref in (sum_s, sum_r, gw1, gw2, gg_ref):
-            ref[...] = jnp.zeros_like(ref)
-
+    loads = loads_of(
+        (pre_far, w2_far, ecot_far, fg_far, w1_far, edge_far, xs_far, node_far),
+        (pre, w2, ecot, fg, w1, edge, xs, node),
+        sems,
+    )
+    for load in loads:
+        load.start()
     hot_r = onehot_t(er[...], n)
-    pre = pre_ref[...]
-    hidden = hidden_of(pre)
-
-    @pl.when(step == 0)
-    def _():
-        loads[0].wait()
-
+    loads[0].wait()
+    hidden = hidden_of(pre[...])
+    loads[1].wait()
     normed, inv_std = normalise(dot(hidden, w2[...]))
-
-    @pl.when(step == 0)
-    def _():
-        loads[1].wait()
-        loads[2].wait()
-
+    loads[2].wait()
+    loads[3].wait()
     cot = ecot[...].astype(F32) + gather_f32(hot_r, fg[...])
-    gain_part, d_proj, d_pre = grad_to_pre(pre, normed, inv_std, cot, gain[...], w2[...])
-    gg_ref[...] += gain_part
-    ge_ref[...] = cot + dot_rt(d_pre, w1[0:lat])
-    gw2[...] += dot_lt(hidden, d_proj)
-    gw1[0:lat] += dot_lt(edge[...], d_pre)
-    gw1[lat:] += dot_lt(xs[...], d_pre)
-    sum_r[...] += dot(hot_r, d_pre)
-    sum_s[...] += dot(onehot_t(es[...], sum_s.shape[0]), d_pre)
-
-    @pl.when(step == pl.num_programs(0) - 1)
-    def _():
-        loads[3].wait()
-        w_s = w1[lat : 2 * lat]
-        recv = sum_r[...].astype(BF)
-        gw2_out[...] = gw2[...].astype(BF)
-        gw1_out[0 : 2 * lat] = gw1[...].astype(BF)
-        gw1_out[2 * lat :] = dot_lt(node[...], recv).astype(BF)
-        np_ref[...] = dot_rt(sum_s[0:n].astype(BF), w_s) + dot_rt(recv, w1[2 * lat :])
-        ret_ref[...] = dot_rt(sum_s[n : n + imports].astype(BF), w_s).astype(BF)
-        cp_ref[...] = dot_rt(sum_s[n + imports :].astype(BF), w_s).astype(BF)
+    gain_part, d_proj, d_pre = grad_to_pre(pre[...], normed, inv_std, cot, gain[...], w2[...])
+    gg_ref[...] = gain_part
+    loads[4].wait()
+    ge[...] = cot + dot_rt(d_pre, w1[0:lat])
+    outs = [store_out(ge, ge_far, out_sems.at[0])]
+    loads[5].wait()
+    gw1[0:lat] = dot_lt(edge[...], d_pre).astype(BF)
+    loads[6].wait()
+    gw1[lat : 2 * lat] = dot_lt(xs[...], d_pre).astype(BF)
+    recv = dot(hot_r, d_pre).astype(BF)
+    loads[7].wait()
+    gw1[2 * lat :] = dot_lt(node[...], recv).astype(BF)
+    outs.append(store_out(gw1, gw1_far, out_sems.at[1]))
+    gw2[...] = dot_lt(hidden, d_proj).astype(BF)
+    outs.append(store_out(gw2, gw2_far, out_sems.at[2]))
+    w_s = w1[lat : 2 * lat]
+    sender = es[...]
+    count = cp.shape[0]
+    sums = dot(onehot_t(sender, count, n + imports), d_pre).astype(BF)
+    cp[...] = dot_rt(sums, w_s).astype(BF)
+    outs.append(store_out(cp, cp_far, out_sems.at[3]))
+    sums = dot(onehot_t(sender, n), d_pre).astype(BF)
+    np_out[...] = dot_rt(sums, w_s) + dot_rt(recv, w1[2 * lat :])
+    outs.append(store_out(np_out, np_far, out_sems.at[4]))
+    sums = dot(onehot_t(sender, imports, n), d_pre).astype(BF)
+    ret_ref[...] = dot_rt(sums, w_s).astype(BF)
+    for out in outs:
+        out.wait()
 
 
 def coarse_kernel(
@@ -412,10 +401,8 @@
     widen_kernel(core, half, coarse_ref, first_ref, second_ref, scale=scale)
 
 
-def params(*semantics):
-    return pltpu.CompilerParams(
-        dimension_semantics=semantics or None, vmem_limit_bytes=VMEM_LIMIT
-    )
+def params(*semantics, limit=VMEM_LIMIT):
+    return pltpu.CompilerParams(dimension_semantics=semantics or None, vmem_limit_bytes=limit)
 
 
 def cost(micros):
@@ -601,24 +588,19 @@
 
     coarse_total = reduce_rows(keep, send)
 
-    tile = math.gcd(ecount, 256)
-    steps = ecount // tile
-    rows_spec = pl.BlockSpec((tile, lat), lambda i: (i, 0))
-    index_spec = pl.BlockSpec((1, tile), lambda i: (0, i))
-    fixed = lambda r, c: pl.BlockSpec((r, c), lambda i: (0, 0))
+    edge_args = (w1, edge, node, coarse, w2)
+    staging = [far(ecount, width, F32), far(ecount, lat, BF)]
     pre, xs, fine_total = pl.pallas_call(
         edge_forward_kernel,
-        grid=(steps,),
-        in_specs=[index_spec, index_spec, rows_spec] + [IN_VMEM] * 2 + [IN_HBM] * 4,
-        out_specs=[pl.BlockSpec((tile, width), lambda i: (i, 0)), rows_spec, fixed(n, lat)],
-        out_shape=(far(ecount, width, F32), far(ecount, lat, BF), far(n, lat, BF)),
-        scratch_shapes=[pltpu.VMEM((n, lat), F32)]
-        + buffers(w1, w2, node, coarse)[:-1]
-        + [pltpu.SemaphoreType.DMA((6,))],
-        compiler_params=params("arbitrary"),
+        in_specs=[IN_VMEM] * 4 + [IN_HBM] * 5,
+        out_specs=[IN_HBM] * 2 + [IN_VMEM],
+        out_shape=(*staging, far(n, lat, BF)),
+        scratch_shapes=buffers(*edge_args, *staging)[:-1]
+        + [pltpu.SemaphoreType.DMA((8,)), pltpu.SemaphoreType.DMA((2,))],
+        compiler_params=params(limit=BIG_VMEM_LIMIT),
         cost_estimate=cost(9.0),
         name="edge_forward",
-    )(es, er, *in_far(edge), halo, gain_row, *in_far(w1, w2, node, coarse))
+    )(es, er, halo, gain_row, *in_far(*edge_args))
 
     fine_grad, grad_n, ngw1, ngw2, ngg = pl.pallas_call(
         node_kernel,
@@ -633,33 +615,21 @@
         name="node_mlp",
     )(*in_far(node, fine_total), ngain_row, *in_far(ncot, nw1, nw2))
 
-    grad_e, gw1, gw2, gg, node_part, returning, coarse_local = pl.pallas_call(
+    edge_args = (pre, w2, ecot, fine_grad, w1, edge, xs, node)
+    staging = [
+        far(ecount, lat, F32), far(3 * lat, width, BF), far(width, lat, BF), far(n, lat, F32),
+        far(ccount, lat, BF),
+    ]
+    gg, returning, grad_e, gw1, gw2, node_part, coarse_local = pl.pallas_call(
         edge_backward_kernel,
-        grid=(steps,),
-        in_specs=[
-            index_spec, index_spec, rows_spec, rows_spec,
-            pl.BlockSpec((tile, width), lambda i: (i, 0)), rows_spec,
-        ]
-        + [IN_VMEM]
-        + [IN_HBM] * 4,
-        out_specs=[
-            rows_spec, fixed(3 * lat, width), fixed(width, lat), fixed(1, lat), fixed(n, lat),
-            fixed(imports, lat), fixed(ccount, lat),
-        ],
-        out_shape=(
-            far(ecount, lat, F32), far(3 * lat, width, BF), far(width, lat, BF),
-            shape(1, lat, F32), far(n, lat, F32), shape(imports, lat, BF),
-            far(ccount, lat, BF),
-        ),
-        scratch_shapes=[
-            pltpu.VMEM((n + imports + ccount, width), F32), pltpu.VMEM((n, width), F32),
-            pltpu.VMEM((2 * lat, width), F32), pltpu.VMEM((width, lat), F32),
-        ]
-        + buffers(w2, fine_grad, w1, node),
-        compiler_params=params("arbitrary"),
+        in_specs=[IN_VMEM] * 3 + [IN_HBM] * 8,
+        out_specs=[IN_VMEM] * 2 + [IN_HBM] * 5,
+        out_shape=(shape(1, lat, F32), shape(imports, lat, BF), *staging),
+        scratch_shapes=buffers(*edge_args) + buffers(*staging),
+        compiler_params=params(limit=BIG_VMEM_LIMIT),
         cost_estimate=cost(15.0),
         name="edge_backward",
-    )(es, er, *in_far(edge, xs, pre, ecot), gain_row, *in_far(w2, fine_grad, w1, node))
+    )(es, er, gain_row, *in_far(*edge_args))
 
     returned = lax.all_to_all(
         returning.reshape(devices, slots, lat), EVERYONE, 0, 0, tiled=True

time: 222 us -> 215 us (0.968)
  Pallas kernels: 66.6 us -> 60.1 us
    pallas_call x2, Pallas kernels: 27.6 us -> 21.1 us  [the longest x1 12.5 us: per_device(): pl.pallas_call(edge_backward_kernel, in_specs=[IN_VMEM] * 3 + [IN_HBM] *...]
  transfers between devices with their start and end apart: 22 -> 22, of which waited for: 12 -> 12; matrix products, arithmetic and copies ran while one was open for 6% -> 6% of each run, Pallas kernels for 19% -> 17%
where the time goes in v4:
time: 215 us; the launch traced here: 214 us
  waiting for transfers between devices  67.9 us (32%)
  Pallas kernels  60.1 us (28%)
  starting transfers between devices  45.5 us (21%)
  blocking collectives  21.5 us (10%)
  other arithmetic  8.39 us (4%)
  local copies, waits for them, and re-layouts  6.92 us (3%)
  matrix products  2.72 us (1%)
    ppermute x14, waiting for transfers between devices, exchange(): return lax.ppermute(x, EVERYONE, [(i, i ^ mask) for i in range(devices)])  31.3 us
    all_to_all x7, waiting for transfers between devices, swap(): return lax.all_to_all(x, axes, 0, 0, tiled=True)  29.2 us
    all_to_all x7, starting transfers between devices, swap(): return lax.all_to_all(x, axes, 0, 0, tiled=True)  25.3 us
    ppermute x14, starting transfers between devices, exchange(): return lax.ppermute(x, EVERYONE, [(i, i ^ mask) for i in range(devices)])  13.2 us
    pallas_call x1, Pallas kernels, per_device(): pl.pallas_call(edge_backward_kernel, in_specs=[IN_VMEM] * 3 + [IN_HBM] *...  12.5 us
    all_to_all x1, blocking collectives, per_device(): lax.all_to_all(returning.reshape(devices, slots, lat), EVERYONE, 0, 0, ti...  11.4 us
    all_to_all x1, blocking collectives, swap(): return lax.all_to_all(x, axes, 0, 0, tiled=True)  10.2 us
    pallas_call x1, Pallas kernels, per_device(): pl.pallas_call(edge_forward_kernel, in_specs=[IN_VMEM] * 4 + [IN_HBM] * 5...  8.61 us
  transfers between devices with their start and end apart: 22, of which 12 were waited for; matrix products, arithmetic and copies ran while one was open for 6% of the time, Pallas kernels for 17%

profile of v4, /device:TPU:0, one launch (start us, length us, event | category | flops | bytes accessed | tf_op | source)
XLA Modules:
  0.0 214.0 jit_solution(15976668191155654766)
XLA Ops:
  0.7 5.4 %up_forward.1 = (f32[256,512]{1,0:T(8,128)}, bf16[256,512]{1,0:T(8,128)(2,1)}, bf16[256,512]{1,0:T(8,128)(2,1)}, bf16[512,512]{1,0:T(8,128)(2,1)}, bf16[512,512]{1,0:T(8,128)(2,1)S(1)}) custom-call(s32[1,256]{1,0:T(1,128)} %bitcast.43, s32[1,256]{1,0:T(1,128)} %bitcast.45, s32[1]{0:T(128)} %bitcast.7.core, bf16[256,512]{1,0:T(8,128)(2,1)} %up.3, ...), custom_call_target="tpu_custom_call" | custom-call | flops 5500000256 | bytes 15000000 | tf_op jit(solution)/shard_map/up_forward/pallas_call | solution.py:576
  7.8 6.9 %all-to-all-start = ((bf16[32,4,512]{2,1,0:T(4,128)(2,1)}), bf16[32,4,512]{2,1,0:T(4,128)(2,1)S(1)}, u32[]{:S(2)}, u32[]{:S(2)}) async-start(bf16[32,4,512]{2,1,0:T(4,128)(2,1)} %reshape.129), calls=%async_computation | async-start | bytes 262144 | tf_op jit(solution)/shard_map/all_to_all | solution.py:572
  15.5 7.4 %all-to-all-done = bf16[32,4,512]{2,1,0:T(4,128)(2,1)S(1)} async-done(((bf16[32,4,512]{2,1,0:T(4,128)(2,1)}), bf16[32,4,512]{2,1,0:T(4,128)(2,1)S(1)}, u32[]{:S(2)}, u32[]{:S(2)}) %all-to-all-start) | async-done | bytes 131104 | tf_op jit(solution)/shard_map/all_to_all | solution.py:572
  23.9 3.5 %all-to-all-start.1 = ((bf16[4,128,512]{2,1,0:T(8,128)(2,1)}), bf16[4,128,512]{2,1,0:T(8,128)(2,1)S(1)}, u32[]{:S(2)}, u32[]{:S(2)}) async-start(bf16[4,128,512]{2,1,0:T(8,128)(2,1)} %bitcast.8), calls=%async_computation.1 | async-start | bytes 1048576 | tf_op jit(solution)/shard_map/all_to_all | solution.py:447
  27.4 8.6 %edge_forward.1 = (f32[1024,512]{1,0:T(8,128)}, bf16[1024,512]{1,0:T(8,128)(2,1)}, bf16[256,512]{1,0:T(8,128)(2,1)}) custom-call(s32[1,1024]{1,0:T(1,128)} %bitcast.33, s32[1,1024]{1,0:T(1,128)} %bitcast.35, bf16[128,512]{1,0:T(8,128)(2,1)S(1)} %reshape.130.halo, f32[1,512]{1,0:T(1,128)} %bitcast.40, bf16[1536,512]{1,0:T(8,128)(2,1)} %w1_far.7, ...), custom_call_target="tpu_custom_call" | custom-call | flops 9900000256 | bytes 27000000 | tf_op jit(solution)/shard_map/edge_forward/pallas_call | solution.py:593
  40.1 5.6 %node_mlp.1 = (f32[256,512]{1,0:T(8,128)}, f32[256,512]{1,0:T(8,128)}, bf16[1024,512]{1,0:T(8,128)(2,1)}, bf16[512,512]{1,0:T(8,128)(2,1)}, f32[1,512]{1,0:T(1,128)S(1)}) custom-call(bf16[256,512]{1,0:T(8,128)(2,1)} %node_far.5, bf16[256,512]{1,0:T(8,128)(2,1)} %get-tuple-element.55.total_in, f32[1,512]{1,0:T(1,128)} %bitcast.37, bf16[256,512]{1,0:T(8,128)(2,1)} %ncot.1, ...), custom_call_target="tpu_custom_call" | custom-call | flops 5500000256 | bytes 15000000 | tf_op jit(solution)/shard_map/node_mlp/pallas_call | solution.py:605
  46.6 4.9 %coarse_mlp.1 = (bf16[32,512]{1,0:T(8,128)(2,1)S(1)}, f32[32,512]{1,0:T(8,128)}, bf16[768,512]{1,0:T(8,128)(2,1)}, bf16[768,512]{1,0:T(8,128)(2,1)S(1)}, f32[1,512]{1,0:T(1,128)S(1)}) custom-call(s32[1]{0:T(128)} %bitcast.7.core, bf16[32,512]{1,0:T(8,128)(2,1)S(1)} %constant_dynamic-slice_fusion.1.rows, f32[32,512]{1,0:T(8,128)S(1)} %convert_reduce_fusion.1.total_in, ...), custom_call_target="tpu_custom_call" | custom-call | flops 5500000256 | bytes 15000000 | tf_op jit(solution)/shard_map/coarse_mlp/pallas_call | solution.py:644
  52.4 10.2 %all_to_all.68 = bf16[4,32,512]{2,1,0:T(8,128)(2,1)S(1)} all-to-all(bf16[4,32,512]{2,1,0:T(8,128)(2,1)S(1)} %broadcast_in_dim.12), channel_id=1, replica_groups=mesh['z'=4,'x'=2,'y'=2,'core'=2] {'z'}, dimensions={0} | all-to-all | bytes 262144 | tf_op jit(solution)/shard_map/all_to_all | solution.py:447
  63.4 4.1 %all-to-all-start.4 = ((bf16[4,128,512]{2,1,0:T(8,128)(2,1)}), bf16[4,128,512]{2,1,0:T(8,128)(2,1)S(1)}, u32[]{:S(2)}, u32[]{:S(2)}) async-start(bf16[4,128,512]{2,1,0:T(8,128)(2,1)} %broadcast_in_dim.14), calls=%async_computation.4 | async-start | bytes 1048576 | tf_op jit(solution)/shard_map/all_to_all | solution.py:447
  67.6 6.5 %all-to-all-done.4 = bf16[4,128,512]{2,1,0:T(8,128)(2,1)S(1)} async-done(((bf16[4,128,512]{2,1,0:T(8,128)(2,1)}), bf16[4,128,512]{2,1,0:T(8,128)(2,1)S(1)}, u32[]{:S(2)}, u32[]{:S(2)}) %all-to-all-start.4) | async-done | bytes 524320 | tf_op jit(solution)/shard_map/all_to_all | solution.py:447
  74.1 12.5 %edge_backward.1 = (f32[1,512]{1,0:T(1,128)S(1)}, bf16[128,512]{1,0:T(8,128)(2,1)S(1)}, f32[1024,512]{1,0:T(8,128)}, bf16[1536,512]{1,0:T(8,128)(2,1)}, bf16[512...) custom-call(s32[1,1024]{1,0:T(1,128)} %bitcast.34, s32[1,1024]{1,0:T(1,128)} %bitcast.36, ...), custom_call_target="tpu_custom_call" | custom-call | flops 16499999744 | bytes 45000000 | tf_op jit(solution)/shard_map/edge_backward/pallas_call | solution.py:623
  86.6 8.5 %up_backward.1 = (f32[256,512]{1,0:T(8,128)}, f32[256,512]{1,0:T(8,128)}, bf16[1552,512]{1,0:T(8,128)(2,1)}, bf16[1552,512]{1,0:T(8,128)(2,1)}) custom-call(s32[1,256]{1,0:T(1,128)} %bitcast.44, s32[1,256]{1,0:T(1,128)} %bitcast.46, s32[2]{0:T(128)S(1)} %pad_add_fusion.place, bf16[256,512]{1,0:T(8,128)(2,1)} %up.3, bf16[256,512]{1,0:T(8,128)(2,1)} %get-tuple-element.61.xs, ...), custom_call_target="tpu_custom_call" | custom-call | flops 8800000000 | bytes 24000000 | tf_op jit(solution)/shard_map/up_backward/pallas_call | solution.py:664
  95.7 11.4 %all_to_all.69 = bf16[32,4,512]{2,1,0:T(4,128)(2,1)S(1)} all-to-all(bf16[32,4,512]{2,1,0:T(4,128)(2,1)S(1)} %reshape.135), channel_id=1, replica_groups=mesh['z'=4,'x'=2,'y'=2,'core'=2] {'z','x','y','core'}, dimensions={0} | all-to-all | bytes 262144 | tf_op jit(solution)/shard_map/all_to_all | solution.py:634
  110.7 3.9 %all-to-all-start.6 = ((bf16[4,400,512]{2,1,0:T(8,128)(2,1)}), bf16[4,400,512]{2,1,0:T(8,128)(2,1)S(1)}, u32[]{:S(2)}, u32[]{:S(2)}) async-start(bf16[4,400,512]{2,1,0:T(8,128)(2,1)} %shard_map.258), calls=%async_computation.6 | async-start | bytes 3276800 | tf_op jit(solution)/shard_map/all_to_all | solution.py:447
  120.0 15.0 %all-to-all-done.6.got = bf16[4,400,512]{2,1,0:T(8,128)(2,1)S(1)} async-done(((bf16[4,400,512]{2,1,0:T(8,128)(2,1)}), bf16[4,400,512]{2,1,0:T(8,128)(2,1)S(1)}, u32[]{:S(2)}, u32[]{:S(2)}) %all-to-all-start.6) | async-done | bytes 1638432 | tf_op jit(solution)/shard_map/all_to_all | solution.py:447
  136.0 3.5 %all-to-all-start.7 = ((bf16[4,112,512]{2,1,0:T(8,128)(2,1)}), bf16[4,112,512]{2,1,0:T(8,128)(2,1)S(1)}, u32[]{:S(2)}, u32[]{:S(2)}) async-start(bf16[4,112,512]{2,1,0:T(8,128)(2,1)} %shard_map.259), calls=%async_computation.7 | async-start | bytes 917504 | tf_op jit(solution)/shard_map/all_to_all | solution.py:447
  142.6 5.1 %collective-permute-done.6.recv = bf16[192,512]{1,0:T(8,128)(2,1)S(1)} collective-permute-done((bf16[192,512]{1,0:T(8,128)(2,1)S(1)}, bf16[192,512]{1,0:T(8,128)(2,1)S(1)}, u32[]{:S(2)}, u32[]{:S(2)}) %collective-permute-start.6) | collective-permute-done | bytes 196640 | tf_op jit(solution)/shard_map/ppermute | solution.py:464
  150.4 3.5 %collective-permute-done.7.recv = bf16[96,512]{1,0:T(8,128)(2,1)S(1)} collective-permute-done((bf16[96,512]{1,0:T(8,128)(2,1)S(1)}, bf16[96,512]{1,0:T(8,128)(2,1)S(1)}, u32[]{:S(2)}, u32[]{:S(2)}) %collective-permute-start.7) | collective-permute-done | bytes 98336 | tf_op jit(solution)/shard_map/ppermute | solution.py:464
  159.6 3.5 %all-to-all-start.8 = ((bf16[4,96,512]{2,1,0:T(8,128)(2,1)}), bf16[4,96,512]{2,1,0:T(8,128)(2,1)S(1)}, u32[]{:S(2)}, u32[]{:S(2)}) async-start(bf16[4,96,512]{2,1,0:T(8,128)(2,1)} %broadcast_in_dim.15), calls=%async_computation.8 | async-start | bytes 786432 | tf_op jit(solution)/shard_map/all_to_all | solution.py:447
  166.0 8.4 %collective-permute-done.9 = bf16[48,512]{1,0:T(8,128)(2,1)S(1)} collective-permute-done((bf16[48,512]{1,0:T(8,128)(2,1)S(1)}, bf16[48,512]{1,0:T(8,128)(2,1)S(1)}, u32[]{:S(2)}, u32[]{:S(2)}) %collective-permute-start.9) | collective-permute-done | bytes 49184 | tf_op jit(solution)/shard_map/ppermute | solution.py:464
  175.2 3.9 %collective-permute-done.10 = bf16[96,512]{1,0:T(8,128)(2,1)S(1)} collective-permute-done((bf16[96,512]{1,0:T(8,128)(2,1)S(1)}, bf16[96,512]{1,0:T(8,128)(2,1)S(1)}, u32[]{:S(2)}, u32[]{:S(2)}) %collective-permute-start.10) | collective-permute-done | bytes 98336 | tf_op jit(solution)/shard_map/ppermute | solution.py:464
  182.6 3.6 %all-to-all-start.9 = ((bf16[4,384,512]{2,1,0:T(8,128)(2,1)}), bf16[4,384,512]{2,1,0:T(8,128)(2,1)S(1)}, u32[]{:S(2)}, u32[]{:S(2)}) async-start(bf16[4,384,512]{2,1,0:T(8,128)(2,1)} %broadcast_in_dim.34), calls=%async_computation.9 | async-start | bytes 3145728 | tf_op jit(solution)/shard_map/all_to_all | solution.py:447
  186.8 7.8 %collective-permute-done.12 = bf16[384,512]{1,0:T(8,128)(2,1)S(1)} collective-permute-done((bf16[384,512]{1,0:T(8,128)(2,1)S(1)}, bf16[384,512]{1,0:T(8,128)(2,1)S(1)}, u32[]{:S(2)}, u32[]{:S(2)}) %collective-permute-start.12) | collective-permute-done | bytes 393248 | tf_op jit(solution)/shard_map/ppermute | solution.py:464
  195.0 6.9 %all-to-all-done.9 = bf16[4,384,512]{2,1,0:T(8,128)(2,1)S(1)} async-done(((bf16[4,384,512]{2,1,0:T(8,128)(2,1)}), bf16[4,384,512]{2,1,0:T(8,128)(2,1)S(1)}, u32[]{:S(2)}, u32[]{:S(2)}) %all-to-all-start.9) | async-done | bytes 1572896 | tf_op jit(solution)/shard_map/all_to_all | solution.py:447
  (83 shorter events, 52.6 us)
Async XLA Ops:
  6.1 16.9 %copy-start.3 = (bf16[512,512]{1,0:T(8,128)(2,1)S(1)}, bf16[512,512]{1,0:T(8,128)(2,1)}, u32[]{:S(2)}) copy-start(bf16[512,512]{1,0:T(8,128)(2,1)} %get-tuple-element.64) | copy-start | bytes 1572868
  6.1 16.9 %collective-permute-start = (bf16[512,512]{1,0:T(8,128)(2,1)S(1)}, bf16[512,512]{1,0:T(8,128)(2,1)S(1)}, u32[]{:S(2)}, u32[]{:S(2)}) collective-permute-start(bf16[512,512]{1,0:T(8,128)(2,1)S(1)} %get-tuple-element.65), channel_id=1, source_target_pairs={{0,1},{1,0},{2,3},{3,2},{4,5},{5,4},{6,7},{7,6},{8,9},{9,8},{10,11... | collective-permute-start | bytes 1572872 | tf_op jit(solution)/shard_map/ppermute | solution.py:464
  7.8 15.2 %all-to-all-start = ((bf16[32,4,512]{2,1,0:T(4,128)(2,1)}), bf16[32,4,512]{2,1,0:T(4,128)(2,1)S(1)}, u32[]{:S(2)}, u32[]{:S(2)}) async-start(bf16[32,4,512]{2,1,0:T(4,128)(2,1)} %reshape.129), calls=%async_computation | async-start | bytes 262144 | tf_op jit(solution)/shard_map/all_to_all | solution.py:572
  23.9 12.1 %all-to-all-start.1 = ((bf16[4,128,512]{2,1,0:T(8,128)(2,1)}), bf16[4,128,512]{2,1,0:T(8,128)(2,1)S(1)}, u32[]{:S(2)}, u32[]{:S(2)}) async-start(bf16[4,128,512]{2,1,0:T(8,128)(2,1)} %bitcast.8), calls=%async_computation.1 | async-start | bytes 1048576 | tf_op jit(solution)/shard_map/all_to_all | solution.py:447
  36.8 9.7 %all-to-all-start.2 = ((bf16[4,32,512]{2,1,0:T(8,128)(2,1)}), bf16[4,32,512]{2,1,0:T(8,128)(2,1)S(1)}, u32[]{:S(2)}, u32[]{:S(2)}) async-start(bf16[4,32,512]{2,1,0:T(8,128)(2,1)} %bitcast.9), calls=%async_computation.2 | async-start | bytes 262144 | tf_op jit(solution)/shard_map/all_to_all | solution.py:447
  63.4 10.7 %all-to-all-start.4 = ((bf16[4,128,512]{2,1,0:T(8,128)(2,1)}), bf16[4,128,512]{2,1,0:T(8,128)(2,1)S(1)}, u32[]{:S(2)}, u32[]{:S(2)}) async-start(bf16[4,128,512]{2,1,0:T(8,128)(2,1)} %broadcast_in_dim.14), calls=%async_computation.4 | async-start | bytes 1048576 | tf_op jit(solution)/shard_map/all_to_all | solution.py:447
  74.1 12.5 %collective-permute-start.1 = (bf16[512,512]{1,0:T(8,128)(2,1)S(1)}, bf16[512,512]{1,0:T(8,128)(2,1)S(1)}, u32[]{:S(2)}, u32[]{:S(2)}) collective-permute-start(bf16[512,512]{1,0:T(8,128)(2,1)S(1)} %bitcast.27), channel_id=1, source_target_pairs={{0,1},{1,0},{2,3},{3,2},{4,5},{5,4},{6,7},{7,6},{8,9},{9,8},{10,11... | collective-permute-start | bytes 1572872 | tf_op jit(solution)/shard_map/ppermute | solution.py:464
  95.1 12.7 %collective-permute-start.2 = (bf16[1552,512]{1,0:T(8,128)(2,1)}, bf16[1552,512]{1,0:T(8,128)(2,1)S(1)}, u32[]{:S(2)}, u32[]{:S(2)}) collective-permute-start(bf16[1552,512]{1,0:T(8,128)(2,1)} %get-tuple-element.77), channel_id=1, source_target_pairs={{0,1},{1,0},{2,3},{3,2},{4,5},{5,4},{6,7},{7,6},{8,9},{9,8},{10,11... | collective-permute-start | bytes 4767752 | tf_op jit(solution)/shard_map/ppermute | solution.py:464
  110.7 24.3 %all-to-all-start.6 = ((bf16[4,400,512]{2,1,0:T(8,128)(2,1)}), bf16[4,400,512]{2,1,0:T(8,128)(2,1)S(1)}, u32[]{:S(2)}, u32[]{:S(2)}) async-start(bf16[4,400,512]{2,1,0:T(8,128)(2,1)} %shard_map.258), calls=%async_computation.6 | async-start | bytes 3276800 | tf_op jit(solution)/shard_map/all_to_all | solution.py:447
  114.7 2.5 %collective-permute-start.4 = (bf16[768,512]{1,0:T(8,128)(2,1)S(1)}, bf16[768,512]{1,0:T(8,128)(2,1)}, u32[]{:S(2)}, u32[]{:S(2)}) collective-permute-start(bf16[768,512]{1,0:T(8,128)(2,1)S(1)} %copy-done.2), channel_id=1, source_target_pairs={{0,1},{1,0},{2,3},{3,2},{4,5},{5,4},{6,7},{7,6},{8,9},{9,8},{10,11... | collective-permute-start | bytes 2359304 | tf_op jit(solution)/shard_map/ppermute | solution.py:464
  119.4 20.1 %collective-permute-start.5 = (bf16[384,512]{1,0:T(8,128)(2,1)S(1)}, bf16[384,512]{1,0:T(8,128)(2,1)S(1)}, u32[]{:S(2)}, u32[]{:S(2)}) collective-permute-start(bf16[384,512]{1,0:T(8,128)(2,1)S(1)} %get-tuple-element.93), channel_id=1, source_target_pairs={{0,8},{1,9},{2,10},{3,11},{4,12},{5,13},{6,14},{7,15},{8,0},{9,1},... | collective-permute-start | bytes 1179656 | tf_op jit(solution)/shard_map/ppermute | solution.py:464
  136.0 22.1 %all-to-all-start.7 = ((bf16[4,112,512]{2,1,0:T(8,128)(2,1)}), bf16[4,112,512]{2,1,0:T(8,128)(2,1)S(1)}, u32[]{:S(2)}, u32[]{:S(2)}) async-start(bf16[4,112,512]{2,1,0:T(8,128)(2,1)} %shard_map.259), calls=%async_computation.7 | async-start | bytes 917504 | tf_op jit(solution)/shard_map/all_to_all | solution.py:447
  141.2 6.5 %collective-permute-start.6 = (bf16[192,512]{1,0:T(8,128)(2,1)S(1)}, bf16[192,512]{1,0:T(8,128)(2,1)S(1)}, u32[]{:S(2)}, u32[]{:S(2)}) collective-permute-start(bf16[192,512]{1,0:T(8,128)(2,1)S(1)} %get-tuple-element.95), channel_id=1, source_target_pairs={{0,4},{1,5},{2,6},{3,7},{4,0},{5,1},{6,2},{7,3},{8,12},{9,13},{10,... | collective-permute-start | bytes 589832 | tf_op jit(solution)/shard_map/ppermute | solution.py:464
  149.3 4.6 %collective-permute-start.7 = (bf16[96,512]{1,0:T(8,128)(2,1)S(1)}, bf16[96,512]{1,0:T(8,128)(2,1)S(1)}, u32[]{:S(2)}, u32[]{:S(2)}) collective-permute-start(bf16[96,512]{1,0:T(8,128)(2,1)S(1)} %get-tuple-element.97), channel_id=1, source_target_pairs={{0,2},{1,3},{2,0},{3,1},{4,6},{5,7},{6,4},{7,5},{8,10},{9,11},{10,... | collective-permute-start | bytes 294920 | tf_op jit(solution)/shard_map/ppermute | solution.py:464
  155.5 7.6 %collective-permute-start.8 = (bf16[48,512]{1,0:T(8,128)(2,1)S(1)}, bf16[48,512]{1,0:T(8,128)(2,1)S(1)}, u32[]{:S(2)}, u32[]{:S(2)}) collective-permute-start(bf16[48,512]{1,0:T(8,128)(2,1)S(1)} %get-tuple-element.99), channel_id=1, source_target_pairs={{0,16},{1,17},{2,18},{3,19},{4,20},{5,21},{6,22},{7,23},{8,24},{9,... | collective-permute-start | bytes 147464 | tf_op jit(solution)/shard_map/ppermute | solution.py:464
  159.6 21.7 %all-to-all-start.8 = ((bf16[4,96,512]{2,1,0:T(8,128)(2,1)}), bf16[4,96,512]{2,1,0:T(8,128)(2,1)S(1)}, u32[]{:S(2)}, u32[]{:S(2)}) async-start(bf16[4,96,512]{2,1,0:T(8,128)(2,1)} %broadcast_in_dim.15), calls=%async_computation.8 | async-start | bytes 786432 | tf_op jit(solution)/shard_map/all_to_all | solution.py:447
  163.1 11.3 %collective-permute-start.9 = (bf16[48,512]{1,0:T(8,128)(2,1)S(1)}, bf16[48,512]{1,0:T(8,128)(2,1)S(1)}, u32[]{:S(2)}, u32[]{:S(2)}) collective-permute-start(bf16[48,512]{1,0:T(8,128)(2,1)S(1)} %add_convert_fusion.1), channel_id=1, source_target_pairs={{0,16},{1,17},{2,18},{3,19},{4,20},{5,21},{6,22},{7,23},{8,24},{9,... | collective-permute-start | bytes 147464 | tf_op jit(solution)/shard_map/ppermute | solution.py:464
  174.4 4.7 %collective-permute-start.10 = (bf16[96,512]{1,0:T(8,128)(2,1)S(1)}, bf16[96,512]{1,0:T(8,128)(2,1)S(1)}, u32[]{:S(2)}, u32[]{:S(2)}) collective-permute-start(bf16[96,512]{1,0:T(8,128)(2,1)S(1)} %maximum_select_fusion.4), channel_id=1, source_target_pairs={{0,2},{1,3},{2,0},{3,1},{4,6},{5,7},{6,4},{7,5},{8,10},{9,11},{10,... | collective-permute-start | bytes 294920 | tf_op jit(solution)/shard_map/ppermute | solution.py:464
  179.2 7.4 %collective-permute-start.11 = (bf16[192,512]{1,0:T(8,128)(2,1)S(1)}, bf16[192,512]{1,0:T(8,128)(2,1)S(1)}, u32[]{:S(2)}, u32[]{:S(2)}) collective-permute-start(bf16[192,512]{1,0:T(8,128)(2,1)S(1)} %maximum_select_fusion.3), channel_id=1, source_target_pairs={{0,4},{1,5},{2,6},{3,7},{4,0},{5,1},{6,2},{7,3},{8,12},{9,13},{10,... | collective-permute-start | bytes 589832 | tf_op jit(solution)/shard_map/ppermute | solution.py:464
  182.6 19.3 %all-to-all-start.9 = ((bf16[4,384,512]{2,1,0:T(8,128)(2,1)}), bf16[4,384,512]{2,1,0:T(8,128)(2,1)S(1)}, u32[]{:S(2)}, u32[]{:S(2)}) async-start(bf16[4,384,512]{2,1,0:T(8,128)(2,1)} %broadcast_in_dim.34), calls=%async_computation.9 | async-start | bytes 3145728 | tf_op jit(solution)/shard_map/all_to_all | solution.py:447
  186.1 15.7 %copy-start.4 = (bf16[128,512]{1,0:T(8,128)(2,1)S(1)}, bf16[128,512]{1,0:T(8,128)(2,1)}, u32[]{:S(2)}) copy-start(bf16[128,512]{1,0:T(8,128)(2,1)} %reshape.136) | copy-start | bytes 393220
  186.7 7.8 %collective-permute-start.12 = (bf16[384,512]{1,0:T(8,128)(2,1)S(1)}, bf16[384,512]{1,0:T(8,128)(2,1)S(1)}, u32[]{:S(2)}, u32[]{:S(2)}) collective-permute-start(bf16[384,512]{1,0:T(8,128)(2,1)S(1)} %maximum_select_fusion.2), channel_id=1, source_target_pairs={{0,8},{1,9},{2,10},{3,11},{4,12},{5,13},{6,14},{7,15},{8,0},{9,1},... | collective-permute-start | bytes 1179656 | tf_op jit(solution)/shard_map/ppermute | solution.py:464
  194.9 9.5 %collective-permute-start.13 = (bf16[768,512]{1,0:T(8,128)(2,1)S(1)}, bf16[768,512]{1,0:T(8,128)(2,1)}, u32[]{:S(2)}, u32[]{:S(2)}) collective-permute-start(bf16[768,512]{1,0:T(8,128)(2,1)S(1)} %maximum_select_fusion.1), channel_id=1, source_target_pairs={{0,1},{1,0},{2,3},{3,2},{4,5},{5,4},{6,7},{7,6},{8,9},{9,8},{10,11... | collective-permute-start | bytes 2359304 | tf_op jit(solution)/shard_map/ppermute | solution.py:464
  201.8 10.4 %collective-permute-start.3 = (bf16[1536,512]{1,0:T(8,128)(2,1)S(1)}, bf16[1536,512]{1,0:T(8,128)(2,1)S(1)}, u32[]{:S(2)}, u32[]{:S(2)}) collective-permute-start(bf16[1536,512]{1,0:T(8,128)(2,1)S(1)} %bitcast.25), channel_id=1, source_target_pairs={{0,1},{1,0},{2,3},{3,2},{4,5},{5,4},{6,7},{7,6},{8,9},{9,8},{10,11... | collective-permute-start | bytes 4718600 | tf_op jit(solution)/shard_map/ppermute | solution.py:464
  (7 other events, 40.2 us)

commit v5 on v4

--- a/solution.py
+++ b/solution.py
@@ -80,14 +80,32 @@
         out_ref[...] = (keep[rows, :].astype(F32) + recv[rows, :].astype(F32)).astype(BF)
 
 
-def fold_pair_kernel(keep, recv, out_ref):
-    count, rows, _ = out_ref.shape
+def fold_pair_kernel(keep_far, recv, out_far, keep, out, sems, out_sems):
+    count, rows, _ = out.shape
     rows -= TAIL
-    tail = (keep[count * rows :].astype(F32) + recv[count * rows :].astype(F32)).astype(BF)
-    for k in range(count):
-        piece = slice(k * rows, (k + 1) * rows)
-        out_ref[k, 0:rows] = (keep[piece].astype(F32) + recv[piece].astype(F32)).astype(BF)
-        out_ref[k, rows:] = tail
+    spans = [(count * rows, TAIL)] + [(k * rows, rows) for k in range(count)]
+    loads = [
+        pltpu.make_async_copy(
+            keep_far.at[pl.ds(at, size)], keep.at[pl.ds(at, size)], sems.at[k]
+        )
+        for k, (at, size) in enumerate(spans)
+    ]
+    for load in loads:
+        load.start()
+    sums = []
+    outs = []
+    for k, (at, size) in enumerate(spans):
+        loads[k].wait()
+        piece = slice(at, at + size)
+        total = (keep[piece].astype(F32) + recv[piece].astype(F32)).astype(BF)
+        if k == 0:
+            sums.append(total)
+            continue
+        out[k - 1, 0:rows] = total
+        out[k - 1, rows:] = sums[0]
+        outs.append(store_out(out.at[k - 1], out_far.at[k - 1], out_sems.at[k - 1]))
+    for copy in outs:
+        copy.wait()
 
 
 def fold_group_kernel(got, out_ref):
@@ -188,29 +206,38 @@
 
 
 def node_kernel(
-    node, total_in, ngain, ncot, nw1_far, nw2_far, fg_ref, gn_ref, ngw1_ref, ngw2_ref, ngg_ref,
-    nw1, nw2, sems,
+    ngain, node_far, total_far, nw1_far, nw2_far, ncot_far,
+    ngg_ref, dp_far, fg_far, gn_far, hidden_far, dy_far,
+    node, total, nw1, nw2, ncot, sems, dp, fg, gn, hidden_out, dy, out_sems,
 ):
-    loads = loads_of((nw1_far, nw2_far), (nw1, nw2), sems)
+    loads = loads_of(
+        (node_far, total_far, nw1_far, nw2_far, ncot_far), (node, total, nw1, nw2, ncot), sems
+    )
     for load in loads:
         load.start()
     lat = node.shape[1]
-    total = total_in[...]
-    loads[0].wait()
-    node_pre = dot(node[...], nw1[0:lat]) + dot(total, nw1[lat:])
-    hidden = hidden_of(node_pre)
-    loads[1].wait()
-    node_normed, inv_std = normalise(dot(hidden, nw2[...]))
+    for load in loads[:3]:
+        load.wait()
+    pre = dot(node[...], nw1[0:lat]) + dot(total[...], nw1[lat:])
+    hidden = hidden_of(pre)
+    hidden_out[...] = hidden
+    outs = [store_out(hidden_out, hidden_far, out_sems.at[0])]
+    loads[3].wait()
+    normed, inv_std = normalise(dot(hidden, nw2[...]))
+    loads[4].wait()
     cot = ncot[...].astype(F32)
-    gain_part, d_proj, d_pre = grad_to_pre(
-        node_pre, node_normed, inv_std, cot, ngain[...], nw2[...]
-    )
+    gain_part, d_proj, d_pre = grad_to_pre(pre, normed, inv_std, cot, ngain[...], nw2[...])
     ngg_ref[...] = gain_part
-    ngw2_ref[...] = dot_lt(hidden, d_proj).astype(BF)
-    ngw1_ref[0:lat] = dot_lt(node[...], d_pre).astype(BF)
-    ngw1_ref[lat:] = dot_lt(total, d_pre).astype(BF)
-    gn_ref[...] = cot + dot_rt(d_pre, nw1[0:lat])
-    fg_ref[...] = dot_rt(d_pre, nw1[lat:])
+    dy[...] = d_proj
+    outs.append(store_out(dy, dy_far, out_sems.at[1]))
+    dp[...] = d_pre
+    outs.append(store_out(dp, dp_far, out_sems.at[2]))
+    fg[...] = dot_rt(d_pre, nw1[lat:])
+    outs.append(store_out(fg, fg_far, out_sems.at[3]))
+    gn[...] = cot + dot_rt(d_pre, nw1[0:lat])
+    outs.append(store_out(gn, gn_far, out_sems.at[4]))
+    for out in outs:
+        out.wait()
 
 
 def edge_backward_kernel(
@@ -267,16 +294,21 @@
 
 
 def coarse_kernel(
-    core, rows, total_in, ccot, ngain, ngg, nw1_far, nw2_far, ngw1_far, ngw2_far,
-    cg_ref, after_ref, keep_ref, send_ref, gg_ref, pay, nw1, nw2, ngw1, ngw2, sems,
+    core, rows, total_in, ccot, ngain, ngg,
+    nw1_far, nw2_far, node_far, dp_far, fine_far, hidden_far, dy_far,
+    cg_ref, after_ref, keep_ref, send_ref, gg_ref,
+    pay, nw1, nw2, node, dp, fine, node_hidden, dy, sems,
 ):
     loads = loads_of(
-        (nw1_far, nw2_far, ngw1_far, ngw2_far), (nw1, nw2, ngw1, ngw2), sems
+        (nw1_far, nw2_far, node_far, dp_far, fine_far, hidden_far, dy_far),
+        (nw1, nw2, node, dp, fine, node_hidden, dy),
+        sems,
     )
     for load in loads:
         load.start()
     lat = rows.shape[1]
-    used = ngw1.shape[0] + ngw2.shape[0]
+    width = nw2.shape[0]
+    used = 2 * lat + width
     total = total_in[...].astype(BF)
     loads[0].wait()
     pre = dot(rows[...], nw1[0:lat]) + dot(total, nw1[lat:])
@@ -287,24 +319,27 @@
     gain_part, d_proj, d_pre = grad_to_pre(pre, normed, inv_std, cot, ngain[...], nw2[...])
     cg_ref[...] = dot_rt(d_pre, nw1[lat:]).astype(BF)
     after_ref[...] = cot + dot_rt(d_pre, nw1[0:lat])
-    loads[2].wait()
-    loads[3].wait()
-    pay[0:lat] = ngw1[0:lat].astype(F32) + dot_lt(rows[...], d_pre)
-    pay[lat : 2 * lat] = ngw1[lat:].astype(F32) + dot_lt(total, d_pre)
-    pay[2 * lat : used] = ngw2[...].astype(F32) + dot_lt(hidden, d_proj)
+    gg_ref[...] = ngg[...] + gain_part
+    for load in loads[2:]:
+        load.wait()
+    pay[0:lat] = dot_lt(node[...], dp[...]) + dot_lt(rows[...], d_pre)
+    pay[lat : 2 * lat] = dot_lt(fine[...], dp[...]) + dot_lt(total, d_pre)
+    pay[2 * lat : used] = dot_lt(node_hidden[...], dy[...]) + dot_lt(hidden, d_proj)
     if used < pay.shape[0]:
         pay[used:] = jnp.zeros((pay.shape[0] - used, lat), F32)
     split_rows(pay, core[0], keep_ref, send_ref)
-    gg_ref[...] = ngg[...] + gain_part
 
 
 def up_backward_kernel(
-    us, ur, place, up, xs, xr, pre_ref, ucot, cg_own, cg_other, gain, gg, ngg, after,
-    w2_far, w1_far, cp_far, gw2_far, gw1_far, gu_ref, np_ref, keep_far, send_far,
-    csum, pay, w2, w1, cp, gw2, gw1, sems, out_sems,
+    us, ur, place, cg_own, cg_other, gain, gg, ngg, after,
+    pre_far, w2_far, ucot_far, w1_far, cp_far, gw2_far, gw1_far, up_far, xs_far, xr_far,
+    gu_far, np_far, keep_far, send_far,
+    csum, pay, gu, np_out, pre_ref, w2, ucot, w1, cp, gw2, gw1, up, xs, xr, sems, out_sems,
 ):
     loads = loads_of(
-        (w2_far, w1_far, cp_far, gw2_far, gw1_far), (w2, w1, cp, gw2, gw1), sems
+        (pre_far, w2_far, ucot_far, w1_far, cp_far, gw2_far, gw1_far, up_far, xs_far, xr_far),
+        (pre_ref, w2, ucot, w1, cp, gw2, gw1, up, xs, xr),
+        sems,
     )
     for load in loads:
         load.start()
@@ -315,21 +350,25 @@
     hot_r = onehot_t(ur[...], coarse)
     turned = ur[...] - core * half
     turned = jnp.where(turned < 0, turned + coarse, turned)
+    loads[2].wait()
     cot = (
         ucot[...].astype(F32)
         + dot_lt(onehot_t(turned, half), cg_own[...])
         + dot_lt(onehot_t(turned, half, half), cg_other[...])
     )
+    loads[0].wait()
     pre = pre_ref[...]
     hidden = hidden_of(pre)
-    loads[0].wait()
+    loads[1].wait()
     normed, inv_std = normalise(dot(hidden, w2[...]))
     gain_part, d_proj, d_pre = grad_to_pre(pre, normed, inv_std, cot, gain[...], w2[...])
-    loads[1].wait()
-    gu_ref[...] = cot + dot_rt(d_pre, w1[0:lat])
-    send = dot(onehot_t(us[...], np_ref.shape[0]), d_pre).astype(BF)
-    np_ref[...] = dot_rt(send, w1[lat : 2 * lat])
-    loads[2].wait()
+    loads[3].wait()
+    gu[...] = cot + dot_rt(d_pre, w1[0:lat])
+    outs = [store_out(gu, gu_far, out_sems.at[2])]
+    send = dot(onehot_t(us[...], np_out.shape[0]), d_pre).astype(BF)
+    np_out[...] = dot_rt(send, w1[lat : 2 * lat])
+    outs.append(store_out(np_out, np_far, out_sems.at[3]))
+    loads[4].wait()
     csum[...] = cp[...].astype(F32) + dot_rt(dot(hot_r, d_pre).astype(BF), w1[2 * lat :])
     count = after.shape[0]
     mine = pl.ds(pl.multiple_of(place[0] * count, 8), count)
@@ -360,10 +399,11 @@
 
     put(0, c_half, csum)
     send_piece(0, c_half)
-    loads[3].wait()
+    loads[5].wait()
     put(c_half + h_half, w_half, gw2[...].astype(F32) + dot_lt(hidden, d_proj))
     send_piece(c_half + h_half, w_half)
-    loads[4].wait()
+    for load in loads[6:]:
+        load.wait()
     w1_part = jnp.concatenate(
         [
             gw1[k * lat : (k + 1) * lat].astype(F32) + dot_lt(x[...], d_pre)
@@ -386,6 +426,8 @@
     send_piece(used, rows + TAIL - used)
     for k, out_far in enumerate((keep_far, send_far)):
         pltpu.make_async_copy(pay.at[pl.ds(0, rows + TAIL)], out_far, out_sems.at[k]).wait()
+    for out in outs:
+        out.wait()
 
 
 def widen_kernel(core, half, coarse_ref, first_ref, second_ref, *, scale):
@@ -493,14 +535,24 @@
     got = exchange(send, 1)
     got, wait_for = lax.optimization_barrier((got, wait_for))
     x = (*in_far(keep), got)
-    for axes, kernel in zip(GROUPS[1:], (fold_pair_kernel, fold_group_kernel)):
+    for step, (axes, kernel) in enumerate(zip(GROUPS[1:], (fold_pair_kernel, fold_group_kernel))):
         count = lax.axis_size(axes)
         part = rows // count
+        shape_out = (count, part + TAIL, cols)
+        manual = dict(
+            in_specs=[IN_HBM, IN_VMEM],
+            out_specs=IN_HBM,
+            scratch_shapes=[
+                pltpu.VMEM(keep.shape, BF), pltpu.VMEM(shape_out, BF),
+                pltpu.SemaphoreType.DMA((count + 1,)), pltpu.SemaphoreType.DMA((count,)),
+            ],
+        )
         x = pl.pallas_call(
             kernel,
-            out_shape=pltpu.HBM((count, part + TAIL, cols), BF),
+            out_shape=pltpu.HBM(shape_out, BF),
             compiler_params=params(),
             cost_estimate=cost(3.0),
+            **(manual if step == 0 else {}),
         )(*x)
         x = (swap(x.reshape(-1, cols), axes, count).reshape(x.shape),)
         rows = part
@@ -602,18 +654,20 @@
         name="edge_forward",
     )(es, er, halo, gain_row, *in_far(*edge_args))
 
-    fine_grad, grad_n, ngw1, ngw2, ngg = pl.pallas_call(
+    node_args = (node, fine_total, nw1, nw2, ncot)
+    staging = [
+        far(n, width, BF), far(n, lat, F32), far(n, lat, F32), far(n, width, BF), far(n, lat, BF),
+    ]
+    ngg, node_dp, fine_grad, grad_n, node_hidden, node_dy = pl.pallas_call(
         node_kernel,
-        in_specs=[IN_VMEM] * 4 + [IN_HBM] * 2,
-        scratch_shapes=buffers(nw1, nw2),
-        out_shape=(
-            far(n, lat, F32), far(n, lat, F32), far(2 * lat, width, BF),
-            far(width, lat, BF), shape(1, lat, F32),
-        ),
+        in_specs=[IN_VMEM] + [IN_HBM] * 5,
+        out_specs=[IN_VMEM] + [IN_HBM] * 5,
+        out_shape=(shape(1, lat, F32), *staging),
+        scratch_shapes=buffers(*node_args) + buffers(*staging),
         compiler_params=params(),
         cost_estimate=cost(5.0),
         name="node_mlp",
-    )(*in_far(node, fine_total), ngain_row, *in_far(ncot, nw1, nw2))
+    )(ngain_row, *in_far(*node_args))
 
     edge_args = (pre, w2, ecot, fine_grad, w1, edge, xs, node)
     staging = [
@@ -641,30 +695,32 @@
     own_coarse = pad(lax.dynamic_slice_in_dim(coarse, own * mine, mine, 0))
     own_cot = pad(lax.dynamic_slice_in_dim(ccot, own * mine, mine, 0))
     node_rows = padded_rows(2 * lat + width, devices)
+    node_args = (nw1, nw2, node, node_dp, fine_total, node_hidden, node_dy)
     coarse_grad, coarse_after, node_keep, node_send, ngg_sum = pl.pallas_call(
         coarse_kernel,
-        in_specs=[IN_SMEM] + [IN_VMEM] * 5 + [IN_HBM] * 4,
+        in_specs=[IN_SMEM] + [IN_VMEM] * 5 + [IN_HBM] * 7,
         out_shape=(
             shape(padded, lat, BF), far(padded, lat, F32), far(node_rows // 2, lat, BF),
             shape(node_rows // 2, lat, BF), shape(1, lat, F32),
         ),
-        scratch_shapes=[pltpu.VMEM((node_rows, lat), F32)] + buffers(nw1, nw2, ngw1, ngw2),
+        scratch_shapes=[pltpu.VMEM((node_rows, lat), F32)] + buffers(*node_args),
         compiler_params=params(),
         cost_estimate=cost(5.0),
         name="coarse_mlp",
     )(
         core, own_coarse, pad(coarse_total), own_cot, ngain_row, ngg,
-        *in_far(nw1, nw2, ngw1, ngw2),
+        *in_far(*node_args),
     )
     cg_own, cg_other = gather_halves(coarse_grad[:mine])
 
     node_total = halving_sum(node_keep, node_send)
 
     edge_rows = padded_rows(ccount + 3 * lat + width, devices)
+    up_args = (up_pre, w2, ucot, w1, coarse_local, gw2, gw1, up, up_xs, up_xr)
     grad_u, up_node_part, keep, send = pl.pallas_call(
         up_backward_kernel,
-        in_specs=[IN_VMEM] * 2 + [IN_SMEM] + [IN_VMEM] * 11 + [IN_HBM] * 5,
-        out_specs=[IN_VMEM] * 2 + [IN_HBM] * 2,
+        in_specs=[IN_VMEM] * 2 + [IN_SMEM] + [IN_VMEM] * 6 + [IN_HBM] * 10,
+        out_specs=[IN_HBM] * 4,
         out_shape=(
             far(ucount, lat, F32), far(n, lat, F32), far(edge_rows // 2 + TAIL, lat, BF),
             far(edge_rows // 2 + TAIL, lat, BF),
@@ -672,15 +728,15 @@
         scratch_shapes=[
             pltpu.VMEM((ccount, lat), F32), pltpu.VMEM((edge_rows + 2 * TAIL, lat), BF),
         ]
-        + buffers(w2, w1, coarse_local, gw2, gw1)
-        + [pltpu.SemaphoreType.DMA((2,))],
+        + [pltpu.VMEM((ucount, lat), F32), pltpu.VMEM((n, lat), F32)]
+        + buffers(*up_args)
+        + [pltpu.SemaphoreType.DMA((4,))],
         compiler_params=params(),
         cost_estimate=cost(8.0),
         name="up_backward",
     )(
-        us, ur, jnp.stack([own, core[0]]), *in_far(up, up_xs, up_xr, up_pre, ucot), cg_own,
-        cg_other, gain_row, gg, ngg_sum, *in_far(coarse_after[:mine]),
-        *in_far(w2, w1, coarse_local, gw2, gw1),
+        us, ur, jnp.stack([own, core[0]]), cg_own, cg_other, gain_row, gg, ngg_sum,
+        *in_far(coarse_after[:mine]), *in_far(*up_args),
     )
     block, gains, returned = reduce_with_tail(keep, send, returned)
     own_half, other_half = gather_halves(block)

time: 215 us -> 213 us (level)
  transfers between devices with their start and end apart: 22 -> 22, of which waited for: 12 -> 12; matrix products, arithmetic and copies ran while one was open for 6% -> 7% of each run, Pallas kernels for 17% -> 17%
where the time goes in v5:
time: 213 us; the launch traced here: 212 us
  waiting for transfers between devices  68.7 us (32%)
  Pallas kernels  58.1 us (27%)
  starting transfers between devices  45.5 us (21%)
  blocking collectives  20.7 us (10%)
  other arithmetic  8.39 us (4%)
  local copies, waits for them, and re-layouts  6.92 us (3%)
  matrix products  2.72 us (1%)
    ppermute x14, waiting for transfers between devices, exchange(): return lax.ppermute(x, EVERYONE, [(i, i ^ mask) for i in range(devices)])  31.3 us
    all_to_all x7, waiting for transfers between devices, swap(): return lax.all_to_all(x, axes, 0, 0, tiled=True)  30.1 us
    all_to_all x7, starting transfers between devices, swap(): return lax.all_to_all(x, axes, 0, 0, tiled=True)  25.3 us
    ppermute x14, starting transfers between devices, exchange(): return lax.ppermute(x, EVERYONE, [(i, i ^ mask) for i in range(devices)])  13.2 us
    pallas_call x1, Pallas kernels, per_device(): pl.pallas_call(edge_backward_kernel, in_specs=[IN_VMEM] * 3 + [IN_HBM] *...  12.5 us
    all_to_all x1, blocking collectives, per_device(): lax.all_to_all(returning.reshape(devices, slots, lat), EVERYONE, 0, 0, ti...  11.4 us
    all_to_all x1, blocking collectives, swap(): return lax.all_to_all(x, axes, 0, 0, tiled=True)  9.29 us
    pallas_call x1, Pallas kernels, per_device(): pl.pallas_call(edge_forward_kernel, in_specs=[IN_VMEM] * 4 + [IN_HBM] * 5...  8.61 us
  transfers between devices with their start and end apart: 22, of which 12 were waited for; matrix products, arithmetic and copies ran while one was open for 7% of the time, Pallas kernels for 17%

profile of v5, /device:TPU:0, one launch (start us, length us, event | category | flops | bytes accessed | tf_op | source)
XLA Modules:
  0.0 212.0 jit_solution(4173705622884025904)
XLA Ops:
  0.7 5.4 %up_forward.1 = (f32[256,512]{1,0:T(8,128)}, bf16[256,512]{1,0:T(8,128)(2,1)}, bf16[256,512]{1,0:T(8,128)(2,1)}, bf16[512,512]{1,0:T(8,128)(2,1)}, bf16[512,512]{1,0:T(8,128)(2,1)S(1)}) custom-call(s32[1,256]{1,0:T(1,128)} %bitcast.43, s32[1,256]{1,0:T(1,128)} %bitcast.45, s32[1]{0:T(128)} %bitcast.7.core, bf16[256,512]{1,0:T(8,128)(2,1)} %up_far.1, ...), custom_call_target="tpu_custom_call" | custom-call | flops 5500000256 | bytes 15000000 | tf_op jit(solution)/shard_map/up_forward/pallas_call | solution.py:628
  7.8 6.9 %all-to-all-start = ((bf16[32,4,512]{2,1,0:T(4,128)(2,1)}), bf16[32,4,512]{2,1,0:T(4,128)(2,1)S(1)}, u32[]{:S(2)}, u32[]{:S(2)}) async-start(bf16[32,4,512]{2,1,0:T(4,128)(2,1)} %reshape.130), calls=%async_computation | async-start | bytes 262144 | tf_op jit(solution)/shard_map/all_to_all | solution.py:624
  15.5 7.4 %all-to-all-done = bf16[32,4,512]{2,1,0:T(4,128)(2,1)S(1)} async-done(((bf16[32,4,512]{2,1,0:T(4,128)(2,1)}), bf16[32,4,512]{2,1,0:T(4,128)(2,1)S(1)}, u32[]{:S(2)}, u32[]{:S(2)}) %all-to-all-start) | async-done | bytes 131104 | tf_op jit(solution)/shard_map/all_to_all | solution.py:624
  23.9 3.5 %all-to-all-start.1 = ((bf16[4,128,512]{2,1,0:T(8,128)(2,1)}), bf16[4,128,512]{2,1,0:T(8,128)(2,1)S(1)}, u32[]{:S(2)}, u32[]{:S(2)}) async-start(bf16[4,128,512]{2,1,0:T(8,128)(2,1)} %bitcast.8), calls=%async_computation.1 | async-start | bytes 1048576 | tf_op jit(solution)/shard_map/all_to_all | solution.py:489
  27.4 8.6 %edge_forward.1 = (f32[1024,512]{1,0:T(8,128)}, bf16[1024,512]{1,0:T(8,128)(2,1)}, bf16[256,512]{1,0:T(8,128)(2,1)}) custom-call(s32[1,1024]{1,0:T(1,128)} %bitcast.33, s32[1,1024]{1,0:T(1,128)} %bitcast.35, bf16[128,512]{1,0:T(8,128)(2,1)S(1)} %reshape.131.halo, f32[1,512]{1,0:T(1,128)} %bitcast.40, bf16[1536,512]{1,0:T(8,128)(2,1)} %w1_far.7, ...), custom_call_target="tpu_custom_call" | custom-call | flops 9900000256 | bytes 27000000 | tf_op jit(solution)/shard_map/edge_forward/pallas_call | solution.py:645
  40.1 4.7 %node_mlp.1 = (f32[1,512]{1,0:T(1,128)S(1)}, bf16[256,512]{1,0:T(8,128)(2,1)}, f32[256,512]{1,0:T(8,128)}, f32[256,512]{1,0:T(8,128)}, bf16[256,512]{1,0:T(8,128)(2,1)}, /*index=5*/bf16[256,512]{1,0:T(8,128)(2,1)}) custom-call(f32[1,512]{1,0:T(1,128)} %bitcast.37, bf16[256,512]{1,0:T(8,128)(2,1)} %node_far.9, ...), custom_call_target="tpu_custom_call" | custom-call | flops 5500000256 | bytes 15000000 | tf_op jit(solution)/shard_map/node_mlp/pallas_call | solution.py:661
  46.6 5.4 %coarse_mlp.1 = (bf16[32,512]{1,0:T(8,128)(2,1)S(1)}, f32[32,512]{1,0:T(8,128)}, bf16[768,512]{1,0:T(8,128)(2,1)}, bf16[768,512]{1,0:T(8,128)(2,1)S(1)}, f32[1,512]{1,0:T(1,128)S(1)}) custom-call(s32[1]{0:T(128)} %bitcast.7.core, bf16[32,512]{1,0:T(8,128)(2,1)S(1)} %constant_dynamic-slice_fusion.1.rows, f32[32,512]{1,0:T(8,128)S(1)} %convert_reduce_fusion.1.total_in, ...), custom_call_target="tpu_custom_call" | custom-call | flops 5500000256 | bytes 15000000 | tf_op jit(solution)/shard_map/coarse_mlp/pallas_call | solution.py:699
  52.8 9.3 %all_to_all.68 = bf16[4,32,512]{2,1,0:T(8,128)(2,1)S(1)} all-to-all(bf16[4,32,512]{2,1,0:T(8,128)(2,1)S(1)} %broadcast_in_dim.12), channel_id=1, replica_groups=mesh['z'=4,'x'=2,'y'=2,'core'=2] {'z'}, dimensions={0} | all-to-all | bytes 262144 | tf_op jit(solution)/shard_map/all_to_all | solution.py:489
  62.9 4.1 %all-to-all-start.4 = ((bf16[4,128,512]{2,1,0:T(8,128)(2,1)}), bf16[4,128,512]{2,1,0:T(8,128)(2,1)S(1)}, u32[]{:S(2)}, u32[]{:S(2)}) async-start(bf16[4,128,512]{2,1,0:T(8,128)(2,1)} %broadcast_in_dim.14), calls=%async_computation.4 | async-start | bytes 1048576 | tf_op jit(solution)/shard_map/all_to_all | solution.py:489
  67.1 6.5 %all-to-all-done.4 = bf16[4,128,512]{2,1,0:T(8,128)(2,1)S(1)} async-done(((bf16[4,128,512]{2,1,0:T(8,128)(2,1)}), bf16[4,128,512]{2,1,0:T(8,128)(2,1)S(1)}, u32[]{:S(2)}, u32[]{:S(2)}) %all-to-all-start.4) | async-done | bytes 524320 | tf_op jit(solution)/shard_map/all_to_all | solution.py:489
  73.6 12.5 %edge_backward.1 = (f32[1,512]{1,0:T(1,128)S(1)}, bf16[128,512]{1,0:T(8,128)(2,1)S(1)}, f32[1024,512]{1,0:T(8,128)}, bf16[1536,512]{1,0:T(8,128)(2,1)}, bf16[512...) custom-call(s32[1,1024]{1,0:T(1,128)} %bitcast.34, s32[1,1024]{1,0:T(1,128)} %bitcast.36, ...), custom_call_target="tpu_custom_call" | custom-call | flops 16499999744 | bytes 45000000 | tf_op jit(solution)/shard_map/edge_backward/pallas_call | solution.py:677
  86.2 7.5 %up_backward.1 = (f32[256,512]{1,0:T(8,128)}, f32[256,512]{1,0:T(8,128)}, bf16[1552,512]{1,0:T(8,128)(2,1)}, bf16[1552,512]{1,0:T(8,128)(2,1)}) custom-call(s32[1,256]{1,0:T(1,128)} %bitcast.44, s32[1,256]{1,0:T(1,128)} %bitcast.46, s32[2]{0:T(128)S(1)} %pad_add_fusion.place, bf16[512,512]{1,0:T(8,128)(2,1)S(1)} %bitcast.28, ...), custom_call_target="tpu_custom_call" | custom-call | flops 8800000000 | bytes 24000000 | tf_op jit(solution)/shard_map/up_backward/pallas_call | solution.py:720
  94.3 11.4 %all_to_all.69 = bf16[32,4,512]{2,1,0:T(4,128)(2,1)S(1)} all-to-all(bf16[32,4,512]{2,1,0:T(4,128)(2,1)S(1)} %reshape.135), channel_id=1, replica_groups=mesh['z'=4,'x'=2,'y'=2,'core'=2] {'z','x','y','core'}, dimensions={0} | all-to-all | bytes 262144 | tf_op jit(solution)/shard_map/all_to_all | solution.py:688
  108.7 3.9 %all-to-all-start.6 = ((bf16[4,400,512]{2,1,0:T(8,128)(2,1)}), bf16[4,400,512]{2,1,0:T(8,128)(2,1)S(1)}, u32[]{:S(2)}, u32[]{:S(2)}) async-start(bf16[4,400,512]{2,1,0:T(8,128)(2,1)} %shard_map.258), calls=%async_computation.6 | async-start | bytes 3276800 | tf_op jit(solution)/shard_map/all_to_all | solution.py:489
  118.0 15.0 %all-to-all-done.6.got = bf16[4,400,512]{2,1,0:T(8,128)(2,1)S(1)} async-done(((bf16[4,400,512]{2,1,0:T(8,128)(2,1)}), bf16[4,400,512]{2,1,0:T(8,128)(2,1)S(1)}, u32[]{:S(2)}, u32[]{:S(2)}) %all-to-all-start.6) | async-done | bytes 1638432 | tf_op jit(solution)/shard_map/all_to_all | solution.py:489
  134.0 3.5 %all-to-all-start.7 = ((bf16[4,112,512]{2,1,0:T(8,128)(2,1)}), bf16[4,112,512]{2,1,0:T(8,128)(2,1)S(1)}, u32[]{:S(2)}, u32[]{:S(2)}) async-start(bf16[4,112,512]{2,1,0:T(8,128)(2,1)} %shard_map.259), calls=%async_computation.7 | async-start | bytes 917504 | tf_op jit(solution)/shard_map/all_to_all | solution.py:489
  140.6 5.1 %collective-permute-done.6.recv = bf16[192,512]{1,0:T(8,128)(2,1)S(1)} collective-permute-done((bf16[192,512]{1,0:T(8,128)(2,1)S(1)}, bf16[192,512]{1,0:T(8,128)(2,1)S(1)}, u32[]{:S(2)}, u32[]{:S(2)}) %collective-permute-start.6) | collective-permute-done | bytes 196640 | tf_op jit(solution)/shard_map/ppermute | solution.py:506
  148.4 3.5 %collective-permute-done.7.recv = bf16[96,512]{1,0:T(8,128)(2,1)S(1)} collective-permute-done((bf16[96,512]{1,0:T(8,128)(2,1)S(1)}, bf16[96,512]{1,0:T(8,128)(2,1)S(1)}, u32[]{:S(2)}, u32[]{:S(2)}) %collective-permute-start.7) | collective-permute-done | bytes 98336 | tf_op jit(solution)/shard_map/ppermute | solution.py:506
  157.6 3.5 %all-to-all-start.8 = ((bf16[4,96,512]{2,1,0:T(8,128)(2,1)}), bf16[4,96,512]{2,1,0:T(8,128)(2,1)S(1)}, u32[]{:S(2)}, u32[]{:S(2)}) async-start(bf16[4,96,512]{2,1,0:T(8,128)(2,1)} %broadcast_in_dim.15), calls=%async_computation.8 | async-start | bytes 786432 | tf_op jit(solution)/shard_map/all_to_all | solution.py:489
  164.1 8.4 %collective-permute-done.9 = bf16[48,512]{1,0:T(8,128)(2,1)S(1)} collective-permute-done((bf16[48,512]{1,0:T(8,128)(2,1)S(1)}, bf16[48,512]{1,0:T(8,128)(2,1)S(1)}, u32[]{:S(2)}, u32[]{:S(2)}) %collective-permute-start.9) | collective-permute-done | bytes 49184 | tf_op jit(solution)/shard_map/ppermute | solution.py:506
  173.3 3.9 %collective-permute-done.10 = bf16[96,512]{1,0:T(8,128)(2,1)S(1)} collective-permute-done((bf16[96,512]{1,0:T(8,128)(2,1)S(1)}, bf16[96,512]{1,0:T(8,128)(2,1)S(1)}, u32[]{:S(2)}, u32[]{:S(2)}) %collective-permute-start.10) | collective-permute-done | bytes 98336 | tf_op jit(solution)/shard_map/ppermute | solution.py:506
  180.6 3.6 %all-to-all-start.9 = ((bf16[4,384,512]{2,1,0:T(8,128)(2,1)}), bf16[4,384,512]{2,1,0:T(8,128)(2,1)S(1)}, u32[]{:S(2)}, u32[]{:S(2)}) async-start(bf16[4,384,512]{2,1,0:T(8,128)(2,1)} %broadcast_in_dim.34), calls=%async_computation.9 | async-start | bytes 3145728 | tf_op jit(solution)/shard_map/all_to_all | solution.py:489
  184.8 7.8 %collective-permute-done.12 = bf16[384,512]{1,0:T(8,128)(2,1)S(1)} collective-permute-done((bf16[384,512]{1,0:T(8,128)(2,1)S(1)}, bf16[384,512]{1,0:T(8,128)(2,1)S(1)}, u32[]{:S(2)}, u32[]{:S(2)}) %collective-permute-start.12) | collective-permute-done | bytes 393248 | tf_op jit(solution)/shard_map/ppermute | solution.py:506
  193.0 6.9 %all-to-all-done.9 = bf16[4,384,512]{2,1,0:T(8,128)(2,1)S(1)} async-done(((bf16[4,384,512]{2,1,0:T(8,128)(2,1)}), bf16[4,384,512]{2,1,0:T(8,128)(2,1)S(1)}, u32[]{:S(2)}, u32[]{:S(2)}) %all-to-all-start.9) | async-done | bytes 1572896 | tf_op jit(solution)/shard_map/all_to_all | solution.py:489
  (83 shorter events, 52.9 us)
Async XLA Ops:
  6.1 16.9 %copy-start.3 = (bf16[512,512]{1,0:T(8,128)(2,1)S(1)}, bf16[512,512]{1,0:T(8,128)(2,1)}, u32[]{:S(2)}) copy-start(bf16[512,512]{1,0:T(8,128)(2,1)} %get-tuple-element.62) | copy-start | bytes 1572868
  6.1 16.9 %collective-permute-start = (bf16[512,512]{1,0:T(8,128)(2,1)S(1)}, bf16[512,512]{1,0:T(8,128)(2,1)S(1)}, u32[]{:S(2)}, u32[]{:S(2)}) collective-permute-start(bf16[512,512]{1,0:T(8,128)(2,1)S(1)} %get-tuple-element.63), channel_id=1, source_target_pairs={{0,1},{1,0},{2,3},{3,2},{4,5},{5,4},{6,7},{7,6},{8,9},{9,8},{10,11... | collective-permute-start | bytes 1572872 | tf_op jit(solution)/shard_map/ppermute | solution.py:506
  7.8 15.2 %all-to-all-start = ((bf16[32,4,512]{2,1,0:T(4,128)(2,1)}), bf16[32,4,512]{2,1,0:T(4,128)(2,1)S(1)}, u32[]{:S(2)}, u32[]{:S(2)}) async-start(bf16[32,4,512]{2,1,0:T(4,128)(2,1)} %reshape.130), calls=%async_computation | async-start | bytes 262144 | tf_op jit(solution)/shard_map/all_to_all | solution.py:624
  23.9 12.1 %all-to-all-start.1 = ((bf16[4,128,512]{2,1,0:T(8,128)(2,1)}), bf16[4,128,512]{2,1,0:T(8,128)(2,1)S(1)}, u32[]{:S(2)}, u32[]{:S(2)}) async-start(bf16[4,128,512]{2,1,0:T(8,128)(2,1)} %bitcast.8), calls=%async_computation.1 | async-start | bytes 1048576 | tf_op jit(solution)/shard_map/all_to_all | solution.py:489
  36.8 9.7 %all-to-all-start.2 = ((bf16[4,32,512]{2,1,0:T(8,128)(2,1)}), bf16[4,32,512]{2,1,0:T(8,128)(2,1)S(1)}, u32[]{:S(2)}, u32[]{:S(2)}) async-start(bf16[4,32,512]{2,1,0:T(8,128)(2,1)} %bitcast.9), calls=%async_computation.2 | async-start | bytes 262144 | tf_op jit(solution)/shard_map/all_to_all | solution.py:489
  62.9 10.7 %all-to-all-start.4 = ((bf16[4,128,512]{2,1,0:T(8,128)(2,1)}), bf16[4,128,512]{2,1,0:T(8,128)(2,1)S(1)}, u32[]{:S(2)}, u32[]{:S(2)}) async-start(bf16[4,128,512]{2,1,0:T(8,128)(2,1)} %broadcast_in_dim.14), calls=%async_computation.4 | async-start | bytes 1048576 | tf_op jit(solution)/shard_map/all_to_all | solution.py:489
  73.6 12.5 %collective-permute-start.1 = (bf16[512,512]{1,0:T(8,128)(2,1)S(1)}, bf16[512,512]{1,0:T(8,128)(2,1)S(1)}, u32[]{:S(2)}, u32[]{:S(2)}) collective-permute-start(bf16[512,512]{1,0:T(8,128)(2,1)S(1)} %bitcast.27), channel_id=1, source_target_pairs={{0,1},{1,0},{2,3},{3,2},{4,5},{5,4},{6,7},{7,6},{8,9},{9,8},{10,11... | collective-permute-start | bytes 1572872 | tf_op jit(solution)/shard_map/ppermute | solution.py:506
  93.7 12.7 %collective-permute-start.2 = (bf16[1552,512]{1,0:T(8,128)(2,1)}, bf16[1552,512]{1,0:T(8,128)(2,1)S(1)}, u32[]{:S(2)}, u32[]{:S(2)}) collective-permute-start(bf16[1552,512]{1,0:T(8,128)(2,1)} %get-tuple-element.79), channel_id=1, source_target_pairs={{0,1},{1,0},{2,3},{3,2},{4,5},{5,4},{6,7},{7,6},{8,9},{9,8},{10,11... | collective-permute-start | bytes 4767752 | tf_op jit(solution)/shard_map/ppermute | solution.py:506
  108.7 24.3 %all-to-all-start.6 = ((bf16[4,400,512]{2,1,0:T(8,128)(2,1)}), bf16[4,400,512]{2,1,0:T(8,128)(2,1)S(1)}, u32[]{:S(2)}, u32[]{:S(2)}) async-start(bf16[4,400,512]{2,1,0:T(8,128)(2,1)} %shard_map.258), calls=%async_computation.6 | async-start | bytes 3276800 | tf_op jit(solution)/shard_map/all_to_all | solution.py:489
  112.7 2.5 %collective-permute-start.4 = (bf16[768,512]{1,0:T(8,128)(2,1)S(1)}, bf16[768,512]{1,0:T(8,128)(2,1)}, u32[]{:S(2)}, u32[]{:S(2)}) collective-permute-start(bf16[768,512]{1,0:T(8,128)(2,1)S(1)} %copy-done.2), channel_id=1, source_target_pairs={{0,1},{1,0},{2,3},{3,2},{4,5},{5,4},{6,7},{7,6},{8,9},{9,8},{10,11... | collective-permute-start | bytes 2359304 | tf_op jit(solution)/shard_map/ppermute | solution.py:506
  117.4 20.1 %collective-permute-start.5 = (bf16[384,512]{1,0:T(8,128)(2,1)S(1)}, bf16[384,512]{1,0:T(8,128)(2,1)S(1)}, u32[]{:S(2)}, u32[]{:S(2)}) collective-permute-start(bf16[384,512]{1,0:T(8,128)(2,1)S(1)} %get-tuple-element.95), channel_id=1, source_target_pairs={{0,8},{1,9},{2,10},{3,11},{4,12},{5,13},{6,14},{7,15},{8,0},{9,1},... | collective-permute-start | bytes 1179656 | tf_op jit(solution)/shard_map/ppermute | solution.py:506
  134.0 22.1 %all-to-all-start.7 = ((bf16[4,112,512]{2,1,0:T(8,128)(2,1)}), bf16[4,112,512]{2,1,0:T(8,128)(2,1)S(1)}, u32[]{:S(2)}, u32[]{:S(2)}) async-start(bf16[4,112,512]{2,1,0:T(8,128)(2,1)} %shard_map.259), calls=%async_computation.7 | async-start | bytes 917504 | tf_op jit(solution)/shard_map/all_to_all | solution.py:489
  139.2 6.5 %collective-permute-start.6 = (bf16[192,512]{1,0:T(8,128)(2,1)S(1)}, bf16[192,512]{1,0:T(8,128)(2,1)S(1)}, u32[]{:S(2)}, u32[]{:S(2)}) collective-permute-start(bf16[192,512]{1,0:T(8,128)(2,1)S(1)} %get-tuple-element.97), channel_id=1, source_target_pairs={{0,4},{1,5},{2,6},{3,7},{4,0},{5,1},{6,2},{7,3},{8,12},{9,13},{10,... | collective-permute-start | bytes 589832 | tf_op jit(solution)/shard_map/ppermute | solution.py:506
  147.3 4.6 %collective-permute-start.7 = (bf16[96,512]{1,0:T(8,128)(2,1)S(1)}, bf16[96,512]{1,0:T(8,128)(2,1)S(1)}, u32[]{:S(2)}, u32[]{:S(2)}) collective-permute-start(bf16[96,512]{1,0:T(8,128)(2,1)S(1)} %get-tuple-element.99), channel_id=1, source_target_pairs={{0,2},{1,3},{2,0},{3,1},{4,6},{5,7},{6,4},{7,5},{8,10},{9,11},{10,... | collective-permute-start | bytes 294920 | tf_op jit(solution)/shard_map/ppermute | solution.py:506
  153.5 7.6 %collective-permute-start.8 = (bf16[48,512]{1,0:T(8,128)(2,1)S(1)}, bf16[48,512]{1,0:T(8,128)(2,1)S(1)}, u32[]{:S(2)}, u32[]{:S(2)}) collective-permute-start(bf16[48,512]{1,0:T(8,128)(2,1)S(1)} %get-tuple-element.101), channel_id=1, source_target_pairs={{0,16},{1,17},{2,18},{3,19},{4,20},{5,21},{6,22},{7,23},{8,24},{9,... | collective-permute-start | bytes 147464 | tf_op jit(solution)/shard_map/ppermute | solution.py:506
  157.6 21.7 %all-to-all-start.8 = ((bf16[4,96,512]{2,1,0:T(8,128)(2,1)}), bf16[4,96,512]{2,1,0:T(8,128)(2,1)S(1)}, u32[]{:S(2)}, u32[]{:S(2)}) async-start(bf16[4,96,512]{2,1,0:T(8,128)(2,1)} %broadcast_in_dim.15), calls=%async_computation.8 | async-start | bytes 786432 | tf_op jit(solution)/shard_map/all_to_all | solution.py:489
  161.1 11.3 %collective-permute-start.9 = (bf16[48,512]{1,0:T(8,128)(2,1)S(1)}, bf16[48,512]{1,0:T(8,128)(2,1)S(1)}, u32[]{:S(2)}, u32[]{:S(2)}) collective-permute-start(bf16[48,512]{1,0:T(8,128)(2,1)S(1)} %add_convert_fusion.1), channel_id=1, source_target_pairs={{0,16},{1,17},{2,18},{3,19},{4,20},{5,21},{6,22},{7,23},{8,24},{9,... | collective-permute-start | bytes 147464 | tf_op jit(solution)/shard_map/ppermute | solution.py:506
  172.5 4.7 %collective-permute-start.10 = (bf16[96,512]{1,0:T(8,128)(2,1)S(1)}, bf16[96,512]{1,0:T(8,128)(2,1)S(1)}, u32[]{:S(2)}, u32[]{:S(2)}) collective-permute-start(bf16[96,512]{1,0:T(8,128)(2,1)S(1)} %maximum_select_fusion.4), channel_id=1, source_target_pairs={{0,2},{1,3},{2,0},{3,1},{4,6},{5,7},{6,4},{7,5},{8,10},{9,11},{10,... | collective-permute-start | bytes 294920 | tf_op jit(solution)/shard_map/ppermute | solution.py:506
  177.2 7.4 %collective-permute-start.11 = (bf16[192,512]{1,0:T(8,128)(2,1)S(1)}, bf16[192,512]{1,0:T(8,128)(2,1)S(1)}, u32[]{:S(2)}, u32[]{:S(2)}) collective-permute-start(bf16[192,512]{1,0:T(8,128)(2,1)S(1)} %maximum_select_fusion.3), channel_id=1, source_target_pairs={{0,4},{1,5},{2,6},{3,7},{4,0},{5,1},{6,2},{7,3},{8,12},{9,13},{10,... | collective-permute-start | bytes 589832 | tf_op jit(solution)/shard_map/ppermute | solution.py:506
  180.6 19.3 %all-to-all-start.9 = ((bf16[4,384,512]{2,1,0:T(8,128)(2,1)}), bf16[4,384,512]{2,1,0:T(8,128)(2,1)S(1)}, u32[]{:S(2)}, u32[]{:S(2)}) async-start(bf16[4,384,512]{2,1,0:T(8,128)(2,1)} %broadcast_in_dim.34), calls=%async_computation.9 | async-start | bytes 3145728 | tf_op jit(solution)/shard_map/all_to_all | solution.py:489
  184.2 15.7 %copy-start.4 = (bf16[128,512]{1,0:T(8,128)(2,1)S(1)}, bf16[128,512]{1,0:T(8,128)(2,1)}, u32[]{:S(2)}) copy-start(bf16[128,512]{1,0:T(8,128)(2,1)} %reshape.136) | copy-start | bytes 393220
  184.7 7.8 %collective-permute-start.12 = (bf16[384,512]{1,0:T(8,128)(2,1)S(1)}, bf16[384,512]{1,0:T(8,128)(2,1)S(1)}, u32[]{:S(2)}, u32[]{:S(2)}) collective-permute-start(bf16[384,512]{1,0:T(8,128)(2,1)S(1)} %maximum_select_fusion.2), channel_id=1, source_target_pairs={{0,8},{1,9},{2,10},{3,11},{4,12},{5,13},{6,14},{7,15},{8,0},{9,1},... | collective-permute-start | bytes 1179656 | tf_op jit(solution)/shard_map/ppermute | solution.py:506
  192.9 9.5 %collective-permute-start.13 = (bf16[768,512]{1,0:T(8,128)(2,1)S(1)}, bf16[768,512]{1,0:T(8,128)(2,1)}, u32[]{:S(2)}, u32[]{:S(2)}) collective-permute-start(bf16[768,512]{1,0:T(8,128)(2,1)S(1)} %maximum_select_fusion.1), channel_id=1, source_target_pairs={{0,1},{1,0},{2,3},{3,2},{4,5},{5,4},{6,7},{7,6},{8,9},{9,8},{10,11... | collective-permute-start | bytes 2359304 | tf_op jit(solution)/shard_map/ppermute | solution.py:506
  199.9 10.4 %collective-permute-start.3 = (bf16[1536,512]{1,0:T(8,128)(2,1)S(1)}, bf16[1536,512]{1,0:T(8,128)(2,1)S(1)}, u32[]{:S(2)}, u32[]{:S(2)}) collective-permute-start(bf16[1536,512]{1,0:T(8,128)(2,1)S(1)} %bitcast.25), channel_id=1, source_target_pairs={{0,1},{1,0},{2,3},{3,2},{4,5},{5,4},{6,7},{7,6},{8,9},{9,8},{10,11... | collective-permute-start | bytes 4718600 | tf_op jit(solution)/shard_map/ppermute | solution.py:506
  (7 other events, 40.2 us)

commit v6 on v5

--- a/solution.py
+++ b/solution.py
@@ -78,6 +78,10 @@
     for side, out_ref in ((bit[0], keep_ref), (1 - bit[0], send_ref)):
         rows = pl.ds(pl.multiple_of(side * half, 16), half)
         out_ref[...] = (keep[rows, :].astype(F32) + recv[rows, :].astype(F32)).astype(BF)
+
+
+def fold_plain_kernel(keep, recv, out_ref):
+    out_ref[...] = (keep[...].astype(F32) + recv[...].astype(F32)).astype(BF)
 
 
 def fold_pair_kernel(keep_far, recv, out_far, keep, out, sems, out_sems):
@@ -127,10 +131,13 @@
 
 
 def up_forward_kernel(
-    us, ur, core, up, gain, node_far, coarse_far, w1_far, w2_far,
-    p_ref, xs_ref, xr_ref, keep_ref, send_ref, part, node, coarse, w1, w2, sems,
+    us, ur, core, gain, node_far, coarse_far, up_far, w1_far, w2_far,
+    p_far, xs_far, xr_far, keep_ref, send_ref,
+    part, node, coarse, up, w1, w2, sems, p_out, xs_out, xr_out, out_sems,
 ):
-    loads = loads_of((node_far, coarse_far, w1_far, w2_far), (node, coarse, w1, w2), sems)
+    loads = loads_of(
+        (node_far, coarse_far, up_far, w1_far, w2_far), (node, coarse, up, w1, w2), sems
+    )
     for load in loads:
         load.start()
     lat = up.shape[1]
@@ -138,18 +145,24 @@
     hot_r = onehot_t(ur[...], coarse.shape[0])
     loads[0].wait()
     xs = dot_lt(hot_s, node[...]).astype(BF)
+    xs_out[...] = xs
+    outs = [store_out(xs_out, xs_far, out_sems.at[0])]
     loads[1].wait()
     xr = dot_lt(hot_r, coarse[...]).astype(BF)
+    xr_out[...] = xr
+    outs.append(store_out(xr_out, xr_far, out_sems.at[1]))
     loads[2].wait()
+    loads[3].wait()
     pre = dot(up[...], w1[0:lat]) + dot(xs, w1[lat : 2 * lat]) + dot(xr, w1[2 * lat :])
-    loads[3].wait()
+    p_out[...] = pre
+    outs.append(store_out(p_out, p_far, out_sems.at[2]))
+    loads[4].wait()
     normed, _ = normalise(dot(hidden_of(pre), w2[...]))
     new = (up[...].astype(F32) + normed * gain[...]).astype(BF)
-    p_ref[...] = pre
-    xs_ref[...] = xs
-    xr_ref[...] = xr
     part[...] = dot(hot_r, new)
     split_rows(part, core[0], keep_ref, send_ref)
+    for out in outs:
+        out.wait()
 
 
 def store_out(staging, target, sem):
@@ -317,7 +330,9 @@
     normed, inv_std = normalise(dot(hidden, nw2[...]))
     cot = ccot[...].astype(F32)
     gain_part, d_proj, d_pre = grad_to_pre(pre, normed, inv_std, cot, ngain[...], nw2[...])
-    cg_ref[...] = dot_rt(d_pre, nw1[lat:]).astype(BF)
+    grad = dot_rt(d_pre, nw1[lat:]).astype(BF)
+    for k in range(cg_ref.shape[0] // grad.shape[0]):
+        cg_ref[k * grad.shape[0] : (k + 1) * grad.shape[0]] = grad
     after_ref[...] = cot + dot_rt(d_pre, nw1[0:lat])
     gg_ref[...] = ngg[...] + gain_part
     for load in loads[2:]:
@@ -515,17 +530,23 @@
 
 
 def reduce_rows(keep, send):
-    x = keep.astype(F32) + exchange(send, 1).astype(F32)
+    x = pl.pallas_call(
+        fold_plain_kernel,
+        out_shape=far(*keep.shape, BF),
+        compiler_params=params(),
+        cost_estimate=cost(1.0),
+        name="fold_plain",
+    )(*in_far(keep), exchange(send, 1))
     for axes in GROUPS[1:]:
         count = lax.axis_size(axes)
         x = sum_group(swap(x.astype(BF), axes, count), count)
     return x
 
 
-def gather_halves(x):
-    for axes in reversed(GROUPS[1:]):
+def gather_halves(x, copied=False):
+    for step, axes in enumerate(reversed(GROUPS[1:])):
         count = lax.axis_size(axes)
-        x = swap(copies(x, count), axes, count)
+        x = swap(x if copied and step == 0 else copies(x, count), axes, count)
     return x, exchange(x, 1)
 
 
@@ -625,18 +646,18 @@
         outgoing.reshape(devices, slots, lat), EVERYONE, 0, 0, tiled=True
     ).reshape(imports, lat)
 
+    up_args = (node, coarse, up, w1, w2)
+    staging = [far(ucount, width, F32), far(ucount, lat, BF), far(ucount, lat, BF)]
     up_pre, up_xs, up_xr, keep, send = pl.pallas_call(
         up_forward_kernel,
-        in_specs=[IN_VMEM] * 2 + [IN_SMEM] + [IN_VMEM] * 2 + [IN_HBM] * 4,
-        out_shape=(
-            far(ucount, width, F32), far(ucount, lat, BF), far(ucount, lat, BF),
-            far(ccount // 2, lat, BF), shape(ccount // 2, lat, BF),
-        ),
-        scratch_shapes=[pltpu.VMEM((ccount, lat), F32)] + buffers(node, coarse, w1, w2),
+        in_specs=[IN_VMEM] * 2 + [IN_SMEM] + [IN_VMEM] + [IN_HBM] * 5,
+        out_specs=[IN_HBM] * 3 + [IN_VMEM] * 2,
+        out_shape=(*staging, far(ccount // 2, lat, BF), shape(ccount // 2, lat, BF)),
+        scratch_shapes=[pltpu.VMEM((ccount, lat), F32)] + buffers(*up_args) + buffers(*staging),
         compiler_params=params(),
         cost_estimate=cost(5.0),
         name="up_forward",
-    )(us, ur, core, *in_far(up), gain_row, *in_far(node, coarse, w1, w2))
+    )(us, ur, core, gain_row, *in_far(*up_args))
 
     coarse_total = reduce_rows(keep, send)
 
@@ -694,13 +715,15 @@
     pad = lambda a: jnp.pad(a, ((0, padded - mine), (0, 0))) if padded > mine else a
     own_coarse = pad(lax.dynamic_slice_in_dim(coarse, own * mine, mine, 0))
     own_cot = pad(lax.dynamic_slice_in_dim(ccot, own * mine, mine, 0))
+    cg_copies = lax.axis_size(GROUPS[-1]) if padded == mine else 1
     node_rows = padded_rows(2 * lat + width, devices)
     node_args = (nw1, nw2, node, node_dp, fine_total, node_hidden, node_dy)
     coarse_grad, coarse_after, node_keep, node_send, ngg_sum = pl.pallas_call(
         coarse_kernel,
         in_specs=[IN_SMEM] + [IN_VMEM] * 5 + [IN_HBM] * 7,
         out_shape=(
-            shape(padded, lat, BF), far(padded, lat, F32), far(node_rows // 2, lat, BF),
+            shape(padded * cg_copies, lat, BF), far(padded, lat, F32),
+            far(node_rows // 2, lat, BF),
             shape(node_rows // 2, lat, BF), shape(1, lat, F32),
         ),
         scratch_shapes=[pltpu.VMEM((node_rows, lat), F32)] + buffers(*node_args),
@@ -711,7 +734,9 @@
         core, own_coarse, pad(coarse_total), own_cot, ngain_row, ngg,
         *in_far(*node_args),
     )
-    cg_own, cg_other = gather_halves(coarse_grad[:mine])
+    if cg_copies == 1:
+        coarse_grad = coarse_grad[:mine]
+    cg_own, cg_other = gather_halves(coarse_grad, copied=cg_copies > 1)
 
     node_total = halving_sum(node_keep, node_send)
 

time: 213 us -> 214 us (level)
  no operation moved by 1% of the time
where the time goes in v6:
time: 214 us; the launch traced here: 213 us
  waiting for transfers between devices  68.7 us (32%)
  Pallas kernels  59.8 us (28%)
  starting transfers between devices  45.5 us (21%)
  blocking collectives  20.7 us (10%)
  other arithmetic  7.47 us (3%)
  local copies, waits for them, and re-layouts  6.91 us (3%)
  matrix products  2.72 us (1%)
    ppermute x14, waiting for transfers between devices, exchange(): return lax.ppermute(x, EVERYONE, [(i, i ^ mask) for i in range(devices)])  31.3 us
    all_to_all x7, waiting for transfers between devices, swap(): return lax.all_to_all(x, axes, 0, 0, tiled=True)  30.1 us
    all_to_all x7, starting transfers between devices, swap(): return lax.all_to_all(x, axes, 0, 0, tiled=True)  25.3 us
    ppermute x14, starting transfers between devices, exchange(): return lax.ppermute(x, EVERYONE, [(i, i ^ mask) for i in range(devices)])  13.2 us
    pallas_call x1, Pallas kernels, per_device(): pl.pallas_call(edge_backward_kernel, in_specs=[IN_VMEM] * 3 + [IN_HBM] *...  12.5 us
    all_to_all x1, blocking collectives, per_device(): lax.all_to_all(returning.reshape(devices, slots, lat), EVERYONE, 0, 0, ti...  11.4 us
    all_to_all x1, blocking collectives, swap(): return lax.all_to_all(x, axes, 0, 0, tiled=True)  9.3 us
    pallas_call x1, Pallas kernels, per_device(): pl.pallas_call(edge_forward_kernel, in_specs=[IN_VMEM] * 4 + [IN_HBM] * 5...  8.59 us
  transfers between devices with their start and end apart: 22, of which 12 were waited for; matrix products, arithmetic and copies ran while one was open for 7% of the time, Pallas kernels for 17%

profile of v6, /device:TPU:0, one launch (start us, length us, event | category | flops | bytes accessed | tf_op | source)
XLA Modules:
  0.0 212.9 jit_solution(5851054119222440299)
XLA Ops:
  0.7 5.2 %up_forward.1 = (f32[256,512]{1,0:T(8,128)}, bf16[256,512]{1,0:T(8,128)(2,1)}, bf16[256,512]{1,0:T(8,128)(2,1)}, bf16[512,512]{1,0:T(8,128)(2,1)}, bf16[512,512]{1,0:T(8,128)(2,1)S(1)}) custom-call(s32[1,256]{1,0:T(1,128)} %bitcast.46, s32[1,256]{1,0:T(1,128)} %bitcast.48, s32[1]{0:T(128)} %bitcast.7.core, f32[1,512]{1,0:T(1,128)} %bitcast.42, ...), custom_call_target="tpu_custom_call" | custom-call | flops 5500000256 | bytes 15000000 | tf_op jit(solution)/shard_map/up_forward/pallas_call | solution.py:651
  7.6 7.0 %all-to-all-start = ((bf16[32,4,512]{2,1,0:T(4,128)(2,1)}), bf16[32,4,512]{2,1,0:T(4,128)(2,1)S(1)}, u32[]{:S(2)}, u32[]{:S(2)}) async-start(bf16[32,4,512]{2,1,0:T(4,128)(2,1)} %reshape.127), calls=%async_computation | async-start | bytes 262144 | tf_op jit(solution)/shard_map/all_to_all | solution.py:645
  15.3 7.4 %all-to-all-done = bf16[32,4,512]{2,1,0:T(4,128)(2,1)S(1)} async-done(((bf16[32,4,512]{2,1,0:T(4,128)(2,1)}), bf16[32,4,512]{2,1,0:T(4,128)(2,1)S(1)}, u32[]{:S(2)}, u32[]{:S(2)}) %all-to-all-start) | async-done | bytes 131104 | tf_op jit(solution)/shard_map/all_to_all | solution.py:645
  24.7 3.5 %all-to-all-start.1 = ((bf16[4,128,512]{2,1,0:T(8,128)(2,1)}), bf16[4,128,512]{2,1,0:T(8,128)(2,1)S(1)}, u32[]{:S(2)}, u32[]{:S(2)}) async-start(bf16[4,128,512]{2,1,0:T(8,128)(2,1)} %bitcast.33), calls=%async_computation.1 | async-start | bytes 1048576 | tf_op jit(solution)/shard_map/all_to_all | solution.py:504
  28.2 8.6 %edge_forward.1 = (f32[1024,512]{1,0:T(8,128)}, bf16[1024,512]{1,0:T(8,128)(2,1)}, bf16[256,512]{1,0:T(8,128)(2,1)}) custom-call(s32[1,1024]{1,0:T(1,128)} %bitcast.36, s32[1,1024]{1,0:T(1,128)} %bitcast.38, bf16[128,512]{1,0:T(8,128)(2,1)S(1)} %reshape.128.halo, f32[1,512]{1,0:T(1,128)} %bitcast.43, bf16[1536,512]{1,0:T(8,128)(2,1)} %w1_far.7, ...), custom_call_target="tpu_custom_call" | custom-call | flops 9900000256 | bytes 27000000 | tf_op jit(solution)/shard_map/edge_forward/pallas_call | solution.py:666
  40.9 4.7 %node_mlp.1 = (f32[1,512]{1,0:T(1,128)S(1)}, bf16[256,512]{1,0:T(8,128)(2,1)}, f32[256,512]{1,0:T(8,128)}, f32[256,512]{1,0:T(8,128)}, bf16[256,512]{1,0:T(8,128)(2,1)}, /*index=5*/bf16[256,512]{1,0:T(8,128)(2,1)}) custom-call(f32[1,512]{1,0:T(1,128)} %bitcast.40, bf16[256,512]{1,0:T(8,128)(2,1)} %node_far.9, ...), custom_call_target="tpu_custom_call" | custom-call | flops 5500000256 | bytes 15000000 | tf_op jit(solution)/shard_map/node_mlp/pallas_call | solution.py:682
  47.3 5.4 %coarse_mlp.1 = (bf16[128,512]{1,0:T(8,128)(2,1)S(1)}, f32[32,512]{1,0:T(8,128)}, bf16[768,512]{1,0:T(8,128)(2,1)}, bf16[768,512]{1,0:T(8,128)(2,1)S(1)}, f32[1,512]{1,0:T(1,128)S(1)}) custom-call(s32[1]{0:T(128)} %bitcast.7.core, bf16[32,512]{1,0:T(8,128)(2,1)S(1)} %constant_dynamic-slice_fusion.1.rows, f32[32,512]{1,0:T(8,128)S(1)} %convert_reduce_fusion.1.total_in, ...), custom_call_target="tpu_custom_call" | custom-call | flops 5500000256 | bytes 15000000 | tf_op jit(solution)/shard_map/coarse_mlp/pallas_call | solution.py:721
  53.6 9.3 %all_to_all.71 = bf16[4,32,512]{2,1,0:T(8,128)(2,1)S(1)} all-to-all(bf16[4,32,512]{2,1,0:T(8,128)(2,1)S(1)} %bitcast.30), channel_id=1, replica_groups=mesh['z'=4,'x'=2,'y'=2,'core'=2] {'z'}, dimensions={0} | all-to-all | bytes 262144 | tf_op jit(solution)/shard_map/all_to_all | solution.py:504
  63.7 4.1 %all-to-all-start.4 = ((bf16[4,128,512]{2,1,0:T(8,128)(2,1)}), bf16[4,128,512]{2,1,0:T(8,128)(2,1)S(1)}, u32[]{:S(2)}, u32[]{:S(2)}) async-start(bf16[4,128,512]{2,1,0:T(8,128)(2,1)} %broadcast_in_dim.11), calls=%async_computation.4 | async-start | bytes 1048576 | tf_op jit(solution)/shard_map/all_to_all | solution.py:504
  67.9 6.5 %all-to-all-done.4 = bf16[4,128,512]{2,1,0:T(8,128)(2,1)S(1)} async-done(((bf16[4,128,512]{2,1,0:T(8,128)(2,1)}), bf16[4,128,512]{2,1,0:T(8,128)(2,1)S(1)}, u32[]{:S(2)}, u32[]{:S(2)}) %all-to-all-start.4) | async-done | bytes 524320 | tf_op jit(solution)/shard_map/all_to_all | solution.py:504
  74.4 12.5 %edge_backward.1 = (f32[1,512]{1,0:T(1,128)S(1)}, bf16[128,512]{1,0:T(8,128)(2,1)S(1)}, f32[1024,512]{1,0:T(8,128)}, bf16[1536,512]{1,0:T(8,128)(2,1)}, bf16[512...) custom-call(s32[1,1024]{1,0:T(1,128)} %bitcast.37, s32[1,1024]{1,0:T(1,128)} %bitcast.39, ...), custom_call_target="tpu_custom_call" | custom-call | flops 16499999744 | bytes 45000000 | tf_op jit(solution)/shard_map/edge_backward/pallas_call | solution.py:698
  86.9 7.5 %up_backward.1 = (f32[256,512]{1,0:T(8,128)}, f32[256,512]{1,0:T(8,128)}, bf16[1552,512]{1,0:T(8,128)(2,1)}, bf16[1552,512]{1,0:T(8,128)(2,1)}) custom-call(s32[1,256]{1,0:T(1,128)} %bitcast.47, s32[1,256]{1,0:T(1,128)} %bitcast.49, s32[2]{0:T(128)S(1)} %pad_add_fusion.place, bf16[512,512]{1,0:T(8,128)(2,1)S(1)} %bitcast.29, ...), custom_call_target="tpu_custom_call" | custom-call | flops 8800000000 | bytes 24000000 | tf_op jit(solution)/shard_map/up_backward/pallas_call | solution.py:745
  95.1 11.4 %all_to_all.72 = bf16[32,4,512]{2,1,0:T(4,128)(2,1)S(1)} all-to-all(bf16[32,4,512]{2,1,0:T(4,128)(2,1)S(1)} %reshape.132), channel_id=1, replica_groups=mesh['z'=4,'x'=2,'y'=2,'core'=2] {'z','x','y','core'}, dimensions={0} | all-to-all | bytes 262144 | tf_op jit(solution)/shard_map/all_to_all | solution.py:709
  109.5 3.9 %all-to-all-start.6 = ((bf16[4,400,512]{2,1,0:T(8,128)(2,1)}), bf16[4,400,512]{2,1,0:T(8,128)(2,1)S(1)}, u32[]{:S(2)}, u32[]{:S(2)}) async-start(bf16[4,400,512]{2,1,0:T(8,128)(2,1)} %shard_map.258), calls=%async_computation.6 | async-start | bytes 3276800 | tf_op jit(solution)/shard_map/all_to_all | solution.py:504
  118.8 15.0 %all-to-all-done.6.got = bf16[4,400,512]{2,1,0:T(8,128)(2,1)S(1)} async-done(((bf16[4,400,512]{2,1,0:T(8,128)(2,1)}), bf16[4,400,512]{2,1,0:T(8,128)(2,1)S(1)}, u32[]{:S(2)}, u32[]{:S(2)}) %all-to-all-start.6) | async-done | bytes 1638432 | tf_op jit(solution)/shard_map/all_to_all | solution.py:504
  134.8 3.5 %all-to-all-start.7 = ((bf16[4,112,512]{2,1,0:T(8,128)(2,1)}), bf16[4,112,512]{2,1,0:T(8,128)(2,1)S(1)}, u32[]{:S(2)}, u32[]{:S(2)}) async-start(bf16[4,112,512]{2,1,0:T(8,128)(2,1)} %shard_map.259), calls=%async_computation.7 | async-start | bytes 917504 | tf_op jit(solution)/shard_map/all_to_all | solution.py:504
  141.4 5.1 %collective-permute-done.6.recv = bf16[192,512]{1,0:T(8,128)(2,1)S(1)} collective-permute-done((bf16[192,512]{1,0:T(8,128)(2,1)S(1)}, bf16[192,512]{1,0:T(8,128)(2,1)S(1)}, u32[]{:S(2)}, u32[]{:S(2)}) %collective-permute-start.6) | collective-permute-done | bytes 196640 | tf_op jit(solution)/shard_map/ppermute | solution.py:521
  149.2 3.5 %collective-permute-done.7.recv = bf16[96,512]{1,0:T(8,128)(2,1)S(1)} collective-permute-done((bf16[96,512]{1,0:T(8,128)(2,1)S(1)}, bf16[96,512]{1,0:T(8,128)(2,1)S(1)}, u32[]{:S(2)}, u32[]{:S(2)}) %collective-permute-start.7) | collective-permute-done | bytes 98336 | tf_op jit(solution)/shard_map/ppermute | solution.py:521
  158.4 3.5 %all-to-all-start.8 = ((bf16[4,96,512]{2,1,0:T(8,128)(2,1)}), bf16[4,96,512]{2,1,0:T(8,128)(2,1)S(1)}, u32[]{:S(2)}, u32[]{:S(2)}) async-start(bf16[4,96,512]{2,1,0:T(8,128)(2,1)} %broadcast_in_dim.12), calls=%async_computation.8 | async-start | bytes 786432 | tf_op jit(solution)/shard_map/all_to_all | solution.py:504
  164.9 8.4 %collective-permute-done.9 = bf16[48,512]{1,0:T(8,128)(2,1)S(1)} collective-permute-done((bf16[48,512]{1,0:T(8,128)(2,1)S(1)}, bf16[48,512]{1,0:T(8,128)(2,1)S(1)}, u32[]{:S(2)}, u32[]{:S(2)}) %collective-permute-start.9) | collective-permute-done | bytes 49184 | tf_op jit(solution)/shard_map/ppermute | solution.py:521
  174.1 3.9 %collective-permute-done.10 = bf16[96,512]{1,0:T(8,128)(2,1)S(1)} collective-permute-done((bf16[96,512]{1,0:T(8,128)(2,1)S(1)}, bf16[96,512]{1,0:T(8,128)(2,1)S(1)}, u32[]{:S(2)}, u32[]{:S(2)}) %collective-permute-start.10) | collective-permute-done | bytes 98336 | tf_op jit(solution)/shard_map/ppermute | solution.py:521
  181.4 3.6 %all-to-all-start.9 = ((bf16[4,384,512]{2,1,0:T(8,128)(2,1)}), bf16[4,384,512]{2,1,0:T(8,128)(2,1)S(1)}, u32[]{:S(2)}, u32[]{:S(2)}) async-start(bf16[4,384,512]{2,1,0:T(8,128)(2,1)} %broadcast_in_dim.27), calls=%async_computation.9 | async-start | bytes 3145728 | tf_op jit(solution)/shard_map/all_to_all | solution.py:504
  185.6 7.8 %collective-permute-done.12 = bf16[384,512]{1,0:T(8,128)(2,1)S(1)} collective-permute-done((bf16[384,512]{1,0:T(8,128)(2,1)S(1)}, bf16[384,512]{1,0:T(8,128)(2,1)S(1)}, u32[]{:S(2)}, u32[]{:S(2)}) %collective-permute-start.12) | collective-permute-done | bytes 393248 | tf_op jit(solution)/shard_map/ppermute | solution.py:521
  193.8 6.9 %all-to-all-done.9 = bf16[4,384,512]{2,1,0:T(8,128)(2,1)S(1)} async-done(((bf16[4,384,512]{2,1,0:T(8,128)(2,1)}), bf16[4,384,512]{2,1,0:T(8,128)(2,1)S(1)}, u32[]{:S(2)}, u32[]{:S(2)}) %all-to-all-start.9) | async-done | bytes 1572896 | tf_op jit(solution)/shard_map/all_to_all | solution.py:504
  (80 shorter events, 53.9 us)
Async XLA Ops:
  0.6 14.7 %copy-start = (bf16[1024,512]{1,0:T(8,128)(2,1)S(1)}, bf16[1024,512]{1,0:T(8,128)(2,1)}, u32[]{:S(2)}) copy-start(bf16[1024,512]{1,0:T(8,128)(2,1)} %param.30) | copy-start | bytes 3145732
  5.9 16.9 %collective-permute-start = (bf16[512,512]{1,0:T(8,128)(2,1)S(1)}, bf16[512,512]{1,0:T(8,128)(2,1)S(1)}, u32[]{:S(2)}, u32[]{:S(2)}) collective-permute-start(bf16[512,512]{1,0:T(8,128)(2,1)S(1)} %get-tuple-element.63), channel_id=1, source_target_pairs={{0,1},{1,0},{2,3},{3,2},{4,5},{5,4},{6,7},{7,6},{8,9},{9,8},{10,11... | collective-permute-start | bytes 1572872 | tf_op jit(solution)/shard_map/ppermute | solution.py:521
  7.6 15.2 %all-to-all-start = ((bf16[32,4,512]{2,1,0:T(4,128)(2,1)}), bf16[32,4,512]{2,1,0:T(4,128)(2,1)S(1)}, u32[]{:S(2)}, u32[]{:S(2)}) async-start(bf16[32,4,512]{2,1,0:T(4,128)(2,1)} %reshape.127), calls=%async_computation | async-start | bytes 262144 | tf_op jit(solution)/shard_map/all_to_all | solution.py:645
  24.7 12.1 %all-to-all-start.1 = ((bf16[4,128,512]{2,1,0:T(8,128)(2,1)}), bf16[4,128,512]{2,1,0:T(8,128)(2,1)S(1)}, u32[]{:S(2)}, u32[]{:S(2)}) async-start(bf16[4,128,512]{2,1,0:T(8,128)(2,1)} %bitcast.33), calls=%async_computation.1 | async-start | bytes 1048576 | tf_op jit(solution)/shard_map/all_to_all | solution.py:504
  37.6 9.7 %all-to-all-start.2 = ((bf16[4,32,512]{2,1,0:T(8,128)(2,1)}), bf16[4,32,512]{2,1,0:T(8,128)(2,1)S(1)}, u32[]{:S(2)}, u32[]{:S(2)}) async-start(bf16[4,32,512]{2,1,0:T(8,128)(2,1)} %bitcast.9), calls=%async_computation.2 | async-start | bytes 262144 | tf_op jit(solution)/shard_map/all_to_all | solution.py:504
  63.7 10.7 %all-to-all-start.4 = ((bf16[4,128,512]{2,1,0:T(8,128)(2,1)}), bf16[4,128,512]{2,1,0:T(8,128)(2,1)S(1)}, u32[]{:S(2)}, u32[]{:S(2)}) async-start(bf16[4,128,512]{2,1,0:T(8,128)(2,1)} %broadcast_in_dim.11), calls=%async_computation.4 | async-start | bytes 1048576 | tf_op jit(solution)/shard_map/all_to_all | solution.py:504
  74.4 12.5 %collective-permute-start.1 = (bf16[512,512]{1,0:T(8,128)(2,1)S(1)}, bf16[512,512]{1,0:T(8,128)(2,1)S(1)}, u32[]{:S(2)}, u32[]{:S(2)}) collective-permute-start(bf16[512,512]{1,0:T(8,128)(2,1)S(1)} %bitcast.28), channel_id=1, source_target_pairs={{0,1},{1,0},{2,3},{3,2},{4,5},{5,4},{6,7},{7,6},{8,9},{9,8},{10,11... | collective-permute-start | bytes 1572872 | tf_op jit(solution)/shard_map/ppermute | solution.py:521
  94.5 12.7 %collective-permute-start.2 = (bf16[1552,512]{1,0:T(8,128)(2,1)}, bf16[1552,512]{1,0:T(8,128)(2,1)S(1)}, u32[]{:S(2)}, u32[]{:S(2)}) collective-permute-start(bf16[1552,512]{1,0:T(8,128)(2,1)} %get-tuple-element.79), channel_id=1, source_target_pairs={{0,1},{1,0},{2,3},{3,2},{4,5},{5,4},{6,7},{7,6},{8,9},{9,8},{10,11... | collective-permute-start | bytes 4767752 | tf_op jit(solution)/shard_map/ppermute | solution.py:521
  109.5 24.3 %all-to-all-start.6 = ((bf16[4,400,512]{2,1,0:T(8,128)(2,1)}), bf16[4,400,512]{2,1,0:T(8,128)(2,1)S(1)}, u32[]{:S(2)}, u32[]{:S(2)}) async-start(bf16[4,400,512]{2,1,0:T(8,128)(2,1)} %shard_map.258), calls=%async_computation.6 | async-start | bytes 3276800 | tf_op jit(solution)/shard_map/all_to_all | solution.py:504
  113.5 2.5 %collective-permute-start.4 = (bf16[768,512]{1,0:T(8,128)(2,1)S(1)}, bf16[768,512]{1,0:T(8,128)(2,1)}, u32[]{:S(2)}, u32[]{:S(2)}) collective-permute-start(bf16[768,512]{1,0:T(8,128)(2,1)S(1)} %copy-done.2), channel_id=1, source_target_pairs={{0,1},{1,0},{2,3},{3,2},{4,5},{5,4},{6,7},{7,6},{8,9},{9,8},{10,11... | collective-permute-start | bytes 2359304 | tf_op jit(solution)/shard_map/ppermute | solution.py:521
  118.2 20.1 %collective-permute-start.5 = (bf16[384,512]{1,0:T(8,128)(2,1)S(1)}, bf16[384,512]{1,0:T(8,128)(2,1)S(1)}, u32[]{:S(2)}, u32[]{:S(2)}) collective-permute-start(bf16[384,512]{1,0:T(8,128)(2,1)S(1)} %get-tuple-element.95), channel_id=1, source_target_pairs={{0,8},{1,9},{2,10},{3,11},{4,12},{5,13},{6,14},{7,15},{8,0},{9,1},... | collective-permute-start | bytes 1179656 | tf_op jit(solution)/shard_map/ppermute | solution.py:521
  134.8 22.1 %all-to-all-start.7 = ((bf16[4,112,512]{2,1,0:T(8,128)(2,1)}), bf16[4,112,512]{2,1,0:T(8,128)(2,1)S(1)}, u32[]{:S(2)}, u32[]{:S(2)}) async-start(bf16[4,112,512]{2,1,0:T(8,128)(2,1)} %shard_map.259), calls=%async_computation.7 | async-start | bytes 917504 | tf_op jit(solution)/shard_map/all_to_all | solution.py:504
  140.0 6.5 %collective-permute-start.6 = (bf16[192,512]{1,0:T(8,128)(2,1)S(1)}, bf16[192,512]{1,0:T(8,128)(2,1)S(1)}, u32[]{:S(2)}, u32[]{:S(2)}) collective-permute-start(bf16[192,512]{1,0:T(8,128)(2,1)S(1)} %get-tuple-element.97), channel_id=1, source_target_pairs={{0,4},{1,5},{2,6},{3,7},{4,0},{5,1},{6,2},{7,3},{8,12},{9,13},{10,... | collective-permute-start | bytes 589832 | tf_op jit(solution)/shard_map/ppermute | solution.py:521
  148.1 4.6 %collective-permute-start.7 = (bf16[96,512]{1,0:T(8,128)(2,1)S(1)}, bf16[96,512]{1,0:T(8,128)(2,1)S(1)}, u32[]{:S(2)}, u32[]{:S(2)}) collective-permute-start(bf16[96,512]{1,0:T(8,128)(2,1)S(1)} %get-tuple-element.99), channel_id=1, source_target_pairs={{0,2},{1,3},{2,0},{3,1},{4,6},{5,7},{6,4},{7,5},{8,10},{9,11},{10,... | collective-permute-start | bytes 294920 | tf_op jit(solution)/shard_map/ppermute | solution.py:521
  154.3 7.6 %collective-permute-start.8 = (bf16[48,512]{1,0:T(8,128)(2,1)S(1)}, bf16[48,512]{1,0:T(8,128)(2,1)S(1)}, u32[]{:S(2)}, u32[]{:S(2)}) collective-permute-start(bf16[48,512]{1,0:T(8,128)(2,1)S(1)} %get-tuple-element.101), channel_id=1, source_target_pairs={{0,16},{1,17},{2,18},{3,19},{4,20},{5,21},{6,22},{7,23},{8,24},{9,... | collective-permute-start | bytes 147464 | tf_op jit(solution)/shard_map/ppermute | solution.py:521
  158.4 21.7 %all-to-all-start.8 = ((bf16[4,96,512]{2,1,0:T(8,128)(2,1)}), bf16[4,96,512]{2,1,0:T(8,128)(2,1)S(1)}, u32[]{:S(2)}, u32[]{:S(2)}) async-start(bf16[4,96,512]{2,1,0:T(8,128)(2,1)} %broadcast_in_dim.12), calls=%async_computation.8 | async-start | bytes 786432 | tf_op jit(solution)/shard_map/all_to_all | solution.py:504
  161.9 11.3 %collective-permute-start.9 = (bf16[48,512]{1,0:T(8,128)(2,1)S(1)}, bf16[48,512]{1,0:T(8,128)(2,1)S(1)}, u32[]{:S(2)}, u32[]{:S(2)}) collective-permute-start(bf16[48,512]{1,0:T(8,128)(2,1)S(1)} %add_convert_fusion), channel_id=1, source_target_pairs={{0,16},{1,17},{2,18},{3,19},{4,20},{5,21},{6,22},{7,23},{8,24},{9,... | collective-permute-start | bytes 147464 | tf_op jit(solution)/shard_map/ppermute | solution.py:521
  173.3 4.7 %collective-permute-start.10 = (bf16[96,512]{1,0:T(8,128)(2,1)S(1)}, bf16[96,512]{1,0:T(8,128)(2,1)S(1)}, u32[]{:S(2)}, u32[]{:S(2)}) collective-permute-start(bf16[96,512]{1,0:T(8,128)(2,1)S(1)} %maximum_select_fusion.4), channel_id=1, source_target_pairs={{0,2},{1,3},{2,0},{3,1},{4,6},{5,7},{6,4},{7,5},{8,10},{9,11},{10,... | collective-permute-start | bytes 294920 | tf_op jit(solution)/shard_map/ppermute | solution.py:521
  178.0 7.4 %collective-permute-start.11 = (bf16[192,512]{1,0:T(8,128)(2,1)S(1)}, bf16[192,512]{1,0:T(8,128)(2,1)S(1)}, u32[]{:S(2)}, u32[]{:S(2)}) collective-permute-start(bf16[192,512]{1,0:T(8,128)(2,1)S(1)} %maximum_select_fusion.3), channel_id=1, source_target_pairs={{0,4},{1,5},{2,6},{3,7},{4,0},{5,1},{6,2},{7,3},{8,12},{9,13},{10,... | collective-permute-start | bytes 589832 | tf_op jit(solution)/shard_map/ppermute | solution.py:521
  181.4 19.3 %all-to-all-start.9 = ((bf16[4,384,512]{2,1,0:T(8,128)(2,1)}), bf16[4,384,512]{2,1,0:T(8,128)(2,1)S(1)}, u32[]{:S(2)}, u32[]{:S(2)}) async-start(bf16[4,384,512]{2,1,0:T(8,128)(2,1)} %broadcast_in_dim.27), calls=%async_computation.9 | async-start | bytes 3145728 | tf_op jit(solution)/shard_map/all_to_all | solution.py:504
  185.0 15.7 %copy-start.3 = (bf16[128,512]{1,0:T(8,128)(2,1)S(1)}, bf16[128,512]{1,0:T(8,128)(2,1)}, u32[]{:S(2)}) copy-start(bf16[128,512]{1,0:T(8,128)(2,1)} %reshape.133) | copy-start | bytes 393220
  185.5 7.8 %collective-permute-start.12 = (bf16[384,512]{1,0:T(8,128)(2,1)S(1)}, bf16[384,512]{1,0:T(8,128)(2,1)S(1)}, u32[]{:S(2)}, u32[]{:S(2)}) collective-permute-start(bf16[384,512]{1,0:T(8,128)(2,1)S(1)} %maximum_select_fusion.2), channel_id=1, source_target_pairs={{0,8},{1,9},{2,10},{3,11},{4,12},{5,13},{6,14},{7,15},{8,0},{9,1},... | collective-permute-start | bytes 1179656 | tf_op jit(solution)/shard_map/ppermute | solution.py:521
  193.7 9.5 %collective-permute-start.13 = (bf16[768,512]{1,0:T(8,128)(2,1)S(1)}, bf16[768,512]{1,0:T(8,128)(2,1)}, u32[]{:S(2)}, u32[]{:S(2)}) collective-permute-start(bf16[768,512]{1,0:T(8,128)(2,1)S(1)} %maximum_select_fusion.1), channel_id=1, source_target_pairs={{0,1},{1,0},{2,3},{3,2},{4,5},{5,4},{6,7},{7,6},{8,9},{9,8},{10,11... | collective-permute-start | bytes 2359304 | tf_op jit(solution)/shard_map/ppermute | solution.py:521
  200.7 10.4 %collective-permute-start.3 = (bf16[1536,512]{1,0:T(8,128)(2,1)S(1)}, bf16[1536,512]{1,0:T(8,128)(2,1)S(1)}, u32[]{:S(2)}, u32[]{:S(2)}) collective-permute-start(bf16[1536,512]{1,0:T(8,128)(2,1)S(1)} %bitcast.26), channel_id=1, source_target_pairs={{0,1},{1,0},{2,3},{3,2},{4,5},{5,4},{6,7},{7,6},{8,9},{9,8},{10,11... | collective-permute-start | bytes 4718600 | tf_op jit(solution)/shard_map/ppermute | solution.py:521
  (6 other events, 24.9 us)
